TPU v7x, 32 devices: a whole 2x2x4 slice. The times are simulated.
32 devices in a mesh: ctx: 8 (over z, x), head: 4 (over y, core).
Axes of the slice: x: 2, y: 2, z: 4, core: 2. Of those that a mesh axis runs over, the one named last changes fastest.
Arguments:
- query_vectors: bfloat16 [3072, 4096], P('ctx', 'head'), may hold values from -6 to 6
- key_vectors: bfloat16 [3072, 4096], P('ctx', 'head'), may hold values from -11 to 11
- value_vectors: bfloat16 [3072, 4096], P('ctx', 'head'), may hold values from -6 to 6
- log_decay: float32 [3072, 4096], P('ctx', 'head'), may hold values from -0.7 to 0, as said below
- write_rate: float32 [3072, 32], P('ctx', 'head'), may hold values from 0 to 1
- out_gate: bfloat16 [3072, 4096], P('ctx', 'head'), may hold values from -6 to 6
- norm_gain: float32 [128], replicated, may hold values from 0.25 to 1.75
- out_weight: bfloat16 [4096, 2304], P('head'), may hold values from -0.09375 to 0.09375
Outputs:
- mixed: bfloat16 [3072, 2304], P(('ctx', 'head'))
Inputs may be any that keep to these rules, and one draw needn't show every extreme that they name: `log_decay`: every decay lies strictly below 1.
All inputs are finite; a program needn't handle non-finite values.
Results may differ from a plain program's by a relative error of at most 0.014.
Values may be sent and summed in bfloat16 or wider, within the bound.
No kernel may reach another device: no remote copies, remote signals or barrier semaphores. Data moves between devices by JAX's collectives and lax.ppermute only.
A program may use at most 128 MiB of HBM per device.

v0:
```python
import jax
import jax.numpy as jnp
from jax import lax
from jax.sharding import PartitionSpec as P

HEAD_SIZE = 128
STRETCH = 64


peak_value = lax.Precision.HIGHEST


def entering(part, axis, combine, identity):
    place = lax.axis_index(axis)
    gathered = jax.tree.map(lambda a: lax.all_gather(a, axis), part)
    state = jax.tree.map(lambda a, e: jnp.zeros_like(a) + jnp.asarray(e, a.dtype), part, identity)

    def one(turn, state):
        return combine(
            state, jax.tree.map(lambda a: lax.dynamic_index_in_dim(a, turn, 0, False), gathered)
        )

    return lax.fori_loop(0, place, one, state)


def chain_mul(left_map, right_map):
    return jnp.einsum("hij,hjk->hik", left_map, right_map, precision=peak_value)


def compose_pair(earlier, later):
    return (chain_mul(later[0], earlier[0]), chain_mul(later[0], earlier[1]) + later[1])


def unit_lower_inverse(coupling):
    stretch_len = coupling.shape[-1]
    power = -coupling
    inverse = jnp.eye(stretch_len, dtype=jnp.float32) + power
    for level_index in range(1, (stretch_len - 1).bit_length()):
        power = jnp.einsum("hnts,hnsu->hntu", power, power, precision=peak_value)
        inverse = inverse + jnp.einsum("hnts,hnsu->hntu", inverse, power, precision=peak_value)
    return inverse


def on_device(
    query_vectors,
    key_vectors,
    value_vectors,
    log_decay,
    write_rate,
    out_gate,
    norm_gain,
    out_weight,
):
    row_count = query_vectors.shape[0]
    head_count = query_vectors.shape[1] // HEAD_SIZE
    block_count = row_count // STRETCH

    def arrange(source):
        return (
            source.astype(jnp.float32)
            .reshape(block_count, STRETCH, head_count, HEAD_SIZE)
            .transpose(2, 0, 1, 3)
        )

    queries = arrange(query_vectors)
    raw_keys = arrange(key_vectors)
    unit_keys = raw_keys / jnp.sqrt(jnp.sum(raw_keys * raw_keys, axis=-1, keepdims=True) + 1e-06)
    values = arrange(value_vectors)
    log_rates = arrange(log_decay)
    write_rates = write_rate.reshape(block_count, STRETCH, head_count).transpose(2, 0, 1)[..., None]
    later_pos = lax.broadcasted_iota(jnp.int32, (STRETCH, STRETCH), 0)
    earlier_pos = lax.broadcasted_iota(jnp.int32, (STRETCH, STRETCH), 1)
    lower_ones = (later_pos >= earlier_pos).astype(jnp.float32)
    strict = (later_pos > earlier_pos).astype(jnp.float32)
    cumulative = jnp.einsum("ts,hnsc->hntc", lower_ones, log_rates, precision=peak_value)
    final_log = cumulative[:, :, -1:, :]
    growth = jnp.exp(cumulative)
    key_now = unit_keys * growth
    key_back = unit_keys * jnp.exp(-cumulative)
    query_now = queries * growth
    key_end = unit_keys * jnp.exp(final_log - cumulative)
    coupling = (
        write_rates
        * jnp.einsum("hntc,hnsc->hnts", key_now, key_back, precision=peak_value)
        * strict
    )
    reading = jnp.einsum("hntc,hnsc->hnts", query_now, key_back, precision=peak_value) * lower_ones
    right_sides = jnp.concatenate([write_rates * key_now, write_rates * values], -1)
    inverse = unit_lower_inverse(coupling)
    solved = jnp.einsum("hnts,hnsd->hntd", inverse, right_sides, precision=peak_value)
    mixed_in = jnp.einsum("hnts,hnsd->hntd", reading, solved, precision=peak_value)
    query_eff = query_now - mixed_in[..., :HEAD_SIZE]
    local_part = mixed_in[..., HEAD_SIZE:]
    carried = jnp.einsum("hnsc,hnsd->hncd", key_end, solved, precision=peak_value)
    identity = jnp.eye(HEAD_SIZE, dtype=jnp.float32)
    transitions = (
        jnp.exp(final_log)[:, :, 0, :, None] * identity - carried[..., :HEAD_SIZE]
    ).transpose(1, 0, 2, 3)
    writes = carried[..., HEAD_SIZE:].transpose(1, 0, 2, 3)

    def advance(running, stretch_item):
        through, local_state = running
        step_map, step_write = stretch_item
        return (
            (chain_mul(step_map, through), chain_mul(step_map, local_state) + step_write),
            (through, local_state),
        )

    eye_heads = jnp.broadcast_to(identity, (head_count, HEAD_SIZE, HEAD_SIZE))
    zero_state = jnp.zeros((head_count, HEAD_SIZE, HEAD_SIZE), jnp.float32)
    (block_map, block_state), (start_maps, start_states) = lax.scan(
        advance, (eye_heads, zero_state), (transitions, writes)
    )
    through_query = jnp.einsum("hntc,nhcd->hntd", query_eff, start_maps, precision=peak_value)
    settled = (
        jnp.einsum("hntc,nhcd->hntd", query_eff, start_states, precision=peak_value) + local_part
    )
    incoming = entering((block_map, block_state), "ctx", compose_pair, (eye_heads, zero_state))[1]
    attended = settled + jnp.einsum("hntc,hcd->hntd", through_query, incoming, precision=peak_value)
    attended = attended.transpose(1, 2, 0, 3).reshape(row_count, head_count, HEAD_SIZE)
    mean_square = jnp.mean(attended * attended, axis=-1, keepdims=True)
    gate_values = jax.nn.sigmoid(
        out_gate.astype(jnp.float32).reshape(row_count, head_count, HEAD_SIZE)
    )
    gated_out = attended / jnp.sqrt(mean_square + 1e-05) * norm_gain * gate_values
    gated_out = gated_out.astype(jnp.bfloat16).reshape(row_count, head_count * HEAD_SIZE)
    return lax.psum_scatter(
        jnp.dot(gated_out, out_weight, preferred_element_type=jnp.float32).astype(jnp.bfloat16),
        "head",
        scatter_dimension=0,
        tiled=True,
    )


def solution(mesh):
    in_specs = (
        P("ctx", "head"),
        P("ctx", "head"),
        P("ctx", "head"),
        P("ctx", "head"),
        P("ctx", "head"),
        P("ctx", "head"),
        P(),
        P("head", None),
    )
    out_specs = P(("ctx", "head"), None)
    return jax.shard_map(
        on_device, mesh=mesh, in_specs=in_specs, out_specs=out_specs, check_vma=False
    )
```

profile of v0, /device:TPU:0, one launch (start us, length us, event | category | flops | bytes accessed | tf_op | source)
XLA Modules:
  0.0 320.3 jit_solution(16300474023155198462)
XLA Ops:
  7.5 1.3 convert_bitcast_fusion.2
  12.1 1.1 copy-done.6
  13.5 1.1 fusion.27
  14.7 0.9 copy.129
  15.6 3.2 exponential_multiply_fusion
  18.8 3.0 multiply_negate_fusion
  21.8 1.8 fusion.60
  23.6 1.8 fusion.61
  25.4 1.9 convolution_add_fusion.6
  27.3 1.8 fusion.62
  29.1 1.8 convolution_add_fusion.5
  30.9 1.9 fusion.63
  32.8 1.8 convolution_add_fusion.4
  34.7 1.8 fusion.64
  36.4 1.8 convolution_add_fusion.3
  38.3 1.8 convolution_add_fusion.2
  40.4 4.2 %fusion.15 = f32[8,6,64,256]{3,2,1,0:T(8,128)S(1)} fusion(f32[8,6,64,64]{3,2,1,0:T(8,128)S(1)} %convolution_add_fusion.2, f32[8,6,64,256]{3,0,2,1:T(8,128)S(1)} %pad_maximum_fusion), kind=kOutput, calls=%fused_computation.23 | convolution fusion | flops 603979776 | bytes 7077888 | tf_op jit(solution)/shard_map/hnts,hnsd->hntd/dot_general | solution.py:90
  44.6 5.7 %fusion.29 = f32[8,6,128,256]{3,2,1,0:T(8,128)S(1)} fusion(f32[8,6,64,256]{3,2,1,0:T(8,128)S(1)} %fusion.15, f32[8,6,64,128]{3,0,2,1:T(8,128)S(1)} %get-tuple-element.183), kind=kOutput, calls=%fused_computation.48 | convolution fusion | flops 1207959552 | bytes 11010048 | tf_op jit(solution)/shard_map/hnsc,hnsd->hncd/dot_general | solution.py:94
  50.3 3.2 slice_bitcast_fusion
  54.3 50.0 %while.30 = (s32[]{:T(128)}, f32[8,128,128]{2,1,0:T(8,128)}, f32[8,128,128]{2,1,0:T(8,128)}, f32[6,8,128,128]{3,2,0,1:T(8,128)}, f32[6,8,128,128]{3,2,0,1:T(8,12...) while((s32[]{:T(128)}, f32[8,128,128]{2,1,0:T(8,128)}, ...), condition=%wide.region_2.3_spmd.clone, body=%wide.region_1.2_spmd.clone.sunk | while | flops 403046400 | bytes 7865975 | solution.py:111
  54.3 1.0 copy.157
  55.3 1.0 copy.158
  56.4 1.1 bitcast_dynamic-update-slice_fusion.3
  57.5 2.7 convolution_add_fusion.10
  60.1 2.5 fusion.106
  62.6 1.0 copy.157
  63.7 1.0 copy.158
  64.7 1.1 bitcast_dynamic-update-slice_fusion.3
  65.8 2.7 convolution_add_fusion.10
  68.5 2.5 fusion.106
  71.0 1.0 copy.157
  72.0 1.0 copy.158
  73.1 1.1 bitcast_dynamic-update-slice_fusion.3
  74.2 2.7 convolution_add_fusion.10
  76.8 2.5 fusion.106
  79.3 1.0 copy.157
  80.3 1.0 copy.158
  81.4 1.1 bitcast_dynamic-update-slice_fusion.3
  82.5 2.7 convolution_add_fusion.10
  85.1 2.5 fusion.106
  87.6 1.0 copy.157
  88.7 1.0 copy.158
  89.7 1.1 bitcast_dynamic-update-slice_fusion.3
  90.8 2.7 convolution_add_fusion.10
  93.5 2.5 fusion.106
  96.0 1.0 copy.157
  97.0 1.0 copy.158
  98.0 1.1 bitcast_dynamic-update-slice_fusion.3
  99.1 2.7 convolution_add_fusion.10
  101.8 2.5 fusion.106
  105.5 4.8 %fusion.33 = f32[8,6,64,64]{3,2,1,0:T(8,128)S(1)} fusion(f32[8,6,64,128]{3,0,2,1:T(8,128)} %get-tuple-element.187, f32[8,6,64,128]{3,0,2,1:T(8,128)} %copy-done.2), kind=kOutput, calls=%fused_computation.52 | convolution fusion | flops 301989888 | bytes 3932160 | tf_op jit(solution)/shard_map/hntc,hnsc->hnts/dot_general | solution.py:87
  110.4 3.1 fusion.37
  113.7 1.5 copy-done.3
  115.2 1.0 copy-done.1
  116.1 1.0 copy_subtract_fusion
  117.1 0.9 copy-done.5
  118.0 4.3 %fusion.41 = f32[8,6,64,128]{3,2,1,0:T(8,128)} fusion(f32[6,8,128,128]{3,2,0,1:T(8,128)S(1)} %copy-done.5, f32[8,6,64,128]{3,0,2,1:T(8,128)S(1)} %copy_subtract_fusion), kind=kOutput, calls=%fused_computation.66 | convolution fusion | flops 603979776 | bytes 6291456 | tf_op jit(solution)/shard_map/hntc,nhcd->hntd/dot_general | solution.py:114
  122.4 57.6 %all-gather.5.cloned.1.call-done = f32[64,128,128]{2,1,0:T(8,128)} async-done(((f32[8,128,128]{2,1,0:T(8,128)}), f32[64,128,128]{2,1,0:T(8,128)}) %all-gather.5.cloned.1.call-update) | async-done | bytes 4194320 | tf_op jit(solution)/shard_map/all_gather | solution.py:15
  180.0 73.5 %all-gather.7.cloned.1.call-done = f32[64,128,128]{2,1,0:T(8,128)} async-done(((f32[8,128,128]{2,1,0:T(8,128)}), f32[64,128,128]{2,1,0:T(8,128)}) %all-gather.7.cloned.1.call-update) | async-done | bytes 4194320 | tf_op jit(solution)/shard_map/all_gather | solution.py:15
  253.7 3.1 fusion.51
  256.8 5.6 %multiply_reduce_fusion = (f32[6,64,8]{1,0,2:T(8,128)S(1)}, f32[6,64,8,128]{3,1,0,2:T(8,128)}) fusion(f32[8,6,64,128]{3,2,1,0:T(8,128)S(1)} %fusion.51, f32[8,6,64,256]{3,2,1,0:T(8,128)S(1)} %copy-done.4, f32[6,8,128,128]{3,2,0,1:T(8,128)} %get-tuple-element.89, f32[8,6,64,128]{3,0,2,1:T(8,128)S(1)} %copy_subtract_fusion), kind=kOutput, calls=%fused_computation.59 | convolution fusion | flops 605549568 | bytes 9449472 | tf_op jit(solution)/shard_map/hntc,nhcd->hntd/dot_general | solution.py:116
  262.5 2.3 copy.70
  266.0 6.0 %convolution_convert_fusion = bf16[384,2304]{1,0:T(8,128)(2,1)} fusion(bf16[1024,2304]{1,0:T(8,128)(2,1)} %param.19, f32[48,8,8,128]{3,2,1,0:T(8,128)S(1)} %bitcast.196, f32[48,8,8,128]{3,2,1,0:T(8,128)S(1)} %bitcast.195, bf16[384,1024]{1,0:T(8,128)(2,1)S(1)} %copy-done.9, f32[1024]{0:T(1024)S(1)} %broadcast_bitcast_fusion), kind=kOutput, calls=%fused_computation.18 | convolution fusion | flops 1815969792 | bytes 10424320 | tf_op jit(solution)/shard_map/dot_general | solution.py:128
  272.0 41.6 %reduce-scatter.2.cloned.1.call-done = bf16[96,2304]{1,0:T(8,128)(2,1)} async-done(((bf16[384,2304]{1,0:T(8,128)(2,1)}), bf16[96,2304]{1,0:T(8,128)(2,1)}) %reduce-scatter.2.cloned.1.call-update) | async-done | bytes 442384 | tf_op jit(solution)/shard_map/reduce_scatter | solution.py:127
  (50 shorter events, 8.4 us)
Async XLA Ops:
  6.5 108.6 %copy-start = (f32[128]{0:T(128)S(1)}, f32[128]{0:T(128)}, u32[]{:S(2)}) copy-start(f32[128]{0:T(128)} %param.18) | copy-start | bytes 1540
  6.5 173.4 %all-gather.5.cloned.1.call-start = ((), (), s32[]{:S(2)}) async-start(), calls=%async_computation.2 | async-start | bytes 4718592 | tf_op jit(solution)/shard_map/all_gather | solution.py:15
  8.8 1.1 copy-start.7
  10.5 1.1 copy-start.8
  11.8 1.4 copy-start.6
  18.8 3.0 copy-start.2
  104.3 149.1 %all-gather.7.cloned.1.call-start = ((), (), s32[]{:S(2)}) async-start(), calls=%async_computation.3 | async-start | bytes 4718592 | tf_op jit(solution)/shard_map/all_gather | solution.py:15
  105.1 208.5 %reduce-scatter.2.cloned.1.call-start = ((), (), s32[]{:S(2)}) async-start(), calls=%async_computation.1 | async-start | bytes 2211840 | tf_op jit(solution)/shard_map/reduce_scatter | solution.py:127
  113.5 1.7 copy-start.3
  113.5 2.6 copy-start.1
  116.1 1.9 copy-start.5
  253.7 3.1 copy-start.4
  264.8 1.1 copy-start.9
Sparse Core Ops, SparseCore 0:
  104.4 75.4 all-gather.4
  182.1 71.3 all-gather.6
  272.1 41.4 reduce-scatter.1
where the time goes:
time: 326 us; the launch traced here: 320 us
  waiting for transfers between devices  173 us (53%)
  matrix products  90.2 us (28%)
  local copies, waits for them, and re-layouts  26 us (8%)
  other arithmetic  16.3 us (5%)
  between operations  13.7 us (4%)
    all_gather x2, waiting for transfers between devices, entering(): gathered = jax.tree.map(lambda a: lax.all_gather(a, axis), part)  131 us
    reduce_scatter x1, waiting for transfers between devices, on_device(): lax.psum_scatter(jnp.dot(gated_out, out_weight, preferred_element_type=jn...  41.6 us
    dot_general x12, matrix products, chain_mul(): return jnp.einsum('hij,hjk->hik', left_map, right_map, precision=peak_value)  30.9 us
    while x12, local copies, waits for them, and re-layouts  12.5 us
    dot_general x5, matrix products, unit_lower_inverse(): jnp.einsum('hnts,hnsu->hntu', inverse, power, precision=peak_value)  9.29 us
    dot_general x5, matrix products, unit_lower_inverse(): power = jnp.einsum('hnts,hnsu->hntu', power, power, precision=peak_value)  8.93 us
    unnamed x24, local copies, waits for them, and re-layouts  7.82 us
    dynamic_update_slice x6, other arithmetic, on_device(): lax.scan(advance, (eye_heads, zero_state), (transitions, writes))  6.54 us
  transfers between devices with their start and end apart: 3, of which 3 were waited for; matrix products, arithmetic and copies ran while one was open for 4% of the time, Pallas kernels for 0%

commit v1 on v0

v1 whole, which is shorter than its diff:
```python
import functools

import jax
import jax.numpy as jnp
from jax import lax
from jax.experimental import pallas as pl
from jax.experimental.pallas import tpu as pltpu
from jax.sharding import PartitionSpec as P

HEAD_SIZE = 128
CHUNK = 128
PAIR = 2
F32 = jnp.float32
BF16 = jnp.bfloat16
NT = (((1,), (1,)), ((), ()))
TN = (((0,), (0,)), ((), ()))
NN = (((1,), (0,)), ((), ()))


def mm(left, right, dims=NN):
    return lax.dot_general(
        left.astype(BF16), right.astype(BF16), dims, preferred_element_type=F32
    )


def positions():
    later = lax.broadcasted_iota(jnp.int32, (CHUNK, CHUNK), 0)
    earlier = lax.broadcasted_iota(jnp.int32, (CHUNK, CHUNK), 1)
    return later, earlier


def maps_kernel(
    query_ref, key_ref, value_ref, decay_ref, rate_ref,
    map_ref, solved_ref, back_ref, now_ref, mid_ref, start_ref,
):
    chunk_count = key_ref.shape[0] // CHUNK
    first_head = pl.program_id(0) * PAIR
    later, earlier = positions()
    lower = (later >= earlier).astype(BF16)
    strict = later > earlier
    eye = (later == earlier).astype(F32)
    rates = rate_ref[...]
    rate_lane = lax.broadcasted_iota(jnp.int32, rates.shape, 1)
    units = [(i, j) for i in range(PAIR) for j in range(chunk_count)]
    rate_cols = [
        jnp.sum(jnp.where(rate_lane == first_head + i, rates, 0.0), axis=1, keepdims=True)
        for i in range(PAIR)
    ]

    def part(ref, unit):
        i, j = unit
        return ref[j * CHUNK : (j + 1) * CHUNK, i * HEAD_SIZE : (i + 1) * HEAD_SIZE]

    right, key_end, final, coupling, inverse = [], [], [], [], []
    for unit in units:
        i, j = unit
        rows = slice(j * CHUNK, (j + 1) * CHUNK)
        lanes = slice(i * HEAD_SIZE, (i + 1) * HEAD_SIZE)
        logs = part(decay_ref, unit)
        high = logs.astype(BF16)
        low = (logs - high.astype(F32)).astype(BF16)
        total = mm(lower, high) + mm(lower, low)
        middle = total[CHUNK // 2 - 1 : CHUNK // 2]
        last = total[CHUNK - 1 :]
        ahead = jnp.exp(total - middle)
        behind = jnp.exp(middle - total)
        mid_scale = jnp.exp(middle)
        keys = part(key_ref, unit).astype(F32)
        keys = keys * lax.rsqrt(jnp.sum(keys * keys, axis=1, keepdims=True) + 1e-06)
        rate = rate_cols[i][rows]
        key_now = keys * ahead
        key_back = keys * behind
        back_ref[rows, lanes] = key_back.astype(BF16)
        now_ref[rows, lanes] = (part(query_ref, unit).astype(F32) * ahead).astype(BF16)
        mid_ref[j : j + 1, lanes] = mid_scale
        coupling.append(jnp.where(strict, rate * mm(key_now, key_back, NT), 0.0))
        right.append(
            jnp.concatenate(
                [
                    (rate * key_now * mid_scale).astype(BF16),
                    (rate * part(value_ref, unit).astype(F32)).astype(BF16),
                ],
                axis=1,
            )
        )
        key_end.append((key_back * jnp.exp(last - middle)).astype(BF16))
        final.append(eye * jnp.exp(last))
    pair_mask = (later // 2) == (earlier // 2)
    inverse = [eye - jnp.where(pair_mask, c, 0.0) for c in coupling]
    width = 2
    while width < CHUNK:
        mask = ((later // (2 * width)) == (earlier // (2 * width))) & (
            (later // width) != (earlier // width)
        )
        inverse_low = [x.astype(BF16) for x in inverse]
        cross = [
            mm(x, jnp.where(mask, c, 0.0)).astype(BF16) for x, c in zip(inverse_low, coupling)
        ]
        inverse = [x - mm(y, z) for x, y, z in zip(inverse, cross, inverse_low)]
        width *= 2
    solved = [mm(x, r).astype(BF16) for x, r in zip(inverse, right)]
    carried = [mm(e, s, TN) for e, s in zip(key_end, solved)]
    for i in range(PAIR):
        running = None
        for j in range(chunk_count):
            u = i * chunk_count + j
            rows = slice(j * CHUNK, (j + 1) * CHUNK)
            solved_ref[rows, 2 * i * HEAD_SIZE : 2 * (i + 1) * HEAD_SIZE] = solved[u]
            step = final[u] - carried[u][:, :HEAD_SIZE]
            write = carried[u][:, HEAD_SIZE:]
            if running is None:
                running = jnp.concatenate([step, write], axis=1)
            else:
                held = running.astype(BF16)
                start_ref[i, j - 1] = held
                moved = mm(step, held)
                running = jnp.concatenate(
                    [moved[:, :HEAD_SIZE], moved[:, HEAD_SIZE:] + write], axis=1
                )
        map_ref[i] = running.astype(BF16)


def read_kernel(now_ref, back_ref, solved_ref, mid_ref, start_ref, through_ref, settled_ref):
    chunk_count = now_ref.shape[0] // CHUNK
    later, earlier = positions()
    lower = later >= earlier
    for i in range(PAIR):
        lanes = slice(i * HEAD_SIZE, (i + 1) * HEAD_SIZE)
        for j in range(chunk_count):
            rows = slice(j * CHUNK, (j + 1) * CHUNK)
            query = now_ref[rows, lanes]
            reading = jnp.where(lower, mm(query, back_ref[rows, lanes], NT), 0.0)
            mixed = mm(reading, solved_ref[rows, 2 * i * HEAD_SIZE : 2 * (i + 1) * HEAD_SIZE])
            effective = query.astype(F32) * mid_ref[j : j + 1, lanes] - mixed[:, :HEAD_SIZE]
            local = mixed[:, HEAD_SIZE:]
            if j:
                moved = mm(effective, start_ref[i, j - 1])
                through_ref[rows, lanes] = moved[:, :HEAD_SIZE].astype(BF16)
                settled_ref[rows, lanes] = moved[:, HEAD_SIZE:] + local
            else:
                through_ref[rows, lanes] = effective.astype(BF16)
                settled_ref[rows, lanes] = local


def chain_kernel(map_ref, state_ref):
    count = map_ref.shape[0]
    state = map_ref[0, :, HEAD_SIZE:].astype(F32)
    state_ref[0] = jnp.zeros((HEAD_SIZE, HEAD_SIZE), BF16)
    for turn in range(1, count):
        high = state.astype(BF16)
        state_ref[turn] = high
        if turn + 1 < count:
            low = (state - high.astype(F32)).astype(BF16)
            moved = mm(map_ref[turn, :, :HEAD_SIZE], jnp.concatenate([high, low], axis=1))
            state = (
                moved[:, :HEAD_SIZE]
                + moved[:, HEAD_SIZE:]
                + map_ref[turn, :, HEAD_SIZE:].astype(F32)
            )


def output_kernel(
    through_ref, settled_ref, gate_ref, state_ref, gain_ref, weight_ref, out_ref, gated_ref
):
    @pl.when(pl.program_id(0) == 0)
    def _():
        gain = gain_ref[...]
        for h in range(state_ref.shape[0]):
            lanes = slice(h * HEAD_SIZE, (h + 1) * HEAD_SIZE)
            attended = settled_ref[:, lanes] + mm(through_ref[:, lanes], state_ref[h])
            scale = lax.rsqrt(jnp.mean(attended * attended, axis=1, keepdims=True) + 1e-05)
            gate = jax.nn.sigmoid(gate_ref[:, lanes].astype(F32))
            gated_ref[:, lanes] = (attended * scale * gain * gate).astype(BF16)

    out_ref[...] = jnp.dot(
        gated_ref[...], weight_ref[...], preferred_element_type=F32
    ).astype(out_ref.dtype)


def entering(maps, axis):
    count = lax.axis_size(axis)
    head_count = maps.shape[0]
    if head_count == count:
        received = lax.all_to_all(maps, axis, 0, 0)
        states = pl.pallas_call(
            chain_kernel,
            out_shape=jax.ShapeDtypeStruct((count, HEAD_SIZE, HEAD_SIZE), BF16),
            name="chain",
        )(received)
        return lax.all_to_all(states, axis, 0, 0)
    gathered = lax.all_gather(maps, axis)

    def one(turn, state):
        item = lax.dynamic_index_in_dim(gathered, turn, 0, False)
        return (
            jnp.einsum(
                "hij,hjk->hik",
                item[..., :HEAD_SIZE].astype(F32),
                state,
                precision=lax.Precision.HIGHEST,
            )
            + item[..., HEAD_SIZE:]
        )

    zero = jnp.zeros((head_count, HEAD_SIZE, HEAD_SIZE), F32)
    return lax.fori_loop(0, lax.axis_index(axis), one, zero).astype(BF16)


def sum_heads(shares, axis):
    count = lax.axis_size(axis)
    if count % 2:
        return lax.psum_scatter(shares, axis, scatter_dimension=0, tiled=True)
    place = lax.axis_index(axis)
    core, chip = lax.rem(place, 2), lax.div(place, 2)
    chips = count // 2
    blocks = shares.reshape(chips, 2, shares.shape[0] // count, shares.shape[1])
    mine = lax.dynamic_index_in_dim(blocks, core, 1, False)
    other = lax.dynamic_index_in_dim(blocks, 1 - core, 1, False)
    came = lax.ppermute(other, axis, [(d, d ^ 1) for d in range(count)])
    both = mine.astype(F32) + came.astype(F32)
    total = lax.dynamic_index_in_dim(both, chip, 0, False)
    for turn in range(1, chips):
        target = lax.rem(chip + turn, chips)
        away = lax.dynamic_index_in_dim(both, target, 0, False).astype(BF16)
        hops = [(d, (d + 2 * turn) % count) for d in range(count)]
        total = total + lax.ppermute(away, axis, hops).astype(F32)
    return total.astype(BF16)


def on_device(
    query_vectors,
    key_vectors,
    value_vectors,
    log_decay,
    write_rate,
    out_gate,
    norm_gain,
    out_weight,
):
    rows, width = query_vectors.shape
    heads = width // HEAD_SIZE
    chunks = rows // CHUNK
    model = out_weight.shape[1]
    lanes = PAIR * HEAD_SIZE
    column = pl.BlockSpec((rows, lanes), lambda h: (0, h))
    double = pl.BlockSpec((rows, 2 * lanes), lambda h: (0, h))
    mid = pl.BlockSpec((chunks, lanes), lambda h: (0, h))
    start = pl.BlockSpec(
        (PAIR, chunks - 1, HEAD_SIZE, 2 * HEAD_SIZE), lambda h: (h, 0, 0, 0)
    )
    maps, solved, back, now, mids, starts = pl.pallas_call(
        maps_kernel,
        grid=(heads // PAIR,),
        in_specs=[
            column, column, column, column,
            pl.BlockSpec((rows, heads), lambda h: (0, 0)),
        ],
        out_specs=[
            pl.BlockSpec((PAIR, HEAD_SIZE, 2 * HEAD_SIZE), lambda h: (h, 0, 0)),
            double, column, column, mid, start,
        ],
        out_shape=[
            jax.ShapeDtypeStruct((heads, HEAD_SIZE, 2 * HEAD_SIZE), BF16),
            jax.ShapeDtypeStruct((rows, 2 * width), BF16),
            jax.ShapeDtypeStruct((rows, width), BF16),
            jax.ShapeDtypeStruct((rows, width), BF16),
            jax.ShapeDtypeStruct((chunks, width), F32),
            jax.ShapeDtypeStruct((heads, chunks - 1, HEAD_SIZE, 2 * HEAD_SIZE), BF16),
        ],
        compiler_params=pltpu.CompilerParams(vmem_limit_bytes=24 << 20),
        name="maps",
    )(query_vectors, key_vectors, value_vectors, log_decay, write_rate)
    through, settled = pl.pallas_call(
        read_kernel,
        grid=(heads // PAIR,),
        in_specs=[column, column, double, mid, start],
        out_specs=[column, column],
        out_shape=[
            jax.ShapeDtypeStruct((rows, width), BF16),
            jax.ShapeDtypeStruct((rows, width), F32),
        ],
        compiler_params=pltpu.CompilerParams(vmem_limit_bytes=16 << 20),
        name="read",
    )(now, back, solved, mids, starts)
    states = entering(maps, "ctx")
    tiles = 3 if model % (3 * 256) == 0 else 1
    whole = pl.BlockSpec((rows, width), lambda n: (0, 0))
    shares = pl.pallas_call(
        output_kernel,
        grid=(tiles,),
        in_specs=[
            whole, whole, whole,
            pl.BlockSpec((heads, HEAD_SIZE, HEAD_SIZE), lambda n: (0, 0, 0)),
            pl.BlockSpec((1, HEAD_SIZE), lambda n: (0, 0)),
            pl.BlockSpec((width, model // tiles), lambda n: (0, n)),
        ],
        out_specs=pl.BlockSpec((rows, model // tiles), lambda n: (0, n)),
        out_shape=jax.ShapeDtypeStruct((rows, model), BF16),
        scratch_shapes=[pltpu.VMEM((rows, width), BF16)],
        compiler_params=pltpu.CompilerParams(vmem_limit_bytes=32 << 20),
        name="output",
    )(through, settled, out_gate, states, norm_gain.reshape(1, HEAD_SIZE), out_weight)
    return sum_heads(shares, "head")


def solution(mesh):
    in_specs = (
        P("ctx", "head"),
        P("ctx", "head"),
        P("ctx", "head"),
        P("ctx", "head"),
        P("ctx", "head"),
        P("ctx", "head"),
        P(),
        P("head", None),
    )
    out_specs = P(("ctx", "head"), None)
    return jax.shard_map(
        on_device, mesh=mesh, in_specs=in_specs, out_specs=out_specs, check_vma=False
    )
```

time: 326 us -> 84.4 us (0.26); the launches traced: 320 us -> 83.6 us
  waiting for transfers between devices: 173 us -> 13.2 us
  matrix products: 90.2 us -> 0 us
  Pallas kernels: 0 us -> 23.2 us
  blocking collectives: 0 us -> 21.7 us
  other arithmetic: 16.3 us -> 2.18 us
  between operations: 13.7 us -> 0.15 us
  local copies, waits for them, and re-layouts: 26 us -> 17.5 us
  starting transfers between devices: 0.49 us -> 5.71 us
    all_gather x2 -> x0, waiting for transfers between devices: 131 us -> none  [entering(): gathered = jax.tree.map(lambda a: lax.all_gather(a, axis), part)]
    dot_general x32 -> x0, matrix products: 90.2 us -> none  [the longest x12 30.9 us: chain_mul(): return jnp.einsum('hij,hjk->hik', left_map, right_map, precision=peak_value)]
    reduce_scatter x1 -> x0, waiting for transfers between devices: 41.6 us -> none  [on_device(): lax.psum_scatter(jnp.dot(gated_out, out_weight, preferred_element_type=jn...]
    pallas_call x0 -> x4, Pallas kernels: none -> 23.2 us  [the longest x1 11.3 us: on_device(): pl.pallas_call(maps_kernel, grid=(heads // PAIR,), in_specs=[column, colu...]
    all_to_all x0 -> x1, blocking collectives: none -> 21.7 us  [entering(): received = lax.all_to_all(maps, axis, 0, 0)]
    ppermute x0 -> x2, waiting for transfers between devices: none -> 13.2 us  [the longest x1 10.7 us: sum_heads(): total = total + lax.ppermute(away, axis, hops).astype(F32)]
    while x12 -> x0, local copies, waits for them, and re-layouts: 12.5 us -> none
    unnamed x24 -> x31, local copies, waits for them, and re-layouts: 7.82 us -> 17.4 us
  transfers between devices with their start and end apart: 3 -> 3, of which waited for: 3 -> 2; matrix products, arithmetic and copies ran while one was open for 4% -> 0% of each run, Pallas kernels for 0% -> 6%
where the time goes in v1:
time: 84.4 us; the launch traced here: 83.6 us
  Pallas kernels  23.2 us (27%)
  blocking collectives  21.7 us (26%)
  local copies, waits for them, and re-layouts  17.5 us (21%)
  waiting for transfers between devices  13.2 us (16%)
  starting transfers between devices  5.71 us (7%)
  other arithmetic  2.18 us (3%)
    all_to_all x1, blocking collectives, entering(): received = lax.all_to_all(maps, axis, 0, 0)  21.7 us
    unnamed x31, local copies, waits for them, and re-layouts  17.4 us
    pallas_call x1, Pallas kernels, on_device(): pl.pallas_call(maps_kernel, grid=(heads // PAIR,), in_specs=[column, colu...  11.3 us
    ppermute x1, waiting for transfers between devices, sum_heads(): total = total + lax.ppermute(away, axis, hops).astype(F32)  10.7 us
    pallas_call x1, Pallas kernels, on_device(): pl.pallas_call(read_kernel, grid=(heads // PAIR,), in_specs=[column, colu...  4.8 us
    pallas_call x1, Pallas kernels, on_device(): pl.pallas_call(output_kernel, grid=(tiles,), in_specs=[whole, whole, whol...  4.42 us
    all_to_all x1, starting transfers between devices, entering(): return lax.all_to_all(states, axis, 0, 0)  4.05 us
    pallas_call x1, Pallas kernels, entering(): pl.pallas_call(chain_kernel, out_shape=jax.ShapeDtypeStruct((count, HEAD_...  2.69 us
  transfers between devices with their start and end apart: 3, of which 2 were waited for; matrix products, arithmetic and copies ran while one was open for 0% of the time, Pallas kernels for 6%

profile of v1, /device:TPU:0, one launch (start us, length us, event | category | flops | bytes accessed | tf_op | source)
XLA Modules:
  0.0 83.6 jit_solution(1794733946121262899)
XLA Ops:
  0.0 0.8 copy.9.rate_ref
  0.8 0.0 copy-start.1
  0.8 1.4 %copy-done.1 = f32[384,1024]{1,0:T(8,128)S(1)} copy-done((f32[384,1024]{1,0:T(8,128)S(1)}, f32[384,1024]{1,0:T(8,128)}, u32[]{:S(2)}) %copy-start.1) | copy-done | bytes 1572888
  2.2 0.0 copy-start.11
  2.3 1.1 %copy-done.11 = bf16[384,1024]{1,0:T(8,128)(2,1)S(1)} copy-done((bf16[384,1024]{1,0:T(8,128)(2,1)S(1)}, bf16[384,1024]{1,0:T(8,128)(2,1)}, u32[]{:S(2)}) %copy-start.11) | copy-done | bytes 786456
  3.4 0.0 copy-start.12
  3.4 1.1 %copy-done.12 = bf16[384,1024]{1,0:T(8,128)(2,1)S(1)} copy-done((bf16[384,1024]{1,0:T(8,128)(2,1)S(1)}, bf16[384,1024]{1,0:T(8,128)(2,1)}, u32[]{:S(2)}) %copy-start.12) | copy-done | bytes 786456
  4.5 0.0 copy-start.13
  4.5 1.1 %copy-done.13 = bf16[384,1024]{1,0:T(8,128)(2,1)S(1)} copy-done((bf16[384,1024]{1,0:T(8,128)(2,1)S(1)}, bf16[384,1024]{1,0:T(8,128)(2,1)}, u32[]{:S(2)}) %copy-start.13) | copy-done | bytes 786456
  5.7 11.3 %maps.1 = (bf16[8,128,256]{2,1,0:T(8,128)(2,1)S(1)}, bf16[384,2048]{1,0:T(8,128)(2,1)S(1)}, bf16[384,1024]{1,0:T(8,128)(2,1)S(1)}, bf16[384,1024]{1,0:T(8,128)(2...) custom-call(bf16[384,1024]{1,0:T(8,128)(2,1)S(1)} %copy-done.11, bf16[384,1024]{1,0:T(8,128)(2,1)S(1)} %copy-done.12, ...), custom_call_target="tpu_custom_call" | custom-call | tf_op jit(solution)/shard_map/maps/pallas_call | solution.py:251
  16.9 0.0 copy-start.2
  17.0 1.0 %copy-done.2 = bf16[8,2,128,256]{3,2,1,0:T(8,128)(2,1)} copy-done((bf16[8,2,128,256]{3,2,1,0:T(8,128)(2,1)}, bf16[8,2,128,256]{3,2,1,0:T(8,128)(2,1)S(1)}, u32[]{:S(2)}) %copy-start.2) | copy-done | bytes 1048600
  17.9 0.0 copy-start.5
  17.9 0.9 %copy-done.5 = bf16[384,1024]{1,0:T(8,128)(2,1)} copy-done((bf16[384,1024]{1,0:T(8,128)(2,1)}, bf16[384,1024]{1,0:T(8,128)(2,1)S(1)}, u32[]{:S(2)}) %copy-start.5) | copy-done | bytes 786456
  18.8 0.0 copy-start.7
  18.8 0.9 %copy-done.7 = bf16[384,1024]{1,0:T(8,128)(2,1)} copy-done((bf16[384,1024]{1,0:T(8,128)(2,1)}, bf16[384,1024]{1,0:T(8,128)(2,1)S(1)}, u32[]{:S(2)}) %copy-start.7) | copy-done | bytes 786456
  19.7 21.7 %all_to_all.10.map_ref = bf16[8,128,256]{2,1,0:T(8,128)(2,1)} all-to-all(bf16[8,128,256]{2,1,0:T(8,128)(2,1)S(1)} %get-tuple-element.20), channel_id=1, replica_groups=mesh['ctx'=8,'head'=4] {'ctx'}, dimensions={0} | all-to-all | bytes 1048576 | tf_op jit(solution)/shard_map/all_to_all | solution.py:184
  41.4 2.7 %chain.1 = bf16[8,128,128]{2,1,0:T(8,128)(2,1)} custom-call(bf16[8,128,256]{2,1,0:T(8,128)(2,1)} %all_to_all.10.map_ref), custom_call_target="tpu_custom_call" | custom-call | tf_op jit(solution)/shard_map/chain/pallas_call | solution.py:185
  44.1 4.0 %all-to-all-start.1 = ((bf16[8,128,128]{2,1,0:T(8,128)(2,1)}), bf16[8,128,128]{2,1,0:T(8,128)(2,1)}, u32[]{:S(2)}, u32[]{:S(2)}) async-start(bf16[8,128,128]{2,1,0:T(8,128)(2,1)} %chain.1), calls=%async_computation.1 | async-start | bytes 524288 | tf_op jit(solution)/shard_map/all_to_all | solution.py:190
  48.2 0.0 copy-start.3
  48.2 1.2 %copy-done.3 = bf16[8,2,128,256]{3,2,1,0:T(8,128)(2,1)S(1)} copy-done((bf16[8,2,128,256]{3,2,1,0:T(8,128)(2,1)S(1)}, bf16[8,2,128,256]{3,2,1,0:T(8,128)(2,1)}, u32[]{:S(2)}) %copy-start.3) | copy-done | bytes 1048600
  49.4 0.0 copy-start.6
  49.4 1.1 %copy-done.6 = bf16[384,1024]{1,0:T(8,128)(2,1)S(1)} copy-done((bf16[384,1024]{1,0:T(8,128)(2,1)S(1)}, bf16[384,1024]{1,0:T(8,128)(2,1)}, u32[]{:S(2)}) %copy-start.6) | copy-done | bytes 786456
  50.5 0.0 copy-start.8
  50.5 1.1 %copy-done.8 = bf16[384,1024]{1,0:T(8,128)(2,1)S(1)} copy-done((bf16[384,1024]{1,0:T(8,128)(2,1)S(1)}, bf16[384,1024]{1,0:T(8,128)(2,1)}, u32[]{:S(2)}) %copy-start.8) | copy-done | bytes 786456
  51.7 0.0 copy-start.14
  51.7 4.8 %read.1 = (bf16[384,1024]{1,0:T(8,128)(2,1)S(1)}, f32[384,1024]{1,0:T(8,128)S(1)}) custom-call(bf16[384,1024]{1,0:T(8,128)(2,1)S(1)} %copy-done.8, bf16[384,1024]{1,0:T(8,128)(2,1)S(1)} %copy-done.6, bf16[384,2048]{1,0:T(8,128)(2,1)S(1)} %get-tuple-element.15.solved_ref, f32[3,1024]{1,0:T(4,128)S(1)} %get-tuple-element.16.mid_ref, ...), custom_call_target="tpu_custom_call" | custom-call | tf_op jit(solution)/shard_map/read/pallas_call | solution.py:273
  56.5 0.0 copy-start.9
  56.5 0.9 %copy-done.9 = bf16[384,1024]{1,0:T(8,128)(2,1)} copy-done((bf16[384,1024]{1,0:T(8,128)(2,1)}, bf16[384,1024]{1,0:T(8,128)(2,1)S(1)}, u32[]{:S(2)}) %copy-start.9) | copy-done | bytes 786456
  57.4 0.0 all-to-all-done.1.state_ref
  57.4 0.0 copy-done.14
  57.4 0.0 copy-start
  57.4 2.3 %copy-done = bf16[1024,2304]{1,0:T(8,128)(2,1)S(1)} copy-done((bf16[1024,2304]{1,0:T(8,128)(2,1)S(1)}, bf16[1024,2304]{1,0:T(8,128)(2,1)}, u32[]{:S(2)}) %copy-start) | copy-done | bytes 4718616
  59.7 0.0 copy-start.4
  59.7 1.1 %copy-done.4 = bf16[384,1024]{1,0:T(8,128)(2,1)S(1)} copy-done((bf16[384,1024]{1,0:T(8,128)(2,1)S(1)}, bf16[384,1024]{1,0:T(8,128)(2,1)}, u32[]{:S(2)}) %copy-start.4) | copy-done | bytes 786456
  60.8 0.0 copy-start.10
  60.8 1.1 %copy-done.10 = bf16[384,1024]{1,0:T(8,128)(2,1)S(1)} copy-done((bf16[384,1024]{1,0:T(8,128)(2,1)S(1)}, bf16[384,1024]{1,0:T(8,128)(2,1)}, u32[]{:S(2)}) %copy-start.10) | copy-done | bytes 786456
  62.0 4.4 %output.1 = bf16[384,2304]{1,0:T(8,128)(2,1)S(1)} custom-call(bf16[384,1024]{1,0:T(8,128)(2,1)S(1)} %copy-done.10, f32[384,1024]{1,0:T(8,128)S(1)} %get-tuple-element.19.settled_ref, bf16[384,1024]{1,0:T(8,128)(2,1)S(1)} %copy-done.4, bf16[8,128,128]{2,1,0:T(8,128)(2,1)} %all-to-all-done.1.state_ref, f32[1,128]{1,0:T(1,128)S(1)} %bitcast.17, ...), custom_call_target="tpu_custom_call" | custom-call | tf_op jit(solution)/shard_map/output/pallas_call | solution.py:288
  66.4 0.1 dynamic-slice_bitcast_fusion
  66.5 0.1 collective-permute-start
  66.6 2.5 %collective-permute-done = bf16[2,96,2304]{2,1,0:T(8,128)(2,1)} collective-permute-done((bf16[2,96,2304]{2,1,0:T(8,128)(2,1)S(1)}, bf16[2,96,2304]{2,1,0:T(8,128)(2,1)}, u32[]{:S(2)}, u32[]{:S(2)}) %collective-permute-start) | collective-permute-done | bytes 884768 | tf_op jit(solution)/shard_map/ppermute | solution.py:219
  69.1 1.3 %convert_add_fusion = f32[2,96,2304]{2,1,0:T(8,128)S(1)} fusion(bf16[2,96,2304]{2,1,0:T(8,128)(2,1)} %collective-permute-done, bf16[2,2,96,2304]{3,2,1,0:T(8,128)(2,1)S(1)} %bitcast.16, s32[]{:T(128)S(6)} %select_n.14), kind=kLoop, calls=%fused_computation | loop fusion | flops 1327104 | bytes 3538948 | tf_op jit(solution)/shard_map/add | solution.py:220
  70.5 0.1 fusion.1
  70.5 1.6 %collective-permute-start.1 = (bf16[96,2304]{1,0:T(8,128)(2,1)S(1)}, bf16[96,2304]{1,0:T(8,128)(2,1)S(1)}, u32[]{:S(2)}, u32[]{:S(2)}) collective-permute-start(bf16[96,2304]{1,0:T(8,128)(2,1)S(1)} %fusion.1), channel_id=1, source_target_pairs={{0,2},{1,3},{2,0},{3,1},{4,6},{5,7},{6,4},{7,5},{8,10},{9,11},{10,... | collective-permute-start | bytes 1327112 | tf_op jit(solution)/shard_map/ppermute | solution.py:226
  72.1 10.7 %collective-permute-done.1 = bf16[96,2304]{1,0:T(8,128)(2,1)S(1)} collective-permute-done((bf16[96,2304]{1,0:T(8,128)(2,1)S(1)}, bf16[96,2304]{1,0:T(8,128)(2,1)S(1)}, u32[]{:S(2)}, u32[]{:S(2)}) %collective-permute-start.1) | collective-permute-done | bytes 442400 | tf_op jit(solution)/shard_map/ppermute | solution.py:226
  82.8 0.8 fusion
Async XLA Ops:
  0.8 1.4 %copy-start.1 = (f32[384,1024]{1,0:T(8,128)S(1)}, f32[384,1024]{1,0:T(8,128)}, u32[]{:S(2)}) copy-start(f32[384,1024]{1,0:T(8,128)} %decay_ref.1) | copy-start | bytes 4718596
  2.2 1.1 %copy-start.11 = (bf16[384,1024]{1,0:T(8,128)(2,1)S(1)}, bf16[384,1024]{1,0:T(8,128)(2,1)}, u32[]{:S(2)}) copy-start(bf16[384,1024]{1,0:T(8,128)(2,1)} %query_ref.1) | copy-start | bytes 2359300
  3.4 1.1 %copy-start.12 = (bf16[384,1024]{1,0:T(8,128)(2,1)S(1)}, bf16[384,1024]{1,0:T(8,128)(2,1)}, u32[]{:S(2)}) copy-start(bf16[384,1024]{1,0:T(8,128)(2,1)} %key_ref.1) | copy-start | bytes 2359300
  4.5 1.1 %copy-start.13 = (bf16[384,1024]{1,0:T(8,128)(2,1)S(1)}, bf16[384,1024]{1,0:T(8,128)(2,1)}, u32[]{:S(2)}) copy-start(bf16[384,1024]{1,0:T(8,128)(2,1)} %value_ref.1) | copy-start | bytes 2359300
  16.9 1.0 %copy-start.2 = (bf16[8,2,128,256]{3,2,1,0:T(8,128)(2,1)}, bf16[8,2,128,256]{3,2,1,0:T(8,128)(2,1)S(1)}, u32[]{:S(2)}) copy-start(bf16[8,2,128,256]{3,2,1,0:T(8,128)(2,1)S(1)} %get-tuple-element.17.start_ref) | copy-start | bytes 3145732
  17.9 0.9 %copy-start.5 = (bf16[384,1024]{1,0:T(8,128)(2,1)}, bf16[384,1024]{1,0:T(8,128)(2,1)S(1)}, u32[]{:S(2)}) copy-start(bf16[384,1024]{1,0:T(8,128)(2,1)S(1)} %get-tuple-element.14.back_ref) | copy-start | bytes 2359300
  18.8 0.9 %copy-start.7 = (bf16[384,1024]{1,0:T(8,128)(2,1)}, bf16[384,1024]{1,0:T(8,128)(2,1)S(1)}, u32[]{:S(2)}) copy-start(bf16[384,1024]{1,0:T(8,128)(2,1)S(1)} %get-tuple-element.13.now_ref) | copy-start | bytes 2359300
  44.1 13.3 %all-to-all-start.1 = ((bf16[8,128,128]{2,1,0:T(8,128)(2,1)}), bf16[8,128,128]{2,1,0:T(8,128)(2,1)}, u32[]{:S(2)}, u32[]{:S(2)}) async-start(bf16[8,128,128]{2,1,0:T(8,128)(2,1)} %chain.1), calls=%async_computation.1 | async-start | bytes 524288 | tf_op jit(solution)/shard_map/all_to_all | solution.py:190
  48.2 1.2 %copy-start.3 = (bf16[8,2,128,256]{3,2,1,0:T(8,128)(2,1)S(1)}, bf16[8,2,128,256]{3,2,1,0:T(8,128)(2,1)}, u32[]{:S(2)}) copy-start(bf16[8,2,128,256]{3,2,1,0:T(8,128)(2,1)} %copy-done.2) | copy-start | bytes 3145732
  49.4 1.1 %copy-start.6 = (bf16[384,1024]{1,0:T(8,128)(2,1)S(1)}, bf16[384,1024]{1,0:T(8,128)(2,1)}, u32[]{:S(2)}) copy-start(bf16[384,1024]{1,0:T(8,128)(2,1)} %copy-done.5) | copy-start | bytes 2359300
  50.5 1.1 %copy-start.8 = (bf16[384,1024]{1,0:T(8,128)(2,1)S(1)}, bf16[384,1024]{1,0:T(8,128)(2,1)}, u32[]{:S(2)}) copy-start(bf16[384,1024]{1,0:T(8,128)(2,1)} %copy-done.7) | copy-start | bytes 2359300
  51.7 5.7 %copy-start.14 = (f32[128]{0:T(128)S(1)}, f32[128]{0:T(128)}, u32[]{:S(2)}) copy-start(f32[128]{0:T(128)} %param.14) | copy-start | bytes 1540
  56.5 0.9 %copy-start.9 = (bf16[384,1024]{1,0:T(8,128)(2,1)}, bf16[384,1024]{1,0:T(8,128)(2,1)S(1)}, u32[]{:S(2)}) copy-start(bf16[384,1024]{1,0:T(8,128)(2,1)S(1)} %get-tuple-element.18.through_ref) | copy-start | bytes 2359300
  57.4 2.3 %copy-start = (bf16[1024,2304]{1,0:T(8,128)(2,1)S(1)}, bf16[1024,2304]{1,0:T(8,128)(2,1)}, u32[]{:S(2)}) copy-start(bf16[1024,2304]{1,0:T(8,128)(2,1)} %weight_ref.1) | copy-start | bytes 14155780
  59.7 1.1 %copy-start.4 = (bf16[384,1024]{1,0:T(8,128)(2,1)S(1)}, bf16[384,1024]{1,0:T(8,128)(2,1)}, u32[]{:S(2)}) copy-start(bf16[384,1024]{1,0:T(8,128)(2,1)} %gate_ref.1) | copy-start | bytes 2359300
  60.8 1.1 %copy-start.10 = (bf16[384,1024]{1,0:T(8,128)(2,1)S(1)}, bf16[384,1024]{1,0:T(8,128)(2,1)}, u32[]{:S(2)}) copy-start(bf16[384,1024]{1,0:T(8,128)(2,1)} %copy-done.9) | copy-start | bytes 2359300
  66.5 2.6 %collective-permute-start = (bf16[2,96,2304]{2,1,0:T(8,128)(2,1)S(1)}, bf16[2,96,2304]{2,1,0:T(8,128)(2,1)}, u32[]{:S(2)}, u32[]{:S(2)}) collective-permute-start(bf16[2,96,2304]{2,1,0:T(8,128)(2,1)S(1)} %dynamic-slice_bitcast_fusion), channel_id=1, source_target_pairs={{0,1},{1,0},{2,3},{3,2},{4,5},{5,4},{6,7},{7,6},{8,9},{9,8},{10,11... | collective-permute-start | bytes 2654216 | tf_op jit(solution)/shard_map/ppermute | solution.py:219
  70.5 12.3 %collective-permute-start.1 = (bf16[96,2304]{1,0:T(8,128)(2,1)S(1)}, bf16[96,2304]{1,0:T(8,128)(2,1)S(1)}, u32[]{:S(2)}, u32[]{:S(2)}) collective-permute-start(bf16[96,2304]{1,0:T(8,128)(2,1)S(1)} %fusion.1), channel_id=1, source_target_pairs={{0,2},{1,3},{2,0},{3,1},{4,6},{5,7},{6,4},{7,5},{8,10},{9,11},{10,... | collective-permute-start | bytes 1327112 | tf_op jit(solution)/shard_map/ppermute | solution.py:226

commit v2 on v1

v2 whole, which is shorter than its diff:
```python
import functools

import jax
import jax.numpy as jnp
from jax import lax
from jax.experimental import pallas as pl
from jax.experimental.pallas import tpu as pltpu
from jax.sharding import PartitionSpec as P


HEAD_SIZE = 128
CHUNK = 128
PAIR = 2
LIMIT = 60
F32 = jnp.float32
BF16 = jnp.bfloat16
NT = (((1,), (1,)), ((), ()))
TN = (((0,), (0,)), ((), ()))
NN = (((1,), (0,)), ((), ()))


def mm(left, right, dims=NN):
    return lax.dot_general(
        left.astype(BF16), right.astype(BF16), dims, preferred_element_type=F32
    )


def positions():
    later = lax.broadcasted_iota(jnp.int32, (CHUNK, CHUNK), 0)
    earlier = lax.broadcasted_iota(jnp.int32, (CHUNK, CHUNK), 1)
    return later, earlier


def maps_kernel(
    top, slots, place_ref, query_ref, key_ref, value_ref, decay_ref, rate_ref, *refs
):
    slot_refs = refs[-(5 + slots) : -5]
    solved_ref, back_ref, now_ref, mid_ref, start_ref = refs[-5:]
    chunk_count = key_ref.shape[0] // CHUNK
    place = place_ref[0]
    first_head = ((place // PAIR) ^ (top - pl.program_id(0))) * PAIR
    later, earlier = positions()
    lower = (later >= earlier).astype(BF16)
    strict = later > earlier
    eye = (later == earlier).astype(F32)
    rates = rate_ref[...].T
    rate_lane = lax.broadcasted_iota(jnp.int32, rates.shape, 1)
    units = [(i, j) for i in range(PAIR) for j in range(chunk_count)]
    rate_cols = [
        jnp.sum(jnp.where(rate_lane == first_head + i, rates, 0.0), axis=1, keepdims=True)
        for i in range(PAIR)
    ]

    def part(ref, unit):
        i, j = unit
        return ref[j * CHUNK : (j + 1) * CHUNK, i * HEAD_SIZE : (i + 1) * HEAD_SIZE]

    right, key_end, final, coupling, inverse = [], [], [], [], []
    for unit in units:
        i, j = unit
        rows = slice(j * CHUNK, (j + 1) * CHUNK)
        lanes = slice(i * HEAD_SIZE, (i + 1) * HEAD_SIZE)
        logs = part(decay_ref, unit)
        high = logs.astype(BF16)
        low = (logs - high.astype(F32)).astype(BF16)
        total = mm(lower, high) + mm(lower, low)
        middle = total[CHUNK // 2 - 1 : CHUNK // 2]
        last = total[CHUNK - 1 :]
        ahead = jnp.exp(total - middle)
        behind = jnp.exp(middle - total)
        mid_scale = jnp.exp(middle)
        keys = part(key_ref, unit).astype(F32)
        keys = keys * lax.rsqrt(jnp.sum(keys * keys, axis=1, keepdims=True) + 1e-06)
        rate = rate_cols[i][rows]
        key_now = keys * ahead
        key_back = keys * behind
        back_ref[rows, lanes] = key_back.astype(BF16)
        now_ref[rows, lanes] = (part(query_ref, unit).astype(F32) * ahead).astype(BF16)
        mid_ref[j : j + 1, lanes] = mid_scale
        coupling.append(jnp.where(strict, rate * mm(key_now, key_back, NT), 0.0))
        right.append(
            jnp.concatenate(
                [
                    (rate * key_now * mid_scale).astype(BF16),
                    (rate * part(value_ref, unit).astype(F32)).astype(BF16),
                ],
                axis=1,
            )
        )
        key_end.append((key_back * jnp.exp(last - middle)).astype(BF16))
        final.append(eye * jnp.exp(last))
    pair_mask = (later // 2) == (earlier // 2)
    inverse = [eye - jnp.where(pair_mask, c, 0.0) for c in coupling]
    width = 2
    while width < CHUNK:
        mask = ((later // (2 * width)) == (earlier // (2 * width))) & (
            (later // width) != (earlier // width)
        )
        inverse_low = [x.astype(BF16) for x in inverse]
        cross = [
            mm(x, jnp.where(mask, c, 0.0)).astype(BF16) for x, c in zip(inverse_low, coupling)
        ]
        inverse = [x - mm(y, z) for x, y, z in zip(inverse, cross, inverse_low)]
        width *= 2
    solved = [mm(x, r).astype(BF16) for x, r in zip(inverse, right)]
    carried = [mm(e, s, TN) for e, s in zip(key_end, solved)]
    results = []
    for i in range(PAIR):
        running = None
        for j in range(chunk_count):
            u = i * chunk_count + j
            rows = slice(j * CHUNK, (j + 1) * CHUNK)
            solved_ref[rows, 2 * i * HEAD_SIZE : 2 * (i + 1) * HEAD_SIZE] = solved[u]
            step = final[u] - carried[u][:, :HEAD_SIZE]
            write = carried[u][:, HEAD_SIZE:]
            if running is None:
                running = jnp.concatenate([step, write], axis=1)
            else:
                held = running.astype(BF16)
                start_ref[i, j - 1] = held
                moved = mm(step, held)
                running = jnp.concatenate(
                    [moved[:, :HEAD_SIZE], moved[:, HEAD_SIZE:] + write], axis=1
                )
        results.append(running.astype(BF16))
    odd = (place & 1) == 1
    pair = [jnp.where(odd, results[1 - i], results[i]) for i in range(PAIR)]
    for s in range(slots // PAIR):

        @pl.when(pl.program_id(0) == s)
        def _():
            for i in range(PAIR):
                slot_refs[slots - PAIR * (s + 1) + i][...] = pair[i]


def read_kernel(now_ref, back_ref, solved_ref, mid_ref, start_ref, through_ref, settled_ref):
    chunk_count = now_ref.shape[0] // CHUNK
    later, earlier = positions()
    lower = later >= earlier
    for i in range(PAIR):
        lanes = slice(i * HEAD_SIZE, (i + 1) * HEAD_SIZE)
        for j in range(chunk_count):
            rows = slice(j * CHUNK, (j + 1) * CHUNK)
            query = now_ref[rows, lanes]
            reading = jnp.where(lower, mm(query, back_ref[rows, lanes], NT), 0.0)
            mixed = mm(reading, solved_ref[rows, 2 * i * HEAD_SIZE : 2 * (i + 1) * HEAD_SIZE])
            effective = query.astype(F32) * mid_ref[j : j + 1, lanes] - mixed[:, :HEAD_SIZE]
            local = mixed[:, HEAD_SIZE:]
            if j:
                moved = mm(effective, start_ref[i, j - 1])
                through_ref[rows, lanes] = moved[:, :HEAD_SIZE].astype(BF16)
                settled_ref[rows, lanes] = moved[:, HEAD_SIZE:] + local
            else:
                through_ref[rows, lanes] = effective.astype(BF16)
                settled_ref[rows, lanes] = local


def chain_kernel(place_ref, *refs):
    count = len(refs) - 2
    state_ref, map_ref = refs[count:]
    place = place_ref[0]
    for slot in range(count):
        map_ref[slot] = refs[slot][...]
    state = map_ref[place, :, HEAD_SIZE:].astype(F32)
    state_ref[0] = jnp.zeros((HEAD_SIZE, HEAD_SIZE), BF16)
    for turn in range(1, count):
        high = state.astype(BF16)
        state_ref[turn] = high
        if turn + 1 < count:
            slot = turn ^ place
            low = (state - high.astype(F32)).astype(BF16)
            moved = mm(map_ref[slot, :, :HEAD_SIZE], jnp.concatenate([high, low], axis=1))
            state = (
                moved[:, :HEAD_SIZE]
                + moved[:, HEAD_SIZE:]
                + map_ref[slot, :, HEAD_SIZE:].astype(F32)
            )


def output_kernel(
    place_ref, through_hbm, settled_hbm, gate_hbm, state_ref, gain_ref, weight_hbm,
    other_ref, mine_ref, through_ref, settled_ref, gate_ref, weight_ref, gated_ref, sems,
):
    core = place_ref[0]
    chips, block = other_ref.shape[:2]
    _, width = through_ref.shape
    heads = state_ref.shape[0]
    halves = 2
    span = width // halves
    tiles, tile = weight_ref.shape[0], weight_ref.shape[2]
    sources = [(through_hbm, through_ref), (settled_hbm, settled_ref), (gate_hbm, gate_ref)]
    copies, count = [], 0
    for half in range(halves):
        group = []
        for source, target in sources:
            for side in range(2):
                for chip in range(chips):
                    first = (2 * chip + (core if side else 1 - core)) * block
                    place = (side * chips + chip) * block
                    copy = pltpu.make_async_copy(
                        source.at[
                            pl.ds(pl.multiple_of(first, block), block),
                            pl.ds(half * span, span),
                        ],
                        target.at[pl.ds(place, block), pl.ds(half * span, span)],
                        sems.at[count],
                    )
                    copy.start()
                    group.append(copy)
                    count += 1
        copies.append(group)
    weights = []
    for n in range(tiles):
        copy = pltpu.make_async_copy(
            weight_hbm.at[:, pl.ds(n * tile, tile)], weight_ref.at[n], sems.at[count]
        )
        copy.start()
        weights.append(copy)
        count += 1
    gain = gain_ref[...]
    for half in range(halves):
        for copy in copies[half]:
            copy.wait()
        for h in range(half * heads // halves, (half + 1) * heads // halves):
            lanes = slice(h * HEAD_SIZE, (h + 1) * HEAD_SIZE)
            attended = settled_ref[:, lanes] + mm(through_ref[:, lanes], state_ref[h])
            scale = lax.rsqrt(jnp.mean(attended * attended, axis=1, keepdims=True) + 1e-05)
            gate = jax.nn.sigmoid(gate_ref[:, lanes].astype(F32))
            gated_ref[:, lanes] = (attended * scale * gain * gate).astype(BF16)
    for n in range(tiles):
        weights[n].wait()
        product = jnp.dot(gated_ref[...], weight_ref[n], preferred_element_type=F32)
        for side, target in enumerate((other_ref, mine_ref)):
            for chip in range(chips):
                place = (side * chips + chip) * block
                target[chip, :, n * tile : (n + 1) * tile] = product[
                    place : place + block
                ].astype(BF16)


def make_maps(operands, place, tops, previous):
    queries = operands[0]
    rows, width = queries.shape
    heads = operands[4].shape[0]
    chunks = rows // CHUNK
    lanes = PAIR * HEAD_SIZE
    top = max(tops)

    def pair(step, place_ref):
        return (place_ref[0] // PAIR) ^ (top - step)

    column = pl.BlockSpec((rows, lanes), lambda s, p: (0, pair(s, p)))
    slots = PAIR * len(tops)
    shapes = [jax.ShapeDtypeStruct((HEAD_SIZE, 2 * HEAD_SIZE), BF16)] * slots + [
        jax.ShapeDtypeStruct((rows, 2 * width), BF16),
        jax.ShapeDtypeStruct((rows, width), BF16),
        jax.ShapeDtypeStruct((rows, width), BF16),
        jax.ShapeDtypeStruct((chunks, width), F32),
        jax.ShapeDtypeStruct((heads, chunks - 1, HEAD_SIZE, 2 * HEAD_SIZE), BF16),
    ]
    share = len(tops) * PAIR * chunks
    return pl.pallas_call(
        functools.partial(maps_kernel, top, slots),
        grid_spec=pltpu.PrefetchScalarGridSpec(
            num_scalar_prefetch=1,
            grid=(len(tops),),
            in_specs=[column] * 4
            + [pl.BlockSpec((heads, rows), lambda s, p: (0, 0))]
            + [pl.BlockSpec(memory_space=pl.ANY)] * len(previous),
            out_specs=[pl.BlockSpec((HEAD_SIZE, 2 * HEAD_SIZE), lambda s, p: (0, 0))] * slots
            + [
                pl.BlockSpec((rows, 2 * lanes), lambda s, p: (0, pair(s, p))),
                column,
                column,
                pl.BlockSpec((chunks, lanes), lambda s, p: (0, pair(s, p))),
                pl.BlockSpec(
                    (PAIR, chunks - 1, HEAD_SIZE, 2 * HEAD_SIZE),
                    lambda s, p: (pair(s, p), 0, 0, 0),
                ),
            ],
        ),
        out_shape=shapes,
        input_output_aliases={6 + n: slots + n for n in range(len(previous))},
        cost_estimate=pl.CostEstimate(
            flops=share * 120_000_000, bytes_accessed=share * 400_000, transcendentals=0
        ),
        compiler_params=pltpu.CompilerParams(vmem_limit_bytes=LIMIT << 20),
        name="maps",
    )(place, *operands, *previous)


def finish_reading(held):
    solved, back, now, mids, starts = held
    rows, width = now.shape
    heads = width // HEAD_SIZE
    chunks = rows // CHUNK
    lanes = PAIR * HEAD_SIZE
    column = pl.BlockSpec((rows, lanes), lambda h: (0, h))
    return pl.pallas_call(
        read_kernel,
        grid=(heads // PAIR,),
        in_specs=[
            column,
            column,
            pl.BlockSpec((rows, 2 * lanes), lambda h: (0, h)),
            pl.BlockSpec((chunks, lanes), lambda h: (0, h)),
            pl.BlockSpec(
                (PAIR, chunks - 1, HEAD_SIZE, 2 * HEAD_SIZE), lambda h: (h, 0, 0, 0)
            ),
        ],
        out_specs=[column, column],
        out_shape=[
            jax.ShapeDtypeStruct((rows, width), BF16),
            jax.ShapeDtypeStruct((rows, width), F32),
        ],
        cost_estimate=pl.CostEstimate(
            flops=heads * chunks * 100_000_000,
            bytes_accessed=heads * chunks * 400_000,
            transcendentals=0,
        ),
        compiler_params=pltpu.CompilerParams(vmem_limit_bytes=LIMIT << 20),
        name="read",
    )(now, back, solved, mids, starts)


def project(core, through, settled, gates, states, gain, weight, groups):
    rows, width = through.shape
    heads = states.shape[0]
    model = weight.shape[1]
    chips = groups // 2
    block = rows // groups
    tiles = 3 if model % (3 * 256) == 0 else 1
    hbm = pl.BlockSpec(memory_space=pltpu.HBM)
    share = pl.BlockSpec((chips, block, model), lambda n, p: (0, 0, 0))
    return pl.pallas_call(
        output_kernel,
        grid_spec=pltpu.PrefetchScalarGridSpec(
            num_scalar_prefetch=1,
            grid=(1,),
            in_specs=[
                hbm,
                hbm,
                hbm,
                pl.BlockSpec((heads, HEAD_SIZE, HEAD_SIZE), lambda n, p: (0, 0, 0)),
                pl.BlockSpec((1, HEAD_SIZE), lambda n, p: (0, 0)),
                hbm,
            ],
            out_specs=[share, share],
            scratch_shapes=[
                pltpu.VMEM((rows, width), BF16),
                pltpu.VMEM((rows, width), F32),
                pltpu.VMEM((rows, width), BF16),
                pltpu.VMEM((tiles, width, model // tiles), BF16),
                pltpu.VMEM((rows, width), BF16),
                pltpu.SemaphoreType.DMA((12 * chips + tiles,)),
            ],
        ),
        out_shape=[jax.ShapeDtypeStruct((chips, block, model), BF16)] * 2,
        cost_estimate=pl.CostEstimate(
            flops=2 * rows * width * model,
            bytes_accessed=2 * width * model,
            transcendentals=0,
        ),
        compiler_params=pltpu.CompilerParams(vmem_limit_bytes=LIMIT << 20),
        name="output",
    )(
        jnp.reshape(core, (1,)).astype(jnp.int32),
        through,
        settled,
        gates,
        states,
        gain.reshape(1, HEAD_SIZE),
        weight,
    )


def carry_apart(operands, place, axis):
    count = lax.axis_size(axis)
    place_at = jnp.reshape(place, (1,)).astype(jnp.int32)

    def swap(block, turn):
        return lax.ppermute(block, axis, [(d, d ^ turn) for d in range(count)])

    pairs = count // PAIR
    half = pairs // 2
    received = [None] * count
    far = make_maps(operands, place_at, range(half, pairs), [])
    for r in range(PAIR * half, count):
        received[r] = swap(far[r - PAIR * half], r)
    near = make_maps(operands, place_at, range(half), far[-5:])
    received[0] = near[0]
    for r in range(1, PAIR * half):
        received[r] = swap(near[r], r)
    reads = finish_reading(near[-5:])
    block = pl.BlockSpec((HEAD_SIZE, 2 * HEAD_SIZE), lambda n, p: (0, 0))
    states = pl.pallas_call(
        chain_kernel,
        grid_spec=pltpu.PrefetchScalarGridSpec(
            num_scalar_prefetch=1,
            grid=(1,),
            in_specs=[block] * count,
            out_specs=pl.BlockSpec((count, HEAD_SIZE, HEAD_SIZE), lambda n, p: (0, 0, 0)),
            scratch_shapes=[pltpu.VMEM((count, HEAD_SIZE, 2 * HEAD_SIZE), BF16)],
        ),
        out_shape=jax.ShapeDtypeStruct((count, HEAD_SIZE, HEAD_SIZE), BF16),
        compiler_params=pltpu.CompilerParams(vmem_limit_bytes=8 << 20),
        name="chain",
    )(place_at, *received)
    return reads, lax.all_to_all(states, axis, 0, 0)


def carry_whole(operands, axis):
    heads = operands[4].shape[0]
    made = make_maps(operands, jnp.zeros((1,), jnp.int32), range(heads // PAIR), [])
    gathered = lax.all_gather(jnp.stack(made[:heads]), axis)

    def one(turn, state):
        item = lax.dynamic_index_in_dim(gathered, turn, 0, False).astype(F32)
        moved = jnp.einsum(
            "hij,hjk->hik", item[..., :HEAD_SIZE], state, precision=lax.Precision.HIGHEST
        )
        return moved + item[..., HEAD_SIZE:]

    zero = jnp.zeros((heads, HEAD_SIZE, HEAD_SIZE), F32)
    state = lax.fori_loop(0, lax.axis_index(axis), one, zero)
    return finish_reading(made[heads:]), state.astype(BF16)


def on_device(
    query_vectors,
    key_vectors,
    value_vectors,
    log_decay,
    write_rate,
    out_gate,
    norm_gain,
    out_weight,
):
    heads = query_vectors.shape[1] // HEAD_SIZE
    operands = [query_vectors, key_vectors, value_vectors, log_decay, write_rate.T]
    count = lax.axis_size("ctx")
    if heads == count and count & (count - 1) == 0 and count >= 4:
        reads, states = carry_apart(operands, lax.axis_index("ctx"), "ctx")
    else:
        reads, states = carry_whole(operands, "ctx")
    groups = lax.axis_size("head")
    place = lax.axis_index("head")
    core, chip = lax.rem(place, 2), lax.div(place, 2)
    chips = groups // 2

    other, mine = project(core, *reads, out_gate, states, norm_gain, out_weight, groups)
    came = lax.ppermute(other, "head", [(d, d ^ 1) for d in range(groups)])

    def both(block):
        return lax.dynamic_index_in_dim(mine, block, 0, False).astype(
            F32
        ) + lax.dynamic_index_in_dim(came, block, 0, False).astype(F32)

    total = both(chip)
    for turn in range(1, chips):
        away = both(lax.rem(chip + turn, chips)).astype(BF16)
        hops = [(d, (d + 2 * turn) % groups) for d in range(groups)]
        total = total + lax.ppermute(away, "head", hops).astype(F32)
    return total.astype(BF16)


def solution(mesh):
    in_specs = (
        P("ctx", "head"),
        P("ctx", "head"),
        P("ctx", "head"),
        P("ctx", "head"),
        P("ctx", "head"),
        P("ctx", "head"),
        P(),
        P("head", None),
    )
    out_specs = P(("ctx", "head"), None)

    return jax.shard_map(
        on_device, mesh=mesh, in_specs=in_specs, out_specs=out_specs, check_vma=False
    )
```

time: 84.4 us -> 76.3 us (0.904)
  blocking collectives: 21.7 us -> 0 us
  local copies, waits for them, and re-layouts: 17.5 us -> 1.56 us
  starting transfers between devices: 5.71 us -> 18.2 us
  waiting for transfers between devices: 13.2 us -> 22.1 us
  Pallas kernels: 23.2 us -> 31.8 us
    all_to_all x1 -> x0, blocking collectives: 21.7 us -> none  [entering(): received = lax.all_to_all(maps, axis, 0, 0)]
    unnamed x31 -> x14, local copies, waits for them, and re-layouts: 17.4 us -> 1.56 us
    ppermute x2 -> x9, starting transfers between devices: 1.66 us -> 14.2 us  [the longest x7 12.5 us: swap(): return lax.ppermute(block, axis, [(d, d ^ turn) for d in range(count)])]
    pallas_call x4 -> x5, Pallas kernels: 23.2 us -> 31.8 us  [the longest x2 15.7 us: make_maps(): pl.pallas_call(functools.partial(maps_kernel, top, slots), grid_spec=pltp...]
    ppermute x2 -> x9, waiting for transfers between devices: 13.2 us -> 20.3 us  [the longest x1 10.7 us: on_device(): total = total + lax.ppermute(away, 'head', hops).astype(F32)]
    all_to_all x1, waiting for transfers between devices: 0.01 us -> 1.78 us  [carry_apart(): return (reads, lax.all_to_all(states, axis, 0, 0))]
    add x1 -> x0, other arithmetic: 1.34 us -> none  [sum_heads(): both = mine.astype(F32) + came.astype(F32)]
    convert_element_type x1 -> x2, other arithmetic: 0.84 us -> 2.04 us  [the longest x1 1.12 us: on_device(): away = both(lax.rem(chip + turn, chips)).astype(BF16)]
  transfers between devices with their start and end apart: 3 -> 10, of which waited for: 2 -> 5; matrix products, arithmetic and copies ran while one was open for 0% -> 0% of each run, Pallas kernels for 6% -> 9%
where the time goes in v2:
time: 76.3 us; the launch traced here: 75.8 us
  Pallas kernels  31.8 us (42%)
  waiting for transfers between devices  22.1 us (29%)
  starting transfers between devices  18.2 us (24%)
  other arithmetic  2.04 us (3%)
  local copies, waits for them, and re-layouts  1.56 us (2%)
    pallas_call x2, Pallas kernels, make_maps(): pl.pallas_call(functools.partial(maps_kernel, top, slots), grid_spec=pltp...  15.7 us
    ppermute x7, starting transfers between devices, swap(): return lax.ppermute(block, axis, [(d, d ^ turn) for d in range(count)])  12.5 us
    ppermute x1, waiting for transfers between devices, on_device(): total = total + lax.ppermute(away, 'head', hops).astype(F32)  10.7 us
    pallas_call x1, Pallas kernels, project(): pl.pallas_call(output_kernel, grid_spec=pltpu.PrefetchScalarGridSpec(num_...  7.56 us
    ppermute x7, waiting for transfers between devices, swap(): return lax.ppermute(block, axis, [(d, d ^ turn) for d in range(count)])  7.02 us
    pallas_call x1, Pallas kernels, finish_reading(): pl.pallas_call(read_kernel, grid=(heads // PAIR,), in_specs=[column, colu...  6.89 us
    all_to_all x1, starting transfers between devices, carry_apart(): return (reads, lax.all_to_all(states, axis, 0, 0))  4.03 us
    ppermute x1, waiting for transfers between devices, on_device(): came = lax.ppermute(other, 'head', [(d, d ^ 1) for d in range(groups)])  2.61 us
  transfers between devices with their start and end apart: 10, of which 5 were waited for; matrix products, arithmetic and copies ran while one was open for 0% of the time, Pallas kernels for 9%

profile of v2, /device:TPU:0, one launch (start us, length us, event | category | flops | bytes accessed | tf_op | source)
XLA Modules:
  0.0 75.8 jit_solution(9247550956010886543)
XLA Ops:
  0.0 7.8 %maps.2 = (bf16[128,256]{1,0:T(8,128)(2,1)}, bf16[128,256]{1,0:T(8,128)(2,1)}, bf16[128,256]{1,0:T(8,128)(2,1)}, bf16[128,256]{1,0:T(8,128)(2,1)}, bf16[384,2048...) custom-call(s32[1]{0:T(128)} %bitcast.1.place_ref, ...), custom_call_target="tpu_custom_call" | custom-call | flops 1440000000 | bytes 4800000 | tf_op jit(solution)/shard_map/maps/pallas_call | solution.py:262
  7.8 0.0 copy-start.6
  7.8 0.0 copy-start.5
  7.8 0.0 copy-start.4
  7.8 0.0 copy-start.3
  7.8 7.9 %maps.3 = (bf16[128,256]{1,0:T(8,128)(2,1)}, bf16[128,256]{1,0:T(8,128)(2,1)}, bf16[128,256]{1,0:T(8,128)(2,1)}, bf16[128,256]{1,0:T(8,128)(2,1)}, bf16[384,2048...) custom-call(s32[1]{0:T(128)} %bitcast.1.place_ref, ...), custom_call_target="tpu_custom_call", output_to_operand_aliasing={{4}: (6, {}), {5}: (7, {}), {6}: (8, {}), {7}: (9, {}), {8}... | custom-call | flops 1440000000 | bytes 4800000 | tf_op jit(solution)/shard_map/maps/pallas_call | solution.py:262
  15.7 3.0 %collective-permute-start = (bf16[128,256]{1,0:T(8,128)(2,1)}, bf16[128,256]{1,0:T(8,128)(2,1)S(1)}, u32[]{:S(2)}, u32[]{:S(2)}) collective-permute-start(bf16[128,256]{1,0:T(8,128)(2,1)} %get-tuple-element.40), channel_id=1, source_target_pairs={{0,4},{4,0},{8,12},{12,8},{16,20},{20,16},{24,28},{28,24},{1,5},{5... | collective-permute-start | bytes 196616 | tf_op jit(solution)/shard_map/ppermute | solution.py:382
  18.8 1.5 %collective-permute-start.1 = (bf16[128,256]{1,0:T(8,128)(2,1)}, bf16[128,256]{1,0:T(8,128)(2,1)S(1)}, u32[]{:S(2)}, u32[]{:S(2)}) collective-permute-start(bf16[128,256]{1,0:T(8,128)(2,1)} %get-tuple-element.41), channel_id=1, source_target_pairs={{0,8},{4,12},{8,0},{12,4},{16,24},{20,28},{24,16},{28,20},{1,9},{5... | collective-permute-start | bytes 196616 | tf_op jit(solution)/shard_map/ppermute | solution.py:382
  20.3 0.0 collective-permute-start.2
  20.3 0.0 copy-done.6
  20.3 3.0 %collective-permute-start.3 = (bf16[128,256]{1,0:T(8,128)(2,1)S(1)}, bf16[128,256]{1,0:T(8,128)(2,1)S(1)}, u32[]{:S(2)}, u32[]{:S(2)}) collective-permute-start(bf16[128,256]{1,0:T(8,128)(2,1)S(1)} %copy-done.6), channel_id=1, source_target_pairs={{0,16},{4,20},{8,24},{12,28},{16,0},{20,4},{24,8},{28,12},{1,17},{... | collective-permute-start | bytes 196616 | tf_op jit(solution)/shard_map/ppermute | solution.py:382
  23.3 0.0 copy-done.5
  23.3 1.3 %collective-permute-start.4 = (bf16[128,256]{1,0:T(8,128)(2,1)S(1)}, bf16[128,256]{1,0:T(8,128)(2,1)S(1)}, u32[]{:S(2)}, u32[]{:S(2)}) collective-permute-start(bf16[128,256]{1,0:T(8,128)(2,1)S(1)} %copy-done.5), channel_id=1, source_target_pairs={{0,20},{4,16},{8,28},{12,24},{16,4},{20,0},{24,12},{28,8},{1,21},{... | collective-permute-start | bytes 196616 | tf_op jit(solution)/shard_map/ppermute | solution.py:382
  24.6 0.0 collective-permute-done.refs_1_
  24.6 0.0 copy-done.4
  24.6 3.6 %collective-permute-start.5 = (bf16[128,256]{1,0:T(8,128)(2,1)S(1)}, bf16[128,256]{1,0:T(8,128)(2,1)S(1)}, u32[]{:S(2)}, u32[]{:S(2)}) collective-permute-start(bf16[128,256]{1,0:T(8,128)(2,1)S(1)} %copy-done.4), channel_id=1, source_target_pairs={{0,24},{4,28},{8,16},{12,20},{16,8},{20,12},{24,0},{28,4},{1,25},{... | collective-permute-start | bytes 196616 | tf_op jit(solution)/shard_map/ppermute | solution.py:382
  28.2 0.0 collective-permute-done.1.refs_2_
  28.2 0.0 copy-done.3
  28.2 0.0 collective-permute-start.6
  28.3 0.0 collective-permute-done.2.refs_3_
  28.3 0.0 collective-permute-done.3.refs_4_
  28.3 5.4 %collective-permute-done.4.refs_5_ = bf16[128,256]{1,0:T(8,128)(2,1)S(1)} collective-permute-done((bf16[128,256]{1,0:T(8,128)(2,1)S(1)}, bf16[128,256]{1,0:T(8,128)(2,1)S(1)}, u32[]{:S(2)}, u32[]{:S(2)}) %collective-permute-start.4) | collective-permute-done | bytes 65568 | tf_op jit(solution)/shard_map/ppermute | solution.py:382
  33.7 0.0 collective-permute-done.5.refs_6_
  33.7 1.6 %collective-permute-done.6.refs_7_ = bf16[128,256]{1,0:T(8,128)(2,1)S(1)} collective-permute-done((bf16[128,256]{1,0:T(8,128)(2,1)S(1)}, bf16[128,256]{1,0:T(8,128)(2,1)S(1)}, u32[]{:S(2)}, u32[]{:S(2)}) %collective-permute-start.6) | collective-permute-done | bytes 65568 | tf_op jit(solution)/shard_map/ppermute | solution.py:382
  35.3 0.0 copy-start
  35.3 0.8 %copy-done = bf16[128,256]{1,0:T(8,128)(2,1)S(1)} copy-done((bf16[128,256]{1,0:T(8,128)(2,1)S(1)}, bf16[128,256]{1,0:T(8,128)(2,1)}, u32[]{:S(2)}) %copy-start) | copy-done | bytes 65560
  36.1 1.7 %chain.1 = bf16[8,128,128]{2,1,0:T(8,128)(2,1)} custom-call(s32[1]{0:T(128)} %bitcast.1.place_ref, bf16[128,256]{1,0:T(8,128)(2,1)S(1)} %copy-done, bf16[128,256]{1,0:T(8,128)(2,1)S(1)} %collective-permute-done.refs_1_, bf16[128,256]{1,0:T(8,128)(2,1)S(1)} %collective-permute-done.1.refs_2_, bf16[128,256]{1,0:T(8,128)(2,1)S(1)} %collective-permute-done.2.refs_3_, ...), custom_call_target="tpu_custom_call" | custom-call | tf_op jit(solution)/shard_map/chain/pallas_call | solution.py:396
  37.8 4.0 %all-to-all-start = ((bf16[8,128,128]{2,1,0:T(8,128)(2,1)}), bf16[8,128,128]{2,1,0:T(8,128)(2,1)S(1)}, u32[]{:S(2)}, u32[]{:S(2)}) async-start(bf16[8,128,128]{2,1,0:T(8,128)(2,1)} %chain.1), calls=%async_computation | async-start | bytes 524288 | tf_op jit(solution)/shard_map/all_to_all | solution.py:409
  41.8 6.9 %read.1 = (bf16[384,1024]{1,0:T(8,128)(2,1)}, f32[384,1024]{1,0:T(8,128)}) custom-call(bf16[384,1024]{1,0:T(8,128)(2,1)} %get-tuple-element.32.now_ref, bf16[384,1024]{1,0:T(8,128)(2,1)} %get-tuple-element.33.back_ref, bf16[384,2048]{1,0:T(8,128)(2,1)} %get-tuple-element.34.solved_ref, f32[3,1024]{1,0:T(4,128)} %get-tuple-element.35.mid_ref, ...), custom_call_target="tpu_custom_call" | custom-call | flops 2400000000 | bytes 9600000 | tf_op jit(solution)/shard_map/read/pallas_call | solution.py:299
  48.7 1.8 %all-to-all-done.state_ref = bf16[8,128,128]{2,1,0:T(8,128)(2,1)S(1)} async-done(((bf16[8,128,128]{2,1,0:T(8,128)(2,1)}), bf16[8,128,128]{2,1,0:T(8,128)(2,1)S(1)}, u32[]{:S(2)}, u32[]{:S(2)}) %all-to-all-start) | async-done | bytes 262176 | tf_op jit(solution)/shard_map/all_to_all | solution.py:409
  50.5 0.0 copy-start.1
  50.5 0.7 copy-done.1
  51.2 7.6 %output.1 = (bf16[2,96,2304]{2,1,0:T(8,128)(2,1)}, bf16[2,96,2304]{2,1,0:T(8,128)(2,1)}) custom-call(s32[1]{0:T(128)} %bitcast.place_ref, bf16[384,1024]{1,0:T(8,128)(2,1)} %get-tuple-element.37.through_hbm, f32[384,1024]{1,0:T(8,128)} %get-tuple-element.38.settled_hbm, bf16[384,1024]{1,0:T(8,128)(2,1)} %gate_hbm.1, bf16[8,128,128]{2,1,0:T(8,128)(2,1)} %copy-done.1, ...), custom_call_target="tpu_custom_call" | custom-call | flops 1811939328 | bytes 4718592 | tf_op jit(solution)/shard_map/output/pallas_call | solution.py:335
  58.8 0.0 copy-start.2
  58.8 0.1 collective-permute-start.7
  58.9 2.6 %collective-permute-done.7 = bf16[2,96,2304]{2,1,0:T(8,128)(2,1)S(1)} collective-permute-done((bf16[2,96,2304]{2,1,0:T(8,128)(2,1)}, bf16[2,96,2304]{2,1,0:T(8,128)(2,1)S(1)}, u32[]{:S(2)}, u32[]{:S(2)}) %collective-permute-start.7) | collective-permute-done | bytes 884768 | tf_op jit(solution)/shard_map/ppermute | solution.py:452
  61.5 1.1 %fusion.1 = bf16[96,2304]{1,0:T(8,128)(2,1)S(1)} fusion(bf16[2,96,2304]{2,1,0:T(8,128)(2,1)S(1)} %collective-permute-done.7, s32[]{:T(128)S(6)} %select_n.10, bf16[2,96,2304]{2,1,0:T(8,128)(2,1)} %get-tuple-element.47), kind=kLoop, calls=%fused_computation.3 | loop fusion | flops 884736 | bytes 1327108 | tf_op jit(solution)/shard_map/convert_element_type | solution.py:461
  62.6 1.6 %collective-permute-start.8 = (bf16[96,2304]{1,0:T(8,128)(2,1)S(1)}, bf16[96,2304]{1,0:T(8,128)(2,1)S(1)}, u32[]{:S(2)}, u32[]{:S(2)}) collective-permute-start(bf16[96,2304]{1,0:T(8,128)(2,1)S(1)} %fusion.1), channel_id=1, source_target_pairs={{0,2},{1,3},{2,0},{3,1},{4,6},{5,7},{6,4},{7,5},{8,10},{9,11},{10,... | collective-permute-start | bytes 1327112 | tf_op jit(solution)/shard_map/ppermute | solution.py:463
  64.2 10.7 %collective-permute-done.8 = bf16[96,2304]{1,0:T(8,128)(2,1)S(1)} collective-permute-done((bf16[96,2304]{1,0:T(8,128)(2,1)S(1)}, bf16[96,2304]{1,0:T(8,128)(2,1)S(1)}, u32[]{:S(2)}, u32[]{:S(2)}) %collective-permute-start.8) | collective-permute-done | bytes 442400 | tf_op jit(solution)/shard_map/ppermute | solution.py:463
  74.9 0.0 copy-done.2
  74.9 0.9 %fusion = bf16[96,2304]{1,0:T(8,128)(2,1)} fusion(bf16[96,2304]{1,0:T(8,128)(2,1)S(1)} %collective-permute-done.8, bf16[2,96,2304]{2,1,0:T(8,128)(2,1)S(1)} %collective-permute-done.7, s32[]{:T(128)S(6)} %select_n.9, bf16[2,96,2304]{2,1,0:T(8,128)(2,1)S(1)} %copy-done.2), kind=kLoop, calls=%fused_computation.1 | loop fusion | flops 1327104 | bytes 1769476 | tf_op jit(solution)/shard_map/convert_element_type | solution.py:464
Async XLA Ops:
  7.8 12.5 %copy-start.6 = (bf16[128,256]{1,0:T(8,128)(2,1)S(1)}, bf16[128,256]{1,0:T(8,128)(2,1)}, u32[]{:S(2)}) copy-start(bf16[128,256]{1,0:T(8,128)(2,1)} %get-tuple-element.43) | copy-start | bytes 196612
  7.8 15.5 %copy-start.5 = (bf16[128,256]{1,0:T(8,128)(2,1)S(1)}, bf16[128,256]{1,0:T(8,128)(2,1)}, u32[]{:S(2)}) copy-start(bf16[128,256]{1,0:T(8,128)(2,1)} %get-tuple-element.44) | copy-start | bytes 196612
  7.8 16.8 %copy-start.4 = (bf16[128,256]{1,0:T(8,128)(2,1)S(1)}, bf16[128,256]{1,0:T(8,128)(2,1)}, u32[]{:S(2)}) copy-start(bf16[128,256]{1,0:T(8,128)(2,1)} %get-tuple-element.45) | copy-start | bytes 196612
  7.8 20.4 %copy-start.3 = (bf16[128,256]{1,0:T(8,128)(2,1)S(1)}, bf16[128,256]{1,0:T(8,128)(2,1)}, u32[]{:S(2)}) copy-start(bf16[128,256]{1,0:T(8,128)(2,1)} %get-tuple-element.46) | copy-start | bytes 196612
  15.7 8.9 %collective-permute-start = (bf16[128,256]{1,0:T(8,128)(2,1)}, bf16[128,256]{1,0:T(8,128)(2,1)S(1)}, u32[]{:S(2)}, u32[]{:S(2)}) collective-permute-start(bf16[128,256]{1,0:T(8,128)(2,1)} %get-tuple-element.40), channel_id=1, source_target_pairs={{0,4},{4,0},{8,12},{12,8},{16,20},{20,16},{24,28},{28,24},{1,5},{5... | collective-permute-start | bytes 196616 | tf_op jit(solution)/shard_map/ppermute | solution.py:382
  18.8 9.4 %collective-permute-start.1 = (bf16[128,256]{1,0:T(8,128)(2,1)}, bf16[128,256]{1,0:T(8,128)(2,1)S(1)}, u32[]{:S(2)}, u32[]{:S(2)}) collective-permute-start(bf16[128,256]{1,0:T(8,128)(2,1)} %get-tuple-element.41), channel_id=1, source_target_pairs={{0,8},{4,12},{8,0},{12,4},{16,24},{20,28},{24,16},{28,20},{1,9},{5... | collective-permute-start | bytes 196616 | tf_op jit(solution)/shard_map/ppermute | solution.py:382
  20.3 8.0 %collective-permute-start.2 = (bf16[128,256]{1,0:T(8,128)(2,1)}, bf16[128,256]{1,0:T(8,128)(2,1)S(1)}, u32[]{:S(2)}, u32[]{:S(2)}) collective-permute-start(bf16[128,256]{1,0:T(8,128)(2,1)} %get-tuple-element.42), channel_id=1, source_target_pairs={{0,12},{4,8},{8,4},{12,0},{16,28},{20,24},{24,20},{28,16},{1,13},{... | collective-permute-start | bytes 196616 | tf_op jit(solution)/shard_map/ppermute | solution.py:382
  20.3 8.0 %collective-permute-start.3 = (bf16[128,256]{1,0:T(8,128)(2,1)S(1)}, bf16[128,256]{1,0:T(8,128)(2,1)S(1)}, u32[]{:S(2)}, u32[]{:S(2)}) collective-permute-start(bf16[128,256]{1,0:T(8,128)(2,1)S(1)} %copy-done.6), channel_id=1, source_target_pairs={{0,16},{4,20},{8,24},{12,28},{16,0},{20,4},{24,8},{28,12},{1,17},{... | collective-permute-start | bytes 196616 | tf_op jit(solution)/shard_map/ppermute | solution.py:382
  23.3 10.4 %collective-permute-start.4 = (bf16[128,256]{1,0:T(8,128)(2,1)S(1)}, bf16[128,256]{1,0:T(8,128)(2,1)S(1)}, u32[]{:S(2)}, u32[]{:S(2)}) collective-permute-start(bf16[128,256]{1,0:T(8,128)(2,1)S(1)} %copy-done.5), channel_id=1, source_target_pairs={{0,20},{4,16},{8,28},{12,24},{16,4},{20,0},{24,12},{28,8},{1,21},{... | collective-permute-start | bytes 196616 | tf_op jit(solution)/shard_map/ppermute | solution.py:382
  24.6 9.1 %collective-permute-start.5 = (bf16[128,256]{1,0:T(8,128)(2,1)S(1)}, bf16[128,256]{1,0:T(8,128)(2,1)S(1)}, u32[]{:S(2)}, u32[]{:S(2)}) collective-permute-start(bf16[128,256]{1,0:T(8,128)(2,1)S(1)} %copy-done.4), channel_id=1, source_target_pairs={{0,24},{4,28},{8,16},{12,20},{16,8},{20,12},{24,0},{28,4},{1,25},{... | collective-permute-start | bytes 196616 | tf_op jit(solution)/shard_map/ppermute | solution.py:382
  28.2 7.1 %collective-permute-start.6 = (bf16[128,256]{1,0:T(8,128)(2,1)S(1)}, bf16[128,256]{1,0:T(8,128)(2,1)S(1)}, u32[]{:S(2)}, u32[]{:S(2)}) collective-permute-start(bf16[128,256]{1,0:T(8,128)(2,1)S(1)} %copy-done.3), channel_id=1, source_target_pairs={{0,28},{4,24},{8,20},{12,16},{16,12},{20,8},{24,4},{28,0},{1,29},{... | collective-permute-start | bytes 196616 | tf_op jit(solution)/shard_map/ppermute | solution.py:382
  35.3 0.8 %copy-start = (bf16[128,256]{1,0:T(8,128)(2,1)S(1)}, bf16[128,256]{1,0:T(8,128)(2,1)}, u32[]{:S(2)}) copy-start(bf16[128,256]{1,0:T(8,128)(2,1)} %get-tuple-element.39.refs_0_) | copy-start | bytes 196612
  37.8 12.7 %all-to-all-start = ((bf16[8,128,128]{2,1,0:T(8,128)(2,1)}), bf16[8,128,128]{2,1,0:T(8,128)(2,1)S(1)}, u32[]{:S(2)}, u32[]{:S(2)}) async-start(bf16[8,128,128]{2,1,0:T(8,128)(2,1)} %chain.1), calls=%async_computation | async-start | bytes 524288 | tf_op jit(solution)/shard_map/all_to_all | solution.py:409
  50.5 0.7 copy-start.1
  58.8 16.1 %copy-start.2 = (bf16[2,96,2304]{2,1,0:T(8,128)(2,1)S(1)}, bf16[2,96,2304]{2,1,0:T(8,128)(2,1)}, u32[]{:S(2)}) copy-start(bf16[2,96,2304]{2,1,0:T(8,128)(2,1)} %get-tuple-element.47) | copy-start | bytes 2654212
  58.8 2.7 %collective-permute-start.7 = (bf16[2,96,2304]{2,1,0:T(8,128)(2,1)}, bf16[2,96,2304]{2,1,0:T(8,128)(2,1)S(1)}, u32[]{:S(2)}, u32[]{:S(2)}) collective-permute-start(bf16[2,96,2304]{2,1,0:T(8,128)(2,1)} %get-tuple-element.48), channel_id=1, source_target_pairs={{0,1},{1,0},{2,3},{3,2},{4,5},{5,4},{6,7},{7,6},{8,9},{9,8},{10,11... | collective-permute-start | bytes 2654216 | tf_op jit(solution)/shard_map/ppermute | solution.py:452
  62.6 12.3 %collective-permute-start.8 = (bf16[96,2304]{1,0:T(8,128)(2,1)S(1)}, bf16[96,2304]{1,0:T(8,128)(2,1)S(1)}, u32[]{:S(2)}, u32[]{:S(2)}) collective-permute-start(bf16[96,2304]{1,0:T(8,128)(2,1)S(1)} %fusion.1), channel_id=1, source_target_pairs={{0,2},{1,3},{2,0},{3,1},{4,6},{5,7},{6,4},{7,5},{8,10},{9,11},{10,... | collective-permute-start | bytes 1327112 | tf_op jit(solution)/shard_map/ppermute | solution.py:463

commit v3 on v2

--- a/solution.py
+++ b/solution.py
@@ -11,7 +11,7 @@
 HEAD_SIZE = 128
 CHUNK = 128
 PAIR = 2
-LIMIT = 60
+LIMIT = 24
 F32 = jnp.float32
 BF16 = jnp.bfloat16
 NT = (((1,), (1,)), ((), ()))
@@ -32,13 +32,11 @@
 
 
 def maps_kernel(
-    top, slots, place_ref, query_ref, key_ref, value_ref, decay_ref, rate_ref, *refs
+    first_ref, query_ref, key_ref, value_ref, decay_ref, rate_ref, *refs
 ):
-    slot_refs = refs[-(5 + slots) : -5]
-    solved_ref, back_ref, now_ref, mid_ref, start_ref = refs[-5:]
+    map_ref, solved_ref, back_ref, now_ref, mid_ref, start_ref = refs[-6:]
     chunk_count = key_ref.shape[0] // CHUNK
-    place = place_ref[0]
-    first_head = ((place // PAIR) ^ (top - pl.program_id(0))) * PAIR
+    first_head = (first_ref[0] + pl.program_id(0)) * PAIR
     later, earlier = positions()
     lower = (later >= earlier).astype(BF16)
     strict = later > earlier
@@ -104,7 +102,6 @@
         width *= 2
     solved = [mm(x, r).astype(BF16) for x, r in zip(inverse, right)]
     carried = [mm(e, s, TN) for e, s in zip(key_end, solved)]
-    results = []
     for i in range(PAIR):
         running = None
         for j in range(chunk_count):
@@ -122,15 +119,7 @@
                 running = jnp.concatenate(
                     [moved[:, :HEAD_SIZE], moved[:, HEAD_SIZE:] + write], axis=1
                 )
-        results.append(running.astype(BF16))
-    odd = (place & 1) == 1
-    pair = [jnp.where(odd, results[1 - i], results[i]) for i in range(PAIR)]
-    for s in range(slots // PAIR):
-
-        @pl.when(pl.program_id(0) == s)
-        def _():
-            for i in range(PAIR):
-                slot_refs[slots - PAIR * (s + 1) + i][...] = pair[i]
+        map_ref[i] = running.astype(BF16)
 
 
 def read_kernel(now_ref, back_ref, solved_ref, mid_ref, start_ref, through_ref, settled_ref):
@@ -155,33 +144,78 @@
                 settled_ref[rows, lanes] = local
 
 
+def follow(later, earlier):
+    moved = mm(later[:, :HEAD_SIZE], earlier)
+    width = earlier.shape[1]
+    if width == HEAD_SIZE:
+        return moved + later[:, HEAD_SIZE:].astype(F32)
+    return jnp.concatenate(
+        [
+            moved[:, :HEAD_SIZE],
+            moved[:, HEAD_SIZE:] + later[:, HEAD_SIZE:].astype(F32),
+        ],
+        axis=1,
+    )
+
+
+def join_kernel(place_ref, own_ref, came_ref, early_ref, *refs):
+    slots, joined_ref = refs[:-1], refs[-1]
+    second = place_ref[0] == 1
+    for j in range(own_ref.shape[0]):
+        own, came = own_ref[j], came_ref[j]
+        early = jnp.where(second, came, own)
+        early_ref[j] = early
+        joined_ref[j] = follow(jnp.where(second, own, came), early).astype(BF16)
+    for r in range(len(slots)):
+        slots[r][...] = joined_ref[place_ref[1] ^ r]
+
+
 def chain_kernel(place_ref, *refs):
-    count = len(refs) - 2
-    state_ref, map_ref = refs[count:]
-    place = place_ref[0]
-    for slot in range(count):
-        map_ref[slot] = refs[slot][...]
+    count = (len(refs) - 2) // 2
+    came, slots = refs[:count], refs[count : 2 * count]
+    map_ref, state_ref = refs[2 * count :]
+    place = place_ref[1]
+    for r in range(count):
+        map_ref[r] = came[r][...]
+    state_ref[0] = jnp.zeros((HEAD_SIZE, HEAD_SIZE), BF16)
     state = map_ref[place, :, HEAD_SIZE:].astype(F32)
-    state_ref[0] = jnp.zeros((HEAD_SIZE, HEAD_SIZE), BF16)
     for turn in range(1, count):
         high = state.astype(BF16)
         state_ref[turn] = high
         if turn + 1 < count:
-            slot = turn ^ place
+            item = map_ref[turn ^ place]
             low = (state - high.astype(F32)).astype(BF16)
-            moved = mm(map_ref[slot, :, :HEAD_SIZE], jnp.concatenate([high, low], axis=1))
+            moved = mm(item[:, :HEAD_SIZE], jnp.concatenate([high, low], axis=1))
             state = (
-                moved[:, :HEAD_SIZE]
-                + moved[:, HEAD_SIZE:]
-                + map_ref[slot, :, HEAD_SIZE:].astype(F32)
+                moved[:, :HEAD_SIZE] + moved[:, HEAD_SIZE:] + item[:, HEAD_SIZE:].astype(F32)
             )
+    for r in range(count):
+        slots[r][...] = state_ref[place ^ r]
+
+
+def pass_kernel(place_ref, early_ref, *refs):
+    count = len(refs) - 3
+    keep_ref, send_ref, state_ref = refs[count:]
+    second = place_ref[0] == 1
+    for r in range(count):
+        state_ref[place_ref[1] ^ r] = refs[r][...]
+    for j in range(count):
+        state = state_ref[j]
+        after = follow(early_ref[j], state).astype(BF16)
+        keep_ref[j] = jnp.where(second, after, state)
+        send_ref[j] = jnp.where(second, state, after)
 
 
 def output_kernel(
-    place_ref, through_hbm, settled_hbm, gate_hbm, state_ref, gain_ref, weight_hbm,
-    other_ref, mine_ref, through_ref, settled_ref, gate_ref, weight_ref, gated_ref, sems,
+    split, place_ref, through_hbm, settled_hbm, gate_hbm, *refs
 ):
+    parts, refs = refs[:split], refs[split:]
+    gain_ref, weight_hbm, other_ref, mine_ref, through_ref = refs[:5]
+    settled_ref, gate_ref, weight_ref, gated_ref, state_ref, sems = refs[5:]
     core = place_ref[0]
+    each = parts[0].shape[0]
+    for n, part in enumerate(parts):
+        state_ref[pl.ds((place_ref[1] ^ n) * each, each)] = part[...]
     chips, block = other_ref.shape[:2]
     _, width = through_ref.shape
     heads = state_ref.shape[0]
@@ -238,55 +272,51 @@
                 ].astype(BF16)
 
 
-def make_maps(operands, place, tops, previous):
-    queries = operands[0]
-    rows, width = queries.shape
+def in_hbm(*arrays):
+    return [pltpu.with_memory_space_constraint(a, pltpu.HBM) for a in arrays]
+
+
+def make_maps(operands, first, pairs, previous):
+    rows, width = operands[0].shape
     heads = operands[4].shape[0]
     chunks = rows // CHUNK
     lanes = PAIR * HEAD_SIZE
-    top = max(tops)
-
-    def pair(step, place_ref):
-        return (place_ref[0] // PAIR) ^ (top - step)
-
-    column = pl.BlockSpec((rows, lanes), lambda s, p: (0, pair(s, p)))
-    slots = PAIR * len(tops)
-    shapes = [jax.ShapeDtypeStruct((HEAD_SIZE, 2 * HEAD_SIZE), BF16)] * slots + [
-        jax.ShapeDtypeStruct((rows, 2 * width), BF16),
-        jax.ShapeDtypeStruct((rows, width), BF16),
-        jax.ShapeDtypeStruct((rows, width), BF16),
-        jax.ShapeDtypeStruct((chunks, width), F32),
-        jax.ShapeDtypeStruct((heads, chunks - 1, HEAD_SIZE, 2 * HEAD_SIZE), BF16),
-    ]
-    share = len(tops) * PAIR * chunks
+    column = pl.BlockSpec((rows, lanes), lambda s, p: (0, p[0] + s))
+    share = pairs * PAIR * chunks
     return pl.pallas_call(
-        functools.partial(maps_kernel, top, slots),
+        maps_kernel,
         grid_spec=pltpu.PrefetchScalarGridSpec(
             num_scalar_prefetch=1,
-            grid=(len(tops),),
+            grid=(pairs,),
             in_specs=[column] * 4
             + [pl.BlockSpec((heads, rows), lambda s, p: (0, 0))]
             + [pl.BlockSpec(memory_space=pl.ANY)] * len(previous),
-            out_specs=[pl.BlockSpec((HEAD_SIZE, 2 * HEAD_SIZE), lambda s, p: (0, 0))] * slots
-            + [
-                pl.BlockSpec((rows, 2 * lanes), lambda s, p: (0, pair(s, p))),
+            out_specs=[
+                pl.BlockSpec((PAIR, HEAD_SIZE, 2 * HEAD_SIZE), lambda s, p: (s, 0, 0)),
+                pl.BlockSpec((rows, 2 * lanes), lambda s, p: (0, p[0] + s)),
                 column,
                 column,
-                pl.BlockSpec((chunks, lanes), lambda s, p: (0, pair(s, p))),
+                pl.BlockSpec((chunks, lanes), lambda s, p: (0, p[0] + s)),
                 pl.BlockSpec(
                     (PAIR, chunks - 1, HEAD_SIZE, 2 * HEAD_SIZE),
-                    lambda s, p: (pair(s, p), 0, 0, 0),
+                    lambda s, p: (p[0] + s, 0, 0, 0),
                 ),
             ],
         ),
-        out_shape=shapes,
-        input_output_aliases={6 + n: slots + n for n in range(len(previous))},
+        out_shape=[
+            jax.ShapeDtypeStruct((PAIR * pairs, HEAD_SIZE, 2 * HEAD_SIZE), BF16),
+            pltpu.HBM((rows, 2 * width), BF16),
+            pltpu.HBM((rows, width), BF16),
+            pltpu.HBM((rows, width), BF16),
+            pltpu.HBM((chunks, width), F32),
+            pltpu.HBM((heads, chunks - 1, HEAD_SIZE, 2 * HEAD_SIZE), BF16),
+        ],
+        input_output_aliases={6 + n: 1 + n for n in range(len(previous))},
         cost_estimate=pl.CostEstimate(
             flops=share * 120_000_000, bytes_accessed=share * 400_000, transcendentals=0
         ),
         compiler_params=pltpu.CompilerParams(vmem_limit_bytes=LIMIT << 20),
-        name="maps",
-    )(place, *operands, *previous)
+    )(first, *operands, *previous)
 
 
 def finish_reading(held):
@@ -310,8 +340,8 @@
         ],
         out_specs=[column, column],
         out_shape=[
-            jax.ShapeDtypeStruct((rows, width), BF16),
-            jax.ShapeDtypeStruct((rows, width), F32),
+            pltpu.HBM((rows, width), BF16),
+            pltpu.HBM((rows, width), F32),
         ],
         cost_estimate=pl.CostEstimate(
             flops=heads * chunks * 100_000_000,
@@ -320,12 +350,12 @@
         ),
         compiler_params=pltpu.CompilerParams(vmem_limit_bytes=LIMIT << 20),
         name="read",
-    )(now, back, solved, mids, starts)
-
-
-def project(core, through, settled, gates, states, gain, weight, groups):
+    )(*in_hbm(now, back, solved, mids, starts))
+
+
+def project(places, through, settled, gates, states, gain, weight, groups):
     rows, width = through.shape
-    heads = states.shape[0]
+    heads = sum(part.shape[0] for part in states)
     model = weight.shape[1]
     chips = groups // 2
     block = rows // groups
@@ -333,7 +363,7 @@
     hbm = pl.BlockSpec(memory_space=pltpu.HBM)
     share = pl.BlockSpec((chips, block, model), lambda n, p: (0, 0, 0))
     return pl.pallas_call(
-        output_kernel,
+        functools.partial(output_kernel, len(states)),
         grid_spec=pltpu.PrefetchScalarGridSpec(
             num_scalar_prefetch=1,
             grid=(1,),
@@ -341,7 +371,9 @@
                 hbm,
                 hbm,
                 hbm,
-                pl.BlockSpec((heads, HEAD_SIZE, HEAD_SIZE), lambda n, p: (0, 0, 0)),
+            ]
+            + [pl.BlockSpec(part.shape, lambda n, p: (0, 0, 0)) for part in states]
+            + [
                 pl.BlockSpec((1, HEAD_SIZE), lambda n, p: (0, 0)),
                 hbm,
             ],
@@ -352,6 +384,7 @@
                 pltpu.VMEM((rows, width), BF16),
                 pltpu.VMEM((tiles, width, model // tiles), BF16),
                 pltpu.VMEM((rows, width), BF16),
+                pltpu.VMEM((heads, HEAD_SIZE, HEAD_SIZE), BF16),
                 pltpu.SemaphoreType.DMA((12 * chips + tiles,)),
             ],
         ),
@@ -364,55 +397,68 @@
         compiler_params=pltpu.CompilerParams(vmem_limit_bytes=LIMIT << 20),
         name="output",
     )(
-        jnp.reshape(core, (1,)).astype(jnp.int32),
-        through,
-        settled,
-        gates,
-        states,
+        places,
+        *in_hbm(through, settled, gates),
+        *states,
         gain.reshape(1, HEAD_SIZE),
-        weight,
-    )
-
-
-def carry_apart(operands, place, axis):
-    count = lax.axis_size(axis)
-    place_at = jnp.reshape(place, (1,)).astype(jnp.int32)
-
-    def swap(block, turn):
-        return lax.ppermute(block, axis, [(d, d ^ turn) for d in range(count)])
-
-    pairs = count // PAIR
-    half = pairs // 2
-    received = [None] * count
-    far = make_maps(operands, place_at, range(half, pairs), [])
-    for r in range(PAIR * half, count):
-        received[r] = swap(far[r - PAIR * half], r)
-    near = make_maps(operands, place_at, range(half), far[-5:])
-    received[0] = near[0]
-    for r in range(1, PAIR * half):
-        received[r] = swap(near[r], r)
-    reads = finish_reading(near[-5:])
-    block = pl.BlockSpec((HEAD_SIZE, 2 * HEAD_SIZE), lambda n, p: (0, 0))
-    states = pl.pallas_call(
-        chain_kernel,
+        *in_hbm(weight),
+    )
+
+
+def small_call(kernel, place, operands, shapes, scratch):
+    def block(shape):
+        return pl.BlockSpec(shape, lambda n, p: (0,) * len(shape))
+
+    return pl.pallas_call(
+        kernel,
         grid_spec=pltpu.PrefetchScalarGridSpec(
             num_scalar_prefetch=1,
             grid=(1,),
-            in_specs=[block] * count,
-            out_specs=pl.BlockSpec((count, HEAD_SIZE, HEAD_SIZE), lambda n, p: (0, 0, 0)),
-            scratch_shapes=[pltpu.VMEM((count, HEAD_SIZE, 2 * HEAD_SIZE), BF16)],
+            in_specs=[block(a.shape) for a in operands],
+            out_specs=[block(shape) for shape in shapes],
+            scratch_shapes=[pltpu.VMEM(shape, BF16) for shape in scratch],
         ),
-        out_shape=jax.ShapeDtypeStruct((count, HEAD_SIZE, HEAD_SIZE), BF16),
+        out_shape=[jax.ShapeDtypeStruct(shape, BF16) for shape in shapes],
         compiler_params=pltpu.CompilerParams(vmem_limit_bytes=8 << 20),
-        name="chain",
-    )(place_at, *received)
-    return reads, lax.all_to_all(states, axis, 0, 0)
+    )(place, *operands)
+
+
+def carry_apart(operands, place, axis):
+    count = lax.axis_size(axis)
+    half = count // 2
+    side, turn = lax.rem(place, 2), lax.div(place, 2)
+    place_at = jnp.stack([side, turn]).astype(jnp.int32)
+    pairs = half // PAIR
+
+    def swap(block, step):
+        return lax.ppermute(block, axis, [(d, d ^ step) for d in range(count)])
+
+    def first(group):
+        return jnp.reshape(group * pairs, (1,)).astype(jnp.int32)
+
+    item, square = (HEAD_SIZE, 2 * HEAD_SIZE), (HEAD_SIZE, HEAD_SIZE)
+    far = make_maps(operands, first(1 - side), pairs, [])
+    came = swap(far[0], 1)
+    near = make_maps(operands, first(side), pairs, far[1:])
+    early, *slots = small_call(
+        join_kernel, place_at, [near[0], came], [(half, *item)] + [item] * half, [(half, *item)]
+    )
+    slots = [slots[0]] + [swap(slots[r], 2 * r) for r in range(1, half)]
+    reads = finish_reading(near[1:])
+    states = small_call(
+        chain_kernel, place_at, slots, [square] * half, [(half, *item), (half, *square)]
+    )
+    states = [states[0]] + [swap(states[r], 2 * r) for r in range(1, half)]
+    keep, send = small_call(
+        pass_kernel, place_at, [early, *states], [(half, *square)] * 2, [(half, *square)]
+    )
+    return reads, [keep, swap(send, 1)], side
 
 
 def carry_whole(operands, axis):
     heads = operands[4].shape[0]
-    made = make_maps(operands, jnp.zeros((1,), jnp.int32), range(heads // PAIR), [])
-    gathered = lax.all_gather(jnp.stack(made[:heads]), axis)
+    made = make_maps(operands, jnp.zeros((1,), jnp.int32), heads // PAIR, [])
+    gathered = lax.all_gather(made[0], axis)
 
     def one(turn, state):
         item = lax.dynamic_index_in_dim(gathered, turn, 0, False).astype(F32)
@@ -423,7 +469,7 @@
 
     zero = jnp.zeros((heads, HEAD_SIZE, HEAD_SIZE), F32)
     state = lax.fori_loop(0, lax.axis_index(axis), one, zero)
-    return finish_reading(made[heads:]), state.astype(BF16)
+    return finish_reading(made[1:]), [state.astype(BF16)], 0
 
 
 def on_device(
@@ -437,18 +483,19 @@
     out_weight,
 ):
     heads = query_vectors.shape[1] // HEAD_SIZE
-    operands = [query_vectors, key_vectors, value_vectors, log_decay, write_rate.T]
+    operands = in_hbm(query_vectors, key_vectors, value_vectors, log_decay, write_rate.T)
     count = lax.axis_size("ctx")
-    if heads == count and count & (count - 1) == 0 and count >= 4:
-        reads, states = carry_apart(operands, lax.axis_index("ctx"), "ctx")
+    if heads == count and count & (count - 1) == 0 and count >= 8:
+        reads, states, twist = carry_apart(operands, lax.axis_index("ctx"), "ctx")
     else:
-        reads, states = carry_whole(operands, "ctx")
+        reads, states, twist = carry_whole(operands, "ctx")
     groups = lax.axis_size("head")
     place = lax.axis_index("head")
     core, chip = lax.rem(place, 2), lax.div(place, 2)
     chips = groups // 2
 
-    other, mine = project(core, *reads, out_gate, states, norm_gain, out_weight, groups)
+    places = jnp.stack([core, jnp.asarray(twist, core.dtype)]).astype(jnp.int32)
+    other, mine = project(places, *reads, out_gate, states, norm_gain, out_weight, groups)
     came = lax.ppermute(other, "head", [(d, d ^ 1) for d in range(groups)])
 
     def both(block):

time: 76.3 us -> 68.2 us (0.89)
  starting transfers between devices: 18.2 us -> 14.2 us
  Pallas kernels: 31.8 us -> 30.1 us
  local copies, waits for them, and re-layouts: 1.56 us -> 0.01 us
  other arithmetic: 2.04 us -> 1.19 us
    all_to_all x1 -> x0, starting transfers between devices: 4.03 us -> none  [carry_apart(): return (reads, lax.all_to_all(states, axis, 0, 0))]
    ppermute x7 -> x8, waiting for transfers between devices: 7.02 us -> 9.24 us  [swap(): return lax.ppermute(block, axis, [(d, d ^ step) for d in range(count)])]
    all_to_all x1 -> x0, waiting for transfers between devices: 1.78 us -> none  [carry_apart(): return (reads, lax.all_to_all(states, axis, 0, 0))]
    pallas_call x4 -> x6, Pallas kernels: 24.9 us -> 23.2 us  [the longest x2 14.7 us: make_maps(): pl.pallas_call(maps_kernel, grid_spec=pltpu.PrefetchScalarGridSpec(num_sc...]
    unnamed x14 -> x2, local copies, waits for them, and re-layouts: 1.56 us -> 0.01 us
    convert_element_type x1, other arithmetic: 1.12 us -> 0.11 us  [on_device(): away = both(lax.rem(chip + turn, chips)).astype(BF16)]
    ppermute x7 -> x8, starting transfers between devices: 12.5 us -> 12.6 us  [swap(): return lax.ppermute(block, axis, [(d, d ^ step) for d in range(count)])]
  transfers between devices with their start and end apart: 10 -> 10, of which waited for: 5 -> 6; matrix products, arithmetic and copies ran while one was open for 0% -> 0% of each run, Pallas kernels for 9% -> 21%
where the time goes in v3:
time: 68.2 us; the launch traced here: 68 us
  Pallas kernels  30.1 us (44%)
  waiting for transfers between devices  22.3 us (33%)
  starting transfers between devices  14.2 us (21%)
  other arithmetic  1.19 us (2%)
    pallas_call x2, Pallas kernels, make_maps(): pl.pallas_call(maps_kernel, grid_spec=pltpu.PrefetchScalarGridSpec(num_sc...  14.7 us
    ppermute x8, starting transfers between devices, swap(): return lax.ppermute(block, axis, [(d, d ^ step) for d in range(count)])  12.6 us
    ppermute x1, waiting for transfers between devices, on_device(): total = total + lax.ppermute(away, 'head', hops).astype(F32)  10.7 us
    ppermute x8, waiting for transfers between devices, swap(): return lax.ppermute(block, axis, [(d, d ^ step) for d in range(count)])  9.24 us
    pallas_call x1, Pallas kernels, finish_reading(): pl.pallas_call(read_kernel, grid=(heads // PAIR,), in_specs=[column, colu...  6.92 us
    pallas_call x1, Pallas kernels, project(): pl.pallas_call(functools.partial(output_kernel, len(states)), grid_spec=p...  5.99 us
    pallas_call x3, Pallas kernels, small_call(): pl.pallas_call(kernel, grid_spec=pltpu.PrefetchScalarGridSpec(num_scalar_...  2.43 us
    ppermute x1, waiting for transfers between devices, on_device(): came = lax.ppermute(other, 'head', [(d, d ^ 1) for d in range(groups)])  2.4 us
  transfers between devices with their start and end apart: 10, of which 6 were waited for; matrix products, arithmetic and copies ran while one was open for 0% of the time, Pallas kernels for 21%

profile of v3, /device:TPU:0, one launch (start us, length us, event | category | flops | bytes accessed | tf_op | source)
XLA Modules:
  0.0 68.0 jit_solution(14074504959665761439)
XLA Ops:
  0.0 7.4 %shard_map.82 = (bf16[4,128,256]{2,1,0:T(8,128)(2,1)S(1)}, bf16[384,2048]{1,0:T(8,128)(2,1)}, bf16[384,1024]{1,0:T(8,128)(2,1)}, bf16[384,1024]{1,0:T(8,128)(2,1...) custom-call(s32[1]{0:T(128)} %bitcast.4.first_ref, bf16[384,1024]{1,0:T(8,128)(2,1)} %query_ref.3, ...), custom_call_target="tpu_custom_call" | custom-call | flops 1440000000 | bytes 4800000 | tf_op jit(solution)/shard_map/pallas_call | solution.py:286
  7.4 3.0 %collective-permute-start = (bf16[4,128,256]{2,1,0:T(8,128)(2,1)S(1)}, bf16[4,128,256]{2,1,0:T(8,128)(2,1)S(1)}, u32[]{:S(2)}, u32[]{:S(2)}) collective-permute-start(bf16[4,128,256]{2,1,0:T(8,128)(2,1)S(1)} %get-tuple-element.45), channel_id=1, source_target_pairs={{0,4},{4,0},{8,12},{12,8},{16,20},{20,16},{24,28},{28,24},{1,5},{5... | collective-permute-start | bytes 786440 | tf_op jit(solution)/shard_map/ppermute | solution.py:434
  10.4 0.1 pad_add_fusion.1.place_ref
  10.5 7.4 %shard_map.83 = (bf16[4,128,256]{2,1,0:T(8,128)(2,1)S(1)}, bf16[384,2048]{1,0:T(8,128)(2,1)}, bf16[384,1024]{1,0:T(8,128)(2,1)}, bf16[384,1024]{1,0:T(8,128)(2,1...) custom-call(s32[1]{0:T(128)} %bitcast.2.first_ref, ...), custom_call_target="tpu_custom_call", output_to_operand_aliasing={{1}: (6, {}), {2}: (7, {}), {3}: (8, {}), {4}: (9, {}), {5}... | custom-call | flops 1440000000 | bytes 4800000 | tf_op jit(solution)/shard_map/pallas_call | solution.py:286
  17.9 0.0 collective-permute-done.came_ref
  17.9 0.8 %shard_map.84 = (bf16[4,128,256]{2,1,0:T(8,128)(2,1)S(1)}, bf16[128,256]{1,0:T(8,128)(2,1)S(1)}, bf16[128,256]{1,0:T(8,128)(2,1)S(1)}, bf16[128,256]{1,0:T(8,128)(2,1)S(1)}, bf16[128,256]{1,0:T(8,128)(2,1)S(1)}) custom-call(s32[2]{0:T(128)S(1)} %pad_add_fusion.1.place_ref, bf16[4,128,256]{2,1,0:T(8,128)(2,1)S(1)} %get-tuple-element.44.own_ref, ...), custom_call_target="tpu_custom_call" | custom-call | tf_op jit(solution)/shard_map/pallas_call | solution.py:412
  18.7 1.6 %collective-permute-start.1 = (bf16[128,256]{1,0:T(8,128)(2,1)S(1)}, bf16[128,256]{1,0:T(8,128)(2,1)S(1)}, u32[]{:S(2)}, u32[]{:S(2)}) collective-permute-start(bf16[128,256]{1,0:T(8,128)(2,1)S(1)} %get-tuple-element.48), channel_id=1, source_target_pairs={{0,8},{4,12},{8,0},{12,4},{16,24},{20,28},{24,16},{28,20},{1,9},{5... | collective-permute-start | bytes 196616 | tf_op jit(solution)/shard_map/ppermute | solution.py:434
  20.3 2.6 %collective-permute-start.2 = (bf16[128,256]{1,0:T(8,128)(2,1)S(1)}, bf16[128,256]{1,0:T(8,128)(2,1)S(1)}, u32[]{:S(2)}, u32[]{:S(2)}) collective-permute-start(bf16[128,256]{1,0:T(8,128)(2,1)S(1)} %get-tuple-element.49), channel_id=1, source_target_pairs={{0,16},{4,20},{8,24},{12,28},{16,0},{20,4},{24,8},{28,12},{1,17},{... | collective-permute-start | bytes 196616 | tf_op jit(solution)/shard_map/ppermute | solution.py:434
  22.9 0.2 collective-permute-start.3
  23.1 0.0 collective-permute-done.1.refs_1_
  23.1 4.2 %collective-permute-done.2.refs_2_ = bf16[128,256]{1,0:T(8,128)(2,1)S(1)} collective-permute-done((bf16[128,256]{1,0:T(8,128)(2,1)S(1)}, bf16[128,256]{1,0:T(8,128)(2,1)S(1)}, u32[]{:S(2)}, u32[]{:S(2)}) %collective-permute-start.2) | collective-permute-done | bytes 65568 | tf_op jit(solution)/shard_map/ppermute | solution.py:434
  27.3 1.7 %collective-permute-done.3.refs_3_ = bf16[128,256]{1,0:T(8,128)(2,1)S(1)} collective-permute-done((bf16[128,256]{1,0:T(8,128)(2,1)S(1)}, bf16[128,256]{1,0:T(8,128)(2,1)S(1)}, u32[]{:S(2)}, u32[]{:S(2)}) %collective-permute-start.3) | collective-permute-done | bytes 65568 | tf_op jit(solution)/shard_map/ppermute | solution.py:434
  29.0 0.9 %shard_map.85 = (bf16[128,128]{1,0:T(8,128)(2,1)S(1)}, bf16[128,128]{1,0:T(8,128)(2,1)S(1)}, bf16[128,128]{1,0:T(8,128)(2,1)S(1)}, bf16[128,128]{1,0:T(8,128)(2,1)S(1)}) custom-call(s32[2]{0:T(128)S(1)} %pad_add_fusion.1.place_ref, bf16[128,256]{1,0:T(8,128)(2,1)S(1)} %get-tuple-element.47.refs_0_, bf16[128,256]{1,0:T(8,128)(2,1)S(1)} %collective-permute-done.1.refs_1_, ...), custom_call_target="tpu_custom_call" | custom-call | tf_op jit(solution)/shard_map/pallas_call | solution.py:412
  29.9 0.1 collective-permute-start.4
  30.0 2.1 %collective-permute-start.5 = (bf16[128,128]{1,0:T(8,128)(2,1)S(1)}, bf16[128,128]{1,0:T(8,128)(2,1)S(1)}, u32[]{:S(2)}, u32[]{:S(2)}) collective-permute-start(bf16[128,128]{1,0:T(8,128)(2,1)S(1)} %get-tuple-element.53), channel_id=1, source_target_pairs={{0,16},{4,20},{8,24},{12,28},{16,0},{20,4},{24,8},{28,12},{1,17},{... | collective-permute-start | bytes 98312 | tf_op jit(solution)/shard_map/ppermute | solution.py:434
  32.0 2.3 %collective-permute-start.6 = (bf16[128,128]{1,0:T(8,128)(2,1)S(1)}, bf16[128,128]{1,0:T(8,128)(2,1)S(1)}, u32[]{:S(2)}, u32[]{:S(2)}) collective-permute-start(bf16[128,128]{1,0:T(8,128)(2,1)S(1)} %get-tuple-element.54), channel_id=1, source_target_pairs={{0,24},{4,28},{8,16},{12,20},{16,8},{20,12},{24,0},{28,4},{1,25},{... | collective-permute-start | bytes 98312 | tf_op jit(solution)/shard_map/ppermute | solution.py:434
  34.3 0.0 collective-permute-done.4.refs_1_
  34.3 0.6 collective-permute-done.5.refs_2_
  35.0 2.8 %collective-permute-done.6.refs_3_ = bf16[128,128]{1,0:T(8,128)(2,1)S(1)} collective-permute-done((bf16[128,128]{1,0:T(8,128)(2,1)S(1)}, bf16[128,128]{1,0:T(8,128)(2,1)S(1)}, u32[]{:S(2)}, u32[]{:S(2)}) %collective-permute-start.6) | collective-permute-done | bytes 32800 | tf_op jit(solution)/shard_map/ppermute | solution.py:434
  37.7 0.7 %shard_map.86 = (bf16[4,128,128]{2,1,0:T(8,128)(2,1)S(1)}, bf16[4,128,128]{2,1,0:T(8,128)(2,1)S(1)}) custom-call(s32[2]{0:T(128)S(1)} %pad_add_fusion.1.place_ref, bf16[4,128,256]{2,1,0:T(8,128)(2,1)S(1)} %get-tuple-element.46.early_ref, bf16[128,128]{1,0:T(8,128)(2,1)S(1)} %get-tuple-element.51.refs_0_, ...), custom_call_target="tpu_custom_call" | custom-call | tf_op jit(solution)/shard_map/pallas_call | solution.py:412
  38.5 0.6 collective-permute-start.7
  39.1 0.0 copy-start
  39.1 6.9 %read.1 = (bf16[384,1024]{1,0:T(8,128)(2,1)}, f32[384,1024]{1,0:T(8,128)}) custom-call(bf16[384,1024]{1,0:T(8,128)(2,1)} %get-tuple-element.37.now_ref, bf16[384,1024]{1,0:T(8,128)(2,1)} %get-tuple-element.38.back_ref, bf16[384,2048]{1,0:T(8,128)(2,1)} %get-tuple-element.39.solved_ref, f32[3,1024]{1,0:T(4,128)} %get-tuple-element.40.mid_ref, ...), custom_call_target="tpu_custom_call" | custom-call | flops 2400000000 | bytes 9600000 | tf_op jit(solution)/shard_map/read/pallas_call | solution.py:329
  46.1 0.1 pad_add_fusion.place_ref
  46.1 0.0 collective-permute-done.7.refs_1_
  46.1 0.0 copy-done
  46.1 6.0 %output.1 = (bf16[2,96,2304]{2,1,0:T(8,128)(2,1)S(1)}, bf16[2,96,2304]{2,1,0:T(8,128)(2,1)S(1)}) custom-call(s32[2]{0:T(128)S(1)} %pad_add_fusion.place_ref, bf16[384,1024]{1,0:T(8,128)(2,1)} %get-tuple-element.42.through_hbm, f32[384,1024]{1,0:T(8,128)} %get-tuple-element.43.settled_hbm, bf16[384,1024]{1,0:T(8,128)(2,1)} %gate_hbm.1, ...), custom_call_target="tpu_custom_call" | custom-call | flops 1811939328 | bytes 4718592 | tf_op jit(solution)/shard_map/output/pallas_call | solution.py:365
  52.1 0.1 collective-permute-start.8
  52.2 2.4 %collective-permute-done.8 = bf16[2,96,2304]{2,1,0:T(8,128)(2,1)S(1)} collective-permute-done((bf16[2,96,2304]{2,1,0:T(8,128)(2,1)S(1)}, bf16[2,96,2304]{2,1,0:T(8,128)(2,1)S(1)}, u32[]{:S(2)}, u32[]{:S(2)}) %collective-permute-start.8) | collective-permute-done | bytes 884768 | tf_op jit(solution)/shard_map/ppermute | solution.py:499
  54.6 0.1 fusion.1
  54.7 1.6 %collective-permute-start.9 = (bf16[96,2304]{1,0:T(8,128)(2,1)S(1)}, bf16[96,2304]{1,0:T(8,128)(2,1)S(1)}, u32[]{:S(2)}, u32[]{:S(2)}) collective-permute-start(bf16[96,2304]{1,0:T(8,128)(2,1)S(1)} %fusion.1), channel_id=1, source_target_pairs={{0,2},{1,3},{2,0},{3,1},{4,6},{5,7},{6,4},{7,5},{8,10},{9,11},{10,... | collective-permute-start | bytes 1327112 | tf_op jit(solution)/shard_map/ppermute | solution.py:510
  56.3 10.7 %collective-permute-done.9 = bf16[96,2304]{1,0:T(8,128)(2,1)S(1)} collective-permute-done((bf16[96,2304]{1,0:T(8,128)(2,1)S(1)}, bf16[96,2304]{1,0:T(8,128)(2,1)S(1)}, u32[]{:S(2)}, u32[]{:S(2)}) %collective-permute-start.9) | collective-permute-done | bytes 442400 | tf_op jit(solution)/shard_map/ppermute | solution.py:510
  67.0 0.9 %fusion = bf16[96,2304]{1,0:T(8,128)(2,1)} fusion(bf16[96,2304]{1,0:T(8,128)(2,1)S(1)} %collective-permute-done.9, bf16[2,96,2304]{2,1,0:T(8,128)(2,1)S(1)} %collective-permute-done.8, s32[]{:T(128)S(6)} %select_n.9, bf16[2,96,2304]{2,1,0:T(8,128)(2,1)S(1)} %get-tuple-element.57), kind=kLoop, calls=%fused_computation.1 | loop fusion | flops 1327104 | bytes 1769476 | tf_op jit(solution)/shard_map/convert_element_type | solution.py:511
Async XLA Ops:
  7.4 10.5 %collective-permute-start = (bf16[4,128,256]{2,1,0:T(8,128)(2,1)S(1)}, bf16[4,128,256]{2,1,0:T(8,128)(2,1)S(1)}, u32[]{:S(2)}, u32[]{:S(2)}) collective-permute-start(bf16[4,128,256]{2,1,0:T(8,128)(2,1)S(1)} %get-tuple-element.45), channel_id=1, source_target_pairs={{0,4},{4,0},{8,12},{12,8},{16,20},{20,16},{24,28},{28,24},{1,5},{5... | collective-permute-start | bytes 786440 | tf_op jit(solution)/shard_map/ppermute | solution.py:434
  18.7 4.5 %collective-permute-start.1 = (bf16[128,256]{1,0:T(8,128)(2,1)S(1)}, bf16[128,256]{1,0:T(8,128)(2,1)S(1)}, u32[]{:S(2)}, u32[]{:S(2)}) collective-permute-start(bf16[128,256]{1,0:T(8,128)(2,1)S(1)} %get-tuple-element.48), channel_id=1, source_target_pairs={{0,8},{4,12},{8,0},{12,4},{16,24},{20,28},{24,16},{28,20},{1,9},{5... | collective-permute-start | bytes 196616 | tf_op jit(solution)/shard_map/ppermute | solution.py:434
  20.3 7.0 %collective-permute-start.2 = (bf16[128,256]{1,0:T(8,128)(2,1)S(1)}, bf16[128,256]{1,0:T(8,128)(2,1)S(1)}, u32[]{:S(2)}, u32[]{:S(2)}) collective-permute-start(bf16[128,256]{1,0:T(8,128)(2,1)S(1)} %get-tuple-element.49), channel_id=1, source_target_pairs={{0,16},{4,20},{8,24},{12,28},{16,0},{20,4},{24,8},{28,12},{1,17},{... | collective-permute-start | bytes 196616 | tf_op jit(solution)/shard_map/ppermute | solution.py:434
  22.9 6.1 %collective-permute-start.3 = (bf16[128,256]{1,0:T(8,128)(2,1)S(1)}, bf16[128,256]{1,0:T(8,128)(2,1)S(1)}, u32[]{:S(2)}, u32[]{:S(2)}) collective-permute-start(bf16[128,256]{1,0:T(8,128)(2,1)S(1)} %get-tuple-element.50), channel_id=1, source_target_pairs={{0,24},{4,28},{8,16},{12,20},{16,8},{20,12},{24,0},{28,4},{1,25},{... | collective-permute-start | bytes 196616 | tf_op jit(solution)/shard_map/ppermute | solution.py:434
  29.9 4.5 %collective-permute-start.4 = (bf16[128,128]{1,0:T(8,128)(2,1)S(1)}, bf16[128,128]{1,0:T(8,128)(2,1)S(1)}, u32[]{:S(2)}, u32[]{:S(2)}) collective-permute-start(bf16[128,128]{1,0:T(8,128)(2,1)S(1)} %get-tuple-element.52), channel_id=1, source_target_pairs={{0,8},{4,12},{8,0},{12,4},{16,24},{20,28},{24,16},{28,20},{1,9},{5... | collective-permute-start | bytes 98312 | tf_op jit(solution)/shard_map/ppermute | solution.py:434
  30.0 5.0 %collective-permute-start.5 = (bf16[128,128]{1,0:T(8,128)(2,1)S(1)}, bf16[128,128]{1,0:T(8,128)(2,1)S(1)}, u32[]{:S(2)}, u32[]{:S(2)}) collective-permute-start(bf16[128,128]{1,0:T(8,128)(2,1)S(1)} %get-tuple-element.53), channel_id=1, source_target_pairs={{0,16},{4,20},{8,24},{12,28},{16,0},{20,4},{24,8},{28,12},{1,17},{... | collective-permute-start | bytes 98312 | tf_op jit(solution)/shard_map/ppermute | solution.py:434
  32.0 5.7 %collective-permute-start.6 = (bf16[128,128]{1,0:T(8,128)(2,1)S(1)}, bf16[128,128]{1,0:T(8,128)(2,1)S(1)}, u32[]{:S(2)}, u32[]{:S(2)}) collective-permute-start(bf16[128,128]{1,0:T(8,128)(2,1)S(1)} %get-tuple-element.54), channel_id=1, source_target_pairs={{0,24},{4,28},{8,16},{12,20},{16,8},{20,12},{24,0},{28,4},{1,25},{... | collective-permute-start | bytes 98312 | tf_op jit(solution)/shard_map/ppermute | solution.py:434
  38.5 7.6 %collective-permute-start.7 = (bf16[4,128,128]{2,1,0:T(8,128)(2,1)S(1)}, bf16[4,128,128]{2,1,0:T(8,128)(2,1)S(1)}, u32[]{:S(2)}, u32[]{:S(2)}) collective-permute-start(bf16[4,128,128]{2,1,0:T(8,128)(2,1)S(1)} %get-tuple-element.56), channel_id=1, source_target_pairs={{0,4},{4,0},{8,12},{12,8},{16,20},{20,16},{24,28},{28,24},{1,5},{5... | collective-permute-start | bytes 393224 | tf_op jit(solution)/shard_map/ppermute | solution.py:434
  39.1 7.0 %copy-start = (f32[128]{0:T(128)S(1)}, f32[128]{0:T(128)}, u32[]{:S(2)}) copy-start(f32[128]{0:T(128)} %param.14) | copy-start | bytes 1540
  52.1 2.5 %collective-permute-start.8 = (bf16[2,96,2304]{2,1,0:T(8,128)(2,1)S(1)}, bf16[2,96,2304]{2,1,0:T(8,128)(2,1)S(1)}, u32[]{:S(2)}, u32[]{:S(2)}) collective-permute-start(bf16[2,96,2304]{2,1,0:T(8,128)(2,1)S(1)} %get-tuple-element.58), channel_id=1, source_target_pairs={{0,1},{1,0},{2,3},{3,2},{4,5},{5,4},{6,7},{7,6},{8,9},{9,8},{10,11... | collective-permute-start | bytes 2654216 | tf_op jit(solution)/shard_map/ppermute | solution.py:499
  54.7 12.3 %collective-permute-start.9 = (bf16[96,2304]{1,0:T(8,128)(2,1)S(1)}, bf16[96,2304]{1,0:T(8,128)(2,1)S(1)}, u32[]{:S(2)}, u32[]{:S(2)}) collective-permute-start(bf16[96,2304]{1,0:T(8,128)(2,1)S(1)} %fusion.1), channel_id=1, source_target_pairs={{0,2},{1,3},{2,0},{3,1},{4,6},{5,7},{6,4},{7,5},{8,10},{9,11},{10,... | collective-permute-start | bytes 1327112 | tf_op jit(solution)/shard_map/ppermute | solution.py:510

commit v4 on v3

--- a/solution.py
+++ b/solution.py
@@ -11,7 +11,9 @@
 HEAD_SIZE = 128
 CHUNK = 128
 PAIR = 2
+BATCH = 4
 LIMIT = 24
+PIECES = (2, 1)
 F32 = jnp.float32
 BF16 = jnp.bfloat16
 NT = (((1,), (1,)), ((), ()))
@@ -36,17 +38,17 @@
 ):
     map_ref, solved_ref, back_ref, now_ref, mid_ref, start_ref = refs[-6:]
     chunk_count = key_ref.shape[0] // CHUNK
-    first_head = (first_ref[0] + pl.program_id(0)) * PAIR
+    first_head = (first_ref[0] + pl.program_id(0)) * BATCH
     later, earlier = positions()
     lower = (later >= earlier).astype(BF16)
     strict = later > earlier
     eye = (later == earlier).astype(F32)
     rates = rate_ref[...].T
     rate_lane = lax.broadcasted_iota(jnp.int32, rates.shape, 1)
-    units = [(i, j) for i in range(PAIR) for j in range(chunk_count)]
+    units = [(i, j) for i in range(BATCH) for j in range(chunk_count)]
     rate_cols = [
         jnp.sum(jnp.where(rate_lane == first_head + i, rates, 0.0), axis=1, keepdims=True)
-        for i in range(PAIR)
+        for i in range(BATCH)
     ]
 
     def part(ref, unit):
@@ -102,7 +104,7 @@
         width *= 2
     solved = [mm(x, r).astype(BF16) for x, r in zip(inverse, right)]
     carried = [mm(e, s, TN) for e, s in zip(key_end, solved)]
-    for i in range(PAIR):
+    for i in range(BATCH):
         running = None
         for j in range(chunk_count):
             u = i * chunk_count + j
@@ -122,7 +124,8 @@
         map_ref[i] = running.astype(BF16)
 
 
-def read_kernel(now_ref, back_ref, solved_ref, mid_ref, start_ref, through_ref, settled_ref):
+def read_kernel(now_ref, back_ref, solved_ref, mid_ref, start_ref, *refs):
+    through_ref, settled_ref = refs[-2:]
     chunk_count = now_ref.shape[0] // CHUNK
     later, earlier = positions()
     lower = later >= earlier
@@ -144,62 +147,54 @@
                 settled_ref[rows, lanes] = local
 
 
-def follow(later, earlier):
-    moved = mm(later[:, :HEAD_SIZE], earlier)
-    width = earlier.shape[1]
-    if width == HEAD_SIZE:
-        return moved + later[:, HEAD_SIZE:].astype(F32)
-    return jnp.concatenate(
-        [
-            moved[:, :HEAD_SIZE],
-            moved[:, HEAD_SIZE:] + later[:, HEAD_SIZE:].astype(F32),
-        ],
-        axis=1,
-    )
-
-
-def join_kernel(place_ref, own_ref, came_ref, early_ref, *refs):
-    slots, joined_ref = refs[:-1], refs[-1]
-    second = place_ref[0] == 1
+def follow(maps, states):
+    moved = mm(maps[:, :HEAD_SIZE], states)
+    written = maps[:, HEAD_SIZE:].astype(F32)
+    if states.shape[1] == HEAD_SIZE:
+        return moved + written
+    return jnp.concatenate([moved[:, :HEAD_SIZE], moved[:, HEAD_SIZE:] + written], axis=1)
+
+
+def join_kernel(level, place_ref, own_ref, came_ref, early_ref, keep_ref, send_ref, joined_ref):
+    second = place_ref[level] == 1
+    half = keep_ref.shape[0]
     for j in range(own_ref.shape[0]):
         own, came = own_ref[j], came_ref[j]
         early = jnp.where(second, came, own)
         early_ref[j] = early
         joined_ref[j] = follow(jnp.where(second, own, came), early).astype(BF16)
-    for r in range(len(slots)):
-        slots[r][...] = joined_ref[place_ref[1] ^ r]
-
-
-def chain_kernel(place_ref, *refs):
-    count = (len(refs) - 2) // 2
-    came, slots = refs[:count], refs[count : 2 * count]
-    map_ref, state_ref = refs[2 * count :]
-    place = place_ref[1]
-    for r in range(count):
-        map_ref[r] = came[r][...]
-    state_ref[0] = jnp.zeros((HEAD_SIZE, HEAD_SIZE), BF16)
-    state = map_ref[place, :, HEAD_SIZE:].astype(F32)
-    for turn in range(1, count):
-        high = state.astype(BF16)
-        state_ref[turn] = high
-        if turn + 1 < count:
-            item = map_ref[turn ^ place]
-            low = (state - high.astype(F32)).astype(BF16)
-            moved = mm(item[:, :HEAD_SIZE], jnp.concatenate([high, low], axis=1))
-            state = (
-                moved[:, :HEAD_SIZE] + moved[:, HEAD_SIZE:] + item[:, HEAD_SIZE:].astype(F32)
-            )
-    for r in range(count):
-        slots[r][...] = state_ref[place ^ r]
-
-
-def pass_kernel(place_ref, early_ref, *refs):
-    count = len(refs) - 3
-    keep_ref, send_ref, state_ref = refs[count:]
-    second = place_ref[0] == 1
-    for r in range(count):
-        state_ref[place_ref[1] ^ r] = refs[r][...]
-    for j in range(count):
+    for j in range(half):
+        keep_ref[j] = joined_ref[place_ref[level + 1] * half + j]
+        send_ref[j] = joined_ref[(1 - place_ref[level + 1]) * half + j]
+
+
+def crest_kernel(level, place_ref, own_ref, came_ref, early_ref, send_ref):
+    second = place_ref[level] == 1
+    for j in range(own_ref.shape[0]):
+        own, came = own_ref[j], came_ref[j]
+        early = jnp.where(second, came, own)
+        early_ref[j] = early
+        late = jnp.where(second, own, came)
+        send_ref[j] = follow(late, early[:, HEAD_SIZE:]).astype(BF16)
+
+
+def turn_kernel(level, place_ref, early_ref, came_ref, keep_ref, send_ref):
+    second, later = place_ref[level] == 1, place_ref[level + 1] == 1
+    for j in range(early_ref.shape[0]):
+        came = came_ref[j]
+        state = jnp.where(later, came, jnp.zeros_like(came))
+        after = follow(early_ref[j], state).astype(BF16)
+        keep_ref[j] = jnp.where(second, after, state)
+        send_ref[j] = jnp.where(second, state, after)
+
+
+def pass_kernel(level, place_ref, early_ref, own_ref, came_ref, keep_ref, send_ref, state_ref):
+    second = place_ref[level] == 1
+    half = own_ref.shape[0]
+    for j in range(half):
+        state_ref[place_ref[level + 1] * half + j] = own_ref[j]
+        state_ref[(1 - place_ref[level + 1]) * half + j] = came_ref[j]
+    for j in range(2 * half):
         state = state_ref[j]
         after = follow(early_ref[j], state).astype(BF16)
         keep_ref[j] = jnp.where(second, after, state)
@@ -280,9 +275,9 @@
     rows, width = operands[0].shape
     heads = operands[4].shape[0]
     chunks = rows // CHUNK
-    lanes = PAIR * HEAD_SIZE
+    lanes = BATCH * HEAD_SIZE
     column = pl.BlockSpec((rows, lanes), lambda s, p: (0, p[0] + s))
-    share = pairs * PAIR * chunks
+    share = pairs * BATCH * chunks
     return pl.pallas_call(
         maps_kernel,
         grid_spec=pltpu.PrefetchScalarGridSpec(
@@ -290,21 +285,21 @@
             grid=(pairs,),
             in_specs=[column] * 4
             + [pl.BlockSpec((heads, rows), lambda s, p: (0, 0))]
-            + [pl.BlockSpec(memory_space=pl.ANY)] * len(previous),
+            + [pl.BlockSpec(memory_space=pltpu.HBM)] * len(previous),
             out_specs=[
-                pl.BlockSpec((PAIR, HEAD_SIZE, 2 * HEAD_SIZE), lambda s, p: (s, 0, 0)),
+                pl.BlockSpec((BATCH, HEAD_SIZE, 2 * HEAD_SIZE), lambda s, p: (s, 0, 0)),
                 pl.BlockSpec((rows, 2 * lanes), lambda s, p: (0, p[0] + s)),
                 column,
                 column,
                 pl.BlockSpec((chunks, lanes), lambda s, p: (0, p[0] + s)),
                 pl.BlockSpec(
-                    (PAIR, chunks - 1, HEAD_SIZE, 2 * HEAD_SIZE),
+                    (BATCH, chunks - 1, HEAD_SIZE, 2 * HEAD_SIZE),
                     lambda s, p: (p[0] + s, 0, 0, 0),
                 ),
             ],
         ),
         out_shape=[
-            jax.ShapeDtypeStruct((PAIR * pairs, HEAD_SIZE, 2 * HEAD_SIZE), BF16),
+            jax.ShapeDtypeStruct((BATCH * pairs, HEAD_SIZE, 2 * HEAD_SIZE), BF16),
             pltpu.HBM((rows, 2 * width), BF16),
             pltpu.HBM((rows, width), BF16),
             pltpu.HBM((rows, width), BF16),
@@ -319,38 +314,35 @@
     )(first, *operands, *previous)
 
 
-def finish_reading(held):
+def finish_reading(held, first, pairs, previous):
     solved, back, now, mids, starts = held
     rows, width = now.shape
-    heads = width // HEAD_SIZE
     chunks = rows // CHUNK
     lanes = PAIR * HEAD_SIZE
-    column = pl.BlockSpec((rows, lanes), lambda h: (0, h))
+    column = pl.BlockSpec((rows, lanes), lambda h: (0, first + h))
     return pl.pallas_call(
         read_kernel,
-        grid=(heads // PAIR,),
+        grid=(pairs,),
         in_specs=[
             column,
             column,
-            pl.BlockSpec((rows, 2 * lanes), lambda h: (0, h)),
-            pl.BlockSpec((chunks, lanes), lambda h: (0, h)),
+            pl.BlockSpec((rows, 2 * lanes), lambda h: (0, first + h)),
+            pl.BlockSpec((chunks, lanes), lambda h: (0, first + h)),
             pl.BlockSpec(
-                (PAIR, chunks - 1, HEAD_SIZE, 2 * HEAD_SIZE), lambda h: (h, 0, 0, 0)
+                (PAIR, chunks - 1, HEAD_SIZE, 2 * HEAD_SIZE), lambda h: (first + h, 0, 0, 0)
             ),
-        ],
+        ]
+        + [pl.BlockSpec(memory_space=pltpu.HBM)] * len(previous),
         out_specs=[column, column],
-        out_shape=[
-            pltpu.HBM((rows, width), BF16),
-            pltpu.HBM((rows, width), F32),
-        ],
+        out_shape=[pltpu.HBM((rows, width), BF16), pltpu.HBM((rows, width), F32)],
+        input_output_aliases={5 + n: n for n in range(len(previous))},
         cost_estimate=pl.CostEstimate(
-            flops=heads * chunks * 100_000_000,
-            bytes_accessed=heads * chunks * 400_000,
+            flops=pairs * PAIR * chunks * 100_000_000,
+            bytes_accessed=pairs * PAIR * chunks * 400_000,
             transcendentals=0,
         ),
         compiler_params=pltpu.CompilerParams(vmem_limit_bytes=LIMIT << 20),
-        name="read",
-    )(*in_hbm(now, back, solved, mids, starts))
+    )(*in_hbm(now, back, solved, mids, starts), *previous)
 
 
 def project(places, through, settled, gates, states, gain, weight, groups):
@@ -425,39 +417,60 @@
 
 def carry_apart(operands, place, axis):
     count = lax.axis_size(axis)
-    half = count // 2
-    side, turn = lax.rem(place, 2), lax.div(place, 2)
-    place_at = jnp.stack([side, turn]).astype(jnp.int32)
-    pairs = half // PAIR
+    heads = operands[4].shape[0]
+    bits = [lax.rem(lax.div(place, 1 << n), 2) for n in range(3)]
+    place_at = jnp.stack(bits).astype(jnp.int32)
+    half, quarter = heads // 2, heads // 4
+    pairs, batches = half // PAIR, half // BATCH
 
     def swap(block, step):
         return lax.ppermute(block, axis, [(d, d ^ step) for d in range(count)])
 
     def first(group):
-        return jnp.reshape(group * pairs, (1,)).astype(jnp.int32)
+        return jnp.reshape(group * batches, (1,)).astype(jnp.int32)
 
     item, square = (HEAD_SIZE, 2 * HEAD_SIZE), (HEAD_SIZE, HEAD_SIZE)
-    far = make_maps(operands, first(1 - side), pairs, [])
+    far = make_maps(operands, first(1 - bits[0]), batches, [])
     came = swap(far[0], 1)
-    near = make_maps(operands, first(side), pairs, far[1:])
-    early, *slots = small_call(
-        join_kernel, place_at, [near[0], came], [(half, *item)] + [item] * half, [(half, *item)]
-    )
-    slots = [slots[0]] + [swap(slots[r], 2 * r) for r in range(1, half)]
-    reads = finish_reading(near[1:])
-    states = small_call(
-        chain_kernel, place_at, slots, [square] * half, [(half, *item), (half, *square)]
-    )
-    states = [states[0]] + [swap(states[r], 2 * r) for r in range(1, half)]
+    near = make_maps(operands, first(bits[0]), batches, far[1:])
+    held = near[1:]
+    early, keep, send = small_call(
+        functools.partial(join_kernel, 0),
+        place_at,
+        [near[0], came],
+        [(half, *item), (quarter, *item), (quarter, *item)],
+        [(half, *item)],
+    )
+    came = swap(send, 2)
+    reads = finish_reading(held, 0, PIECES[0], [])
+    crest, send = small_call(
+        functools.partial(crest_kernel, 1),
+        place_at,
+        [keep, came],
+        [(quarter, *item), (quarter, *square)],
+        [],
+    )
+    came = swap(send, 4)
+    reads = finish_reading(held, PIECES[0], PIECES[1], reads)
     keep, send = small_call(
-        pass_kernel, place_at, [early, *states], [(half, *square)] * 2, [(half, *square)]
-    )
-    return reads, [keep, swap(send, 1)], side
+        functools.partial(turn_kernel, 1), place_at, [crest, came], [(quarter, *square)] * 2, []
+    )
+    came = swap(send, 2)
+    done = PIECES[0] + PIECES[1]
+    reads = finish_reading(held, done, 2 * pairs - done, reads)
+    keep, send = small_call(
+        functools.partial(pass_kernel, 0),
+        place_at,
+        [early, keep, came],
+        [(half, *square)] * 2,
+        [(half, *square)],
+    )
+    return reads, [keep, swap(send, 1)], bits[0]
 
 
 def carry_whole(operands, axis):
     heads = operands[4].shape[0]
-    made = make_maps(operands, jnp.zeros((1,), jnp.int32), heads // PAIR, [])
+    made = make_maps(operands, jnp.zeros((1,), jnp.int32), heads // BATCH, [])
     gathered = lax.all_gather(made[0], axis)
 
     def one(turn, state):
@@ -469,7 +482,8 @@
 
     zero = jnp.zeros((heads, HEAD_SIZE, HEAD_SIZE), F32)
     state = lax.fori_loop(0, lax.axis_index(axis), one, zero)
-    return finish_reading(made[1:]), [state.astype(BF16)], 0
+    reads = finish_reading(made[1:], 0, heads // PAIR, [])
+    return reads, [state.astype(BF16)], 0
 
 
 def on_device(
@@ -485,7 +499,7 @@
     heads = query_vectors.shape[1] // HEAD_SIZE
     operands = in_hbm(query_vectors, key_vectors, value_vectors, log_decay, write_rate.T)
     count = lax.axis_size("ctx")
-    if heads == count and count & (count - 1) == 0 and count >= 8:
+    if count == 8 and heads == 8:
         reads, states, twist = carry_apart(operands, lax.axis_index("ctx"), "ctx")
     else:
         reads, states, twist = carry_whole(operands, "ctx")

time: 68.2 us -> 64.3 us (0.943)
  waiting for transfers between devices: 22.3 us -> 19.6 us
  starting transfers between devices: 14.2 us -> 12.9 us
    pallas_call x2, Pallas kernels: 14.7 us -> 10.6 us  [make_maps(): pl.pallas_call(maps_kernel, grid_spec=pltpu.PrefetchScalarGridSpec(num_sc...]
    pallas_call x1 -> x3, Pallas kernels: 6.92 us -> 10.8 us  [finish_reading(): pl.pallas_call(read_kernel, grid=(pairs,), in_specs=[column, column, pl.B...]
    ppermute x8 -> x5, waiting for transfers between devices: 9.24 us -> 6.53 us  [swap(): return lax.ppermute(block, axis, [(d, d ^ step) for d in range(count)])]
    ppermute x8 -> x5, starting transfers between devices: 12.6 us -> 11.2 us  [swap(): return lax.ppermute(block, axis, [(d, d ^ step) for d in range(count)])]
    pallas_call x3 -> x4, Pallas kernels: 2.43 us -> 2.95 us  [small_call(): pl.pallas_call(kernel, grid_spec=pltpu.PrefetchScalarGridSpec(num_scalar_...]
  transfers between devices with their start and end apart: 10 -> 7, of which waited for: 6 -> 6; matrix products, arithmetic and copies ran while one was open for 0% -> 0% of each run, Pallas kernels for 21% -> 25%
where the time goes in v4:
time: 64.3 us; the launch traced here: 64.1 us
  Pallas kernels  30.3 us (47%)
  waiting for transfers between devices  19.6 us (30%)
  starting transfers between devices  12.9 us (20%)
  other arithmetic  1.19 us (2%)
    ppermute x5, starting transfers between devices, swap(): return lax.ppermute(block, axis, [(d, d ^ step) for d in range(count)])  11.2 us
    pallas_call x3, Pallas kernels, finish_reading(): pl.pallas_call(read_kernel, grid=(pairs,), in_specs=[column, column, pl.B...  10.8 us
    ppermute x1, waiting for transfers between devices, on_device(): total = total + lax.ppermute(away, 'head', hops).astype(F32)  10.7 us
    pallas_call x2, Pallas kernels, make_maps(): pl.pallas_call(maps_kernel, grid_spec=pltpu.PrefetchScalarGridSpec(num_sc...  10.6 us
    ppermute x5, waiting for transfers between devices, swap(): return lax.ppermute(block, axis, [(d, d ^ step) for d in range(count)])  6.53 us
    pallas_call x1, Pallas kernels, project(): pl.pallas_call(functools.partial(output_kernel, len(states)), grid_spec=p...  5.99 us
    pallas_call x4, Pallas kernels, small_call(): pl.pallas_call(kernel, grid_spec=pltpu.PrefetchScalarGridSpec(num_scalar_...  2.95 us
    ppermute x1, waiting for transfers between devices, on_device(): came = lax.ppermute(other, 'head', [(d, d ^ 1) for d in range(groups)])  2.4 us
  transfers between devices with their start and end apart: 7, of which 6 were waited for; matrix products, arithmetic and copies ran while one was open for 0% of the time, Pallas kernels for 25%

profile of v4, /device:TPU:0, one launch (start us, length us, event | category | flops | bytes accessed | tf_op | source)
XLA Modules:
  0.0 64.1 jit_solution(8018729434949952844)
XLA Ops:
  0.0 5.3 %shard_map.82 = (bf16[4,128,256]{2,1,0:T(8,128)(2,1)S(1)}, bf16[384,2048]{1,0:T(8,128)(2,1)}, bf16[384,1024]{1,0:T(8,128)(2,1)}, bf16[384,1024]{1,0:T(8,128)(2,1...) custom-call(s32[1]{0:T(128)} %bitcast.3.first_ref, bf16[384,1024]{1,0:T(8,128)(2,1)} %query_ref.3, ...), custom_call_target="tpu_custom_call" | custom-call | flops 1440000000 | bytes 4800000 | tf_op jit(solution)/shard_map/pallas_call | solution.py:281
  5.3 3.0 %collective-permute-start = (bf16[4,128,256]{2,1,0:T(8,128)(2,1)S(1)}, bf16[4,128,256]{2,1,0:T(8,128)(2,1)S(1)}, u32[]{:S(2)}, u32[]{:S(2)}) collective-permute-start(bf16[4,128,256]{2,1,0:T(8,128)(2,1)S(1)} %get-tuple-element.51), channel_id=1, source_target_pairs={{0,4},{4,0},{8,12},{12,8},{16,20},{20,16},{24,28},{28,24},{1,5},{5... | collective-permute-start | bytes 786440 | tf_op jit(solution)/shard_map/ppermute | solution.py:427
  8.3 0.1 pad_add_fusion.1.place_ref
  8.4 5.3 %shard_map.83 = (bf16[4,128,256]{2,1,0:T(8,128)(2,1)S(1)}, bf16[384,2048]{1,0:T(8,128)(2,1)}, bf16[384,1024]{1,0:T(8,128)(2,1)}, bf16[384,1024]{1,0:T(8,128)(2,1...) custom-call(s32[1]{0:T(128)} %bitcast.1.first_ref, ...), custom_call_target="tpu_custom_call", output_to_operand_aliasing={{1}: (6, {}), {2}: (7, {}), {3}: (8, {}), {4}: (9, {}), {5}... | custom-call | flops 1440000000 | bytes 4800000 | tf_op jit(solution)/shard_map/pallas_call | solution.py:281
  13.7 0.9 %collective-permute-done.came_ref = bf16[4,128,256]{2,1,0:T(8,128)(2,1)S(1)} collective-permute-done((bf16[4,128,256]{2,1,0:T(8,128)(2,1)S(1)}, bf16[4,128,256]{2,1,0:T(8,128)(2,1)S(1)}, u32[]{:S(2)}, u32[]{:S(2)}) %collective-permute-start) | collective-permute-done | bytes 262176 | tf_op jit(solution)/shard_map/ppermute | solution.py:427
  14.6 0.8 %shard_map.87 = (bf16[4,128,256]{2,1,0:T(8,128)(2,1)S(1)}, bf16[2,128,256]{2,1,0:T(8,128)(2,1)S(1)}, bf16[2,128,256]{2,1,0:T(8,128)(2,1)S(1)}) custom-call(s32[3]{0:T(128)S(1)} %pad_add_fusion.1.place_ref, bf16[4,128,256]{2,1,0:T(8,128)(2,1)S(1)} %get-tuple-element.50.own_ref, bf16[4,128,256]{2,1,0:T(8,128)(2,1)S(1)} %collective-permute-done.came_ref), custom_call_target="tpu_custom_call" | custom-call | tf_op jit(solution)/shard_map/pallas_call | solution.py:404
  15.4 1.9 %collective-permute-start.1 = (bf16[2,128,256]{2,1,0:T(8,128)(2,1)S(1)}, bf16[2,128,256]{2,1,0:T(8,128)(2,1)S(1)}, u32[]{:S(2)}, u32[]{:S(2)}) collective-permute-start(bf16[2,128,256]{2,1,0:T(8,128)(2,1)S(1)} %get-tuple-element.54), channel_id=1, source_target_pairs={{0,8},{4,12},{8,0},{12,4},{16,24},{20,28},{24,16},{28,20},{1,9},{5... | collective-permute-start | bytes 393224 | tf_op jit(solution)/shard_map/ppermute | solution.py:427
  17.3 3.1 %collective-permute-done.1.came_ref = bf16[2,128,256]{2,1,0:T(8,128)(2,1)S(1)} collective-permute-done((bf16[2,128,256]{2,1,0:T(8,128)(2,1)S(1)}, bf16[2,128,256]{2,1,0:T(8,128)(2,1)S(1)}, u32[]{:S(2)}, u32[]{:S(2)}) %collective-permute-start.1) | collective-permute-done | bytes 131104 | tf_op jit(solution)/shard_map/ppermute | solution.py:427
  20.4 0.7 %shard_map.88 = (bf16[2,128,256]{2,1,0:T(8,128)(2,1)S(1)}, bf16[2,128,128]{2,1,0:T(8,128)(2,1)S(1)}) custom-call(s32[3]{0:T(128)S(1)} %pad_add_fusion.1.place_ref, bf16[2,128,256]{2,1,0:T(8,128)(2,1)S(1)} %get-tuple-element.53.own_ref, bf16[2,128,256]{2,1,0:T(8,128)(2,1)S(1)} %collective-permute-done.1.came_ref), custom_call_target="tpu_custom_call" | custom-call | tf_op jit(solution)/shard_map/pallas_call | solution.py:404
  21.1 2.9 %collective-permute-start.2 = (bf16[2,128,128]{2,1,0:T(8,128)(2,1)S(1)}, bf16[2,128,128]{2,1,0:T(8,128)(2,1)S(1)}, u32[]{:S(2)}, u32[]{:S(2)}) collective-permute-start(bf16[2,128,128]{2,1,0:T(8,128)(2,1)S(1)} %get-tuple-element.56), channel_id=1, source_target_pairs={{0,16},{4,20},{8,24},{12,28},{16,0},{20,4},{24,8},{28,12},{1,17},{... | collective-permute-start | bytes 196616 | tf_op jit(solution)/shard_map/ppermute | solution.py:427
  24.0 2.3 %collective-permute-done.2.came_ref = bf16[2,128,128]{2,1,0:T(8,128)(2,1)S(1)} collective-permute-done((bf16[2,128,128]{2,1,0:T(8,128)(2,1)S(1)}, bf16[2,128,128]{2,1,0:T(8,128)(2,1)S(1)}, u32[]{:S(2)}, u32[]{:S(2)}) %collective-permute-start.2) | collective-permute-done | bytes 65568 | tf_op jit(solution)/shard_map/ppermute | solution.py:427
  26.3 0.7 %shard_map.89 = (bf16[2,128,128]{2,1,0:T(8,128)(2,1)S(1)}, bf16[2,128,128]{2,1,0:T(8,128)(2,1)S(1)}) custom-call(s32[3]{0:T(128)S(1)} %pad_add_fusion.1.place_ref, bf16[2,128,256]{2,1,0:T(8,128)(2,1)S(1)} %get-tuple-element.55.early_ref, bf16[2,128,128]{2,1,0:T(8,128)(2,1)S(1)} %collective-permute-done.2.came_ref), custom_call_target="tpu_custom_call" | custom-call | tf_op jit(solution)/shard_map/pallas_call | solution.py:404
  27.1 1.9 %collective-permute-start.3 = (bf16[2,128,128]{2,1,0:T(8,128)(2,1)S(1)}, bf16[2,128,128]{2,1,0:T(8,128)(2,1)S(1)}, u32[]{:S(2)}, u32[]{:S(2)}) collective-permute-start(bf16[2,128,128]{2,1,0:T(8,128)(2,1)S(1)} %get-tuple-element.58), channel_id=1, source_target_pairs={{0,8},{4,12},{8,0},{12,4},{16,24},{20,28},{24,16},{28,20},{1,9},{5... | collective-permute-start | bytes 196616 | tf_op jit(solution)/shard_map/ppermute | solution.py:427
  29.0 4.3 %shard_map.84 = (bf16[384,1024]{1,0:T(8,128)(2,1)}, f32[384,1024]{1,0:T(8,128)}) custom-call(bf16[384,1024]{1,0:T(8,128)(2,1)} %get-tuple-element.39.now_ref, bf16[384,1024]{1,0:T(8,128)(2,1)} %get-tuple-element.40.back_ref, bf16[384,2048]{1,0:T(8,128)(2,1)} %get-tuple-element.41.solved_ref, f32[3,1024]{1,0:T(4,128)} %get-tuple-element.42.mid_ref, ...), custom_call_target="tpu_custom_call" | custom-call | flops 1200000000 | bytes 4800000 | tf_op jit(solution)/shard_map/pallas_call | solution.py:323
  33.3 3.2 %shard_map.85 = (bf16[384,1024]{1,0:T(8,128)(2,1)}, f32[384,1024]{1,0:T(8,128)}) custom-call(bf16[384,1024]{1,0:T(8,128)(2,1)} %get-tuple-element.39.now_ref, bf16[384,1024]{1,0:T(8,128)(2,1)} %get-tuple-element.40.back_ref, bf16[384,2048]{1,0:T(8,128)(2,1)} %get-tuple-element.41.solved_ref, ...), custom_call_target="tpu_custom_call", output_to_operand_aliasing={{0}: (5, {}), {1}: (6, {})} | custom-call | flops 600000000 | bytes 2400000 | tf_op jit(solution)/shard_map/pallas_call | solution.py:323
  36.5 0.0 collective-permute-done.3.came_ref
  36.5 0.7 %shard_map.90 = (bf16[4,128,128]{2,1,0:T(8,128)(2,1)S(1)}, bf16[4,128,128]{2,1,0:T(8,128)(2,1)S(1)}) custom-call(s32[3]{0:T(128)S(1)} %pad_add_fusion.1.place_ref, bf16[4,128,256]{2,1,0:T(8,128)(2,1)S(1)} %get-tuple-element.52.early_ref, bf16[2,128,128]{2,1,0:T(8,128)(2,1)S(1)} %get-tuple-element.57.own_ref, ...), custom_call_target="tpu_custom_call" | custom-call | tf_op jit(solution)/shard_map/pallas_call | solution.py:404
  37.3 1.5 %collective-permute-start.4 = (bf16[4,128,128]{2,1,0:T(8,128)(2,1)S(1)}, bf16[4,128,128]{2,1,0:T(8,128)(2,1)S(1)}, u32[]{:S(2)}, u32[]{:S(2)}) collective-permute-start(bf16[4,128,128]{2,1,0:T(8,128)(2,1)S(1)} %get-tuple-element.60), channel_id=1, source_target_pairs={{0,4},{4,0},{8,12},{12,8},{16,20},{20,16},{24,28},{28,24},{1,5},{5... | collective-permute-start | bytes 393224 | tf_op jit(solution)/shard_map/ppermute | solution.py:427
  38.8 0.0 copy-start
  38.8 3.2 %shard_map.86 = (bf16[384,1024]{1,0:T(8,128)(2,1)}, f32[384,1024]{1,0:T(8,128)}) custom-call(bf16[384,1024]{1,0:T(8,128)(2,1)} %get-tuple-element.39.now_ref, bf16[384,1024]{1,0:T(8,128)(2,1)} %get-tuple-element.40.back_ref, bf16[384,2048]{1,0:T(8,128)(2,1)} %get-tuple-element.41.solved_ref, ...), custom_call_target="tpu_custom_call", output_to_operand_aliasing={{0}: (5, {}), {1}: (6, {})} | custom-call | flops 600000000 | bytes 2400000 | tf_op jit(solution)/shard_map/pallas_call | solution.py:323
  42.0 0.1 pad_add_fusion.place_ref
  42.1 0.2 collective-permute-done.4.refs_1_
  42.3 0.0 copy-done
  42.3 6.0 %output.1 = (bf16[2,96,2304]{2,1,0:T(8,128)(2,1)S(1)}, bf16[2,96,2304]{2,1,0:T(8,128)(2,1)S(1)}) custom-call(s32[2]{0:T(128)S(1)} %pad_add_fusion.place_ref, bf16[384,1024]{1,0:T(8,128)(2,1)} %get-tuple-element.48.through_hbm, f32[384,1024]{1,0:T(8,128)} %get-tuple-element.49.settled_hbm, bf16[384,1024]{1,0:T(8,128)(2,1)} %gate_hbm.1, ...), custom_call_target="tpu_custom_call" | custom-call | flops 1811939328 | bytes 4718592 | tf_op jit(solution)/shard_map/output/pallas_call | solution.py:357
  48.3 0.1 collective-permute-start.5
  48.4 2.4 %collective-permute-done.5 = bf16[2,96,2304]{2,1,0:T(8,128)(2,1)S(1)} collective-permute-done((bf16[2,96,2304]{2,1,0:T(8,128)(2,1)S(1)}, bf16[2,96,2304]{2,1,0:T(8,128)(2,1)S(1)}, u32[]{:S(2)}, u32[]{:S(2)}) %collective-permute-start.5) | collective-permute-done | bytes 884768 | tf_op jit(solution)/shard_map/ppermute | solution.py:513
  50.8 0.1 fusion.1
  50.9 1.6 %collective-permute-start.6 = (bf16[96,2304]{1,0:T(8,128)(2,1)S(1)}, bf16[96,2304]{1,0:T(8,128)(2,1)S(1)}, u32[]{:S(2)}, u32[]{:S(2)}) collective-permute-start(bf16[96,2304]{1,0:T(8,128)(2,1)S(1)} %fusion.1), channel_id=1, source_target_pairs={{0,2},{1,3},{2,0},{3,1},{4,6},{5,7},{6,4},{7,5},{8,10},{9,11},{10,... | collective-permute-start | bytes 1327112 | tf_op jit(solution)/shard_map/ppermute | solution.py:524
  52.5 10.7 %collective-permute-done.6 = bf16[96,2304]{1,0:T(8,128)(2,1)S(1)} collective-permute-done((bf16[96,2304]{1,0:T(8,128)(2,1)S(1)}, bf16[96,2304]{1,0:T(8,128)(2,1)S(1)}, u32[]{:S(2)}, u32[]{:S(2)}) %collective-permute-start.6) | collective-permute-done | bytes 442400 | tf_op jit(solution)/shard_map/ppermute | solution.py:524
  63.2 0.9 %fusion = bf16[96,2304]{1,0:T(8,128)(2,1)} fusion(bf16[96,2304]{1,0:T(8,128)(2,1)S(1)} %collective-permute-done.6, bf16[2,96,2304]{2,1,0:T(8,128)(2,1)S(1)} %collective-permute-done.5, s32[]{:T(128)S(6)} %select_n.9, bf16[2,96,2304]{2,1,0:T(8,128)(2,1)S(1)} %get-tuple-element.61), kind=kLoop, calls=%fused_computation.1 | loop fusion | flops 1327104 | bytes 1769476 | tf_op jit(solution)/shard_map/convert_element_type | solution.py:525
Async XLA Ops:
  5.3 9.3 %collective-permute-start = (bf16[4,128,256]{2,1,0:T(8,128)(2,1)S(1)}, bf16[4,128,256]{2,1,0:T(8,128)(2,1)S(1)}, u32[]{:S(2)}, u32[]{:S(2)}) collective-permute-start(bf16[4,128,256]{2,1,0:T(8,128)(2,1)S(1)} %get-tuple-element.51), channel_id=1, source_target_pairs={{0,4},{4,0},{8,12},{12,8},{16,20},{20,16},{24,28},{28,24},{1,5},{5... | collective-permute-start | bytes 786440 | tf_op jit(solution)/shard_map/ppermute | solution.py:427
  15.4 5.0 %collective-permute-start.1 = (bf16[2,128,256]{2,1,0:T(8,128)(2,1)S(1)}, bf16[2,128,256]{2,1,0:T(8,128)(2,1)S(1)}, u32[]{:S(2)}, u32[]{:S(2)}) collective-permute-start(bf16[2,128,256]{2,1,0:T(8,128)(2,1)S(1)} %get-tuple-element.54), channel_id=1, source_target_pairs={{0,8},{4,12},{8,0},{12,4},{16,24},{20,28},{24,16},{28,20},{1,9},{5... | collective-permute-start | bytes 393224 | tf_op jit(solution)/shard_map/ppermute | solution.py:427
  21.1 5.2 %collective-permute-start.2 = (bf16[2,128,128]{2,1,0:T(8,128)(2,1)S(1)}, bf16[2,128,128]{2,1,0:T(8,128)(2,1)S(1)}, u32[]{:S(2)}, u32[]{:S(2)}) collective-permute-start(bf16[2,128,128]{2,1,0:T(8,128)(2,1)S(1)} %get-tuple-element.56), channel_id=1, source_target_pairs={{0,16},{4,20},{8,24},{12,28},{16,0},{20,4},{24,8},{28,12},{1,17},{... | collective-permute-start | bytes 196616 | tf_op jit(solution)/shard_map/ppermute | solution.py:427
  27.1 9.4 %collective-permute-start.3 = (bf16[2,128,128]{2,1,0:T(8,128)(2,1)S(1)}, bf16[2,128,128]{2,1,0:T(8,128)(2,1)S(1)}, u32[]{:S(2)}, u32[]{:S(2)}) collective-permute-start(bf16[2,128,128]{2,1,0:T(8,128)(2,1)S(1)} %get-tuple-element.58), channel_id=1, source_target_pairs={{0,8},{4,12},{8,0},{12,4},{16,24},{20,28},{24,16},{28,20},{1,9},{5... | collective-permute-start | bytes 196616 | tf_op jit(solution)/shard_map/ppermute | solution.py:427
  37.3 5.0 %collective-permute-start.4 = (bf16[4,128,128]{2,1,0:T(8,128)(2,1)S(1)}, bf16[4,128,128]{2,1,0:T(8,128)(2,1)S(1)}, u32[]{:S(2)}, u32[]{:S(2)}) collective-permute-start(bf16[4,128,128]{2,1,0:T(8,128)(2,1)S(1)} %get-tuple-element.60), channel_id=1, source_target_pairs={{0,4},{4,0},{8,12},{12,8},{16,20},{20,16},{24,28},{28,24},{1,5},{5... | collective-permute-start | bytes 393224 | tf_op jit(solution)/shard_map/ppermute | solution.py:427
  38.8 3.5 %copy-start = (f32[128]{0:T(128)S(1)}, f32[128]{0:T(128)}, u32[]{:S(2)}) copy-start(f32[128]{0:T(128)} %param.14) | copy-start | bytes 1540
  48.3 2.5 %collective-permute-start.5 = (bf16[2,96,2304]{2,1,0:T(8,128)(2,1)S(1)}, bf16[2,96,2304]{2,1,0:T(8,128)(2,1)S(1)}, u32[]{:S(2)}, u32[]{:S(2)}) collective-permute-start(bf16[2,96,2304]{2,1,0:T(8,128)(2,1)S(1)} %get-tuple-element.62), channel_id=1, source_target_pairs={{0,1},{1,0},{2,3},{3,2},{4,5},{5,4},{6,7},{7,6},{8,9},{9,8},{10,11... | collective-permute-start | bytes 2654216 | tf_op jit(solution)/shard_map/ppermute | solution.py:513
  50.9 12.3 %collective-permute-start.6 = (bf16[96,2304]{1,0:T(8,128)(2,1)S(1)}, bf16[96,2304]{1,0:T(8,128)(2,1)S(1)}, u32[]{:S(2)}, u32[]{:S(2)}) collective-permute-start(bf16[96,2304]{1,0:T(8,128)(2,1)S(1)} %fusion.1), channel_id=1, source_target_pairs={{0,2},{1,3},{2,0},{3,1},{4,6},{5,7},{6,4},{7,5},{8,10},{9,11},{10,... | collective-permute-start | bytes 1327112 | tf_op jit(solution)/shard_map/ppermute | solution.py:524

commit v5 on v4

v5 whole, which is shorter than its diff:
```python
import functools

import jax
import jax.numpy as jnp
from jax import lax
from jax.experimental import pallas as pl
from jax.experimental.pallas import tpu as pltpu
from jax.sharding import PartitionSpec as P


HEAD_SIZE = 128
CHUNK = 128
BATCH = 4
LIMIT = 24
F32 = jnp.float32
BF16 = jnp.bfloat16
NT = (((1,), (1,)), ((), ()))
TN = (((0,), (0,)), ((), ()))
NN = (((1,), (0,)), ((), ()))


def mm(left, right, dims=NN):
    return lax.dot_general(
        left.astype(BF16), right.astype(BF16), dims, preferred_element_type=F32
    )


def positions():
    later = lax.broadcasted_iota(jnp.int32, (CHUNK, CHUNK), 0)
    earlier = lax.broadcasted_iota(jnp.int32, (CHUNK, CHUNK), 1)
    return later, earlier


def maps_kernel(
    first_ref, query_ref, key_ref, value_ref, decay_ref, rate_ref, *refs
):
    map_ref, through_ref, settled_ref = refs[-3:]
    chunk_count = key_ref.shape[0] // CHUNK
    first_head = (first_ref[0] + pl.program_id(0)) * BATCH
    later, earlier = positions()
    ones = (later >= earlier).astype(BF16)
    strict = later > earlier
    eye = (later == earlier).astype(F32)
    rates = rate_ref[...].T
    rate_lane = lax.broadcasted_iota(jnp.int32, rates.shape, 1)
    units = [(i, j) for i in range(BATCH) for j in range(chunk_count)]
    rate_cols = [
        jnp.sum(jnp.where(rate_lane == first_head + i, rates, 0.0), axis=1, keepdims=True)
        for i in range(BATCH)
    ]

    def part(ref, unit):
        i, j = unit
        return ref[j * CHUNK : (j + 1) * CHUNK, i * HEAD_SIZE : (i + 1) * HEAD_SIZE]

    right, key_end, final, coupling, inverse = [], [], [], [], []
    now, back, mid = [], [], []
    for unit in units:
        i, j = unit
        rows = slice(j * CHUNK, (j + 1) * CHUNK)
        logs = part(decay_ref, unit)
        high = logs.astype(BF16)
        low = (logs - high.astype(F32)).astype(BF16)
        total = mm(ones, high) + mm(ones, low)
        middle = total[CHUNK // 2 - 1 : CHUNK // 2]
        last = total[CHUNK - 1 :]
        ahead = jnp.exp(total - middle)
        behind = jnp.exp(middle - total)
        mid_scale = jnp.exp(middle)
        keys = part(key_ref, unit).astype(F32)
        keys = keys * lax.rsqrt(jnp.sum(keys * keys, axis=1, keepdims=True) + 1e-06)
        rate = rate_cols[i][rows]
        key_now = keys * ahead
        key_back = keys * behind
        now.append((part(query_ref, unit).astype(F32) * ahead).astype(BF16))
        back.append(key_back.astype(BF16))
        mid.append(mid_scale)
        coupling.append(jnp.where(strict, rate * mm(key_now, key_back, NT), 0.0))
        right.append(
            jnp.concatenate(
                [
                    (rate * key_now * mid_scale).astype(BF16),
                    (rate * part(value_ref, unit).astype(F32)).astype(BF16),
                ],
                axis=1,
            )
        )
        key_end.append((key_back * jnp.exp(last - middle)).astype(BF16))
        final.append(eye * jnp.exp(last))
    pair_mask = (later // 2) == (earlier // 2)
    inverse = [eye - jnp.where(pair_mask, c, 0.0) for c in coupling]
    width = 2
    while width < CHUNK:
        mask = ((later // (2 * width)) == (earlier // (2 * width))) & (
            (later // width) != (earlier // width)
        )
        inverse_low = [x.astype(BF16) for x in inverse]
        cross = [
            mm(x, jnp.where(mask, c, 0.0)).astype(BF16) for x, c in zip(inverse_low, coupling)
        ]
        inverse = [x - mm(y, z) for x, y, z in zip(inverse, cross, inverse_low)]
        width *= 2
    solved = [mm(x, r).astype(BF16) for x, r in zip(inverse, right)]
    carried = [mm(e, s, TN) for e, s in zip(key_end, solved)]
    lower = later >= earlier
    reading = [jnp.where(lower, mm(q, k, NT), 0.0) for q, k in zip(now, back)]
    mixed = [mm(r, s) for r, s in zip(reading, solved)]
    for i in range(BATCH):
        lanes = slice(i * HEAD_SIZE, (i + 1) * HEAD_SIZE)
        running = None
        for j in range(chunk_count):
            u = i * chunk_count + j
            rows = slice(j * CHUNK, (j + 1) * CHUNK)
            effective = now[u].astype(F32) * mid[u] - mixed[u][:, :HEAD_SIZE]
            local = mixed[u][:, HEAD_SIZE:]
            step = final[u] - carried[u][:, :HEAD_SIZE]
            write = carried[u][:, HEAD_SIZE:]
            if running is None:
                through_ref[rows, lanes] = effective.astype(BF16)
                settled_ref[rows, lanes] = local
                running = jnp.concatenate([step, write], axis=1)
            else:
                held = running.astype(BF16)
                seen = mm(effective, held)
                through_ref[rows, lanes] = seen[:, :HEAD_SIZE].astype(BF16)
                settled_ref[rows, lanes] = seen[:, HEAD_SIZE:] + local
                moved = mm(step, held)
                running = jnp.concatenate(
                    [moved[:, :HEAD_SIZE], moved[:, HEAD_SIZE:] + write], axis=1
                )
        map_ref[i] = running.astype(BF16)


def follow(maps, states):
    moved = mm(maps[:, :HEAD_SIZE], states)
    written = maps[:, HEAD_SIZE:].astype(F32)
    if states.shape[1] == HEAD_SIZE:
        return moved + written
    return jnp.concatenate([moved[:, :HEAD_SIZE], moved[:, HEAD_SIZE:] + written], axis=1)


def join_kernel(level, place_ref, own_ref, came_ref, early_ref, keep_ref, send_ref, joined_ref):
    second = place_ref[level] == 1
    half = keep_ref.shape[0]
    for j in range(own_ref.shape[0]):
        own, came = own_ref[j], came_ref[j]
        early = jnp.where(second, came, own)
        early_ref[j] = early
        joined_ref[j] = follow(jnp.where(second, own, came), early).astype(BF16)
    for j in range(half):
        keep_ref[j] = joined_ref[place_ref[level + 1] * half + j]
        send_ref[j] = joined_ref[(1 - place_ref[level + 1]) * half + j]


def crest_kernel(level, place_ref, own_ref, came_ref, early_ref, send_ref):
    second = place_ref[level] == 1
    for j in range(own_ref.shape[0]):
        own, came = own_ref[j], came_ref[j]
        early = jnp.where(second, came, own)
        early_ref[j] = early
        late = jnp.where(second, own, came)
        send_ref[j] = follow(late, early[:, HEAD_SIZE:]).astype(BF16)


def turn_kernel(level, place_ref, early_ref, came_ref, keep_ref, send_ref):
    second, later = place_ref[level] == 1, place_ref[level + 1] == 1
    for j in range(early_ref.shape[0]):
        came = came_ref[j]
        state = jnp.where(later, came, jnp.zeros_like(came))
        after = follow(early_ref[j], state).astype(BF16)
        keep_ref[j] = jnp.where(second, after, state)
        send_ref[j] = jnp.where(second, state, after)


def pass_kernel(level, place_ref, early_ref, own_ref, came_ref, keep_ref, send_ref, state_ref):
    second = place_ref[level] == 1
    half = own_ref.shape[0]
    for j in range(half):
        state_ref[place_ref[level + 1] * half + j] = own_ref[j]
        state_ref[(1 - place_ref[level + 1]) * half + j] = came_ref[j]
    for j in range(2 * half):
        state = state_ref[j]
        after = follow(early_ref[j], state).astype(BF16)
        keep_ref[j] = jnp.where(second, after, state)
        send_ref[j] = jnp.where(second, state, after)


def gate_heads(through_ref, settled_ref, gate_ref, state_ref, gain_ref, gated_ref):
    gain = gain_ref[...]
    for h in range(state_ref.shape[0]):
        lanes = slice(h * HEAD_SIZE, (h + 1) * HEAD_SIZE)
        attended = settled_ref[:, lanes] + mm(through_ref[:, lanes], state_ref[h])
        scale = lax.rsqrt(jnp.mean(attended * attended, axis=1, keepdims=True) + 1e-05)
        gate = jax.nn.sigmoid(gate_ref[:, lanes].astype(F32))
        gated_ref[:, lanes] = (attended * scale * gain * gate).astype(BF16)


def tile_spans(model):
    tile = model // 3 if model % 768 == 0 else model
    return [slice(n, n + tile) for n in range(0, model, tile)]


def early_kernel(
    chips, place_ref, through_hbm, settled_hbm, gate_hbm, weight_hbm, state_ref, gain_ref,
    total_ref, through_rest, settled_rest, gate_rest, weight_rest,
    through_ref, settled_ref, gate_ref, weight_ref, gated_ref, sems,
):
    core, side = place_ref[0], place_ref[1]
    rows, span = through_ref.shape
    block = rows // (2 * chips)
    waits = []

    def load(source, target):
        copy = pltpu.make_async_copy(source, target, sems.at[len(waits)])
        copy.start()
        waits.append(copy)

    def load_group(group, targets, weight_target):
        columns = pl.ds(pl.multiple_of(group * span, span), span)
        for source, target in zip((through_hbm, settled_hbm, gate_hbm), targets):
            for own in range(2):
                for chip in range(chips):
                    first = (2 * chip + (core if own else 1 - core)) * block
                    load(
                        source.at[pl.ds(pl.multiple_of(first, block), block), columns],
                        target.at[pl.ds((own * chips + chip) * block, block)],
                    )
        load(weight_hbm.at[columns], weight_target)

    load_group(side, (through_ref, settled_ref, gate_ref), weight_ref)
    near = len(waits)
    load_group(1 - side, (through_rest, settled_rest, gate_rest), weight_rest)
    for copy in waits[: near - 1]:
        copy.wait()
    gate_heads(through_ref, settled_ref, gate_ref, state_ref, gain_ref, gated_ref)
    waits[near - 1].wait()
    for tile in tile_spans(weight_ref.shape[1]):
        total_ref[:, tile] = jnp.dot(
            gated_ref[...], weight_ref[:, tile], preferred_element_type=F32
        )
    for copy in waits[near:]:
        copy.wait()


def late_kernel(
    through_ref, settled_ref, gate_ref, weight_ref, total_ref, state_ref, gain_ref,
    other_ref, mine_ref, gated_ref,
):
    chips, block = other_ref.shape[:2]
    gate_heads(through_ref, settled_ref, gate_ref, state_ref, gain_ref, gated_ref)
    for tile in tile_spans(weight_ref.shape[1]):
        product = total_ref[:, tile] + jnp.dot(
            gated_ref[...], weight_ref[:, tile], preferred_element_type=F32
        )
        for own, target in enumerate((other_ref, mine_ref)):
            for chip in range(chips):
                first = (own * chips + chip) * block
                target[chip, :, tile] = product[first : first + block].astype(BF16)


def in_hbm(*arrays):
    return [pltpu.with_memory_space_constraint(a, pltpu.HBM) for a in arrays]


def make_maps(operands, first, pairs, previous):
    rows, width = operands[0].shape
    heads = operands[4].shape[0]
    chunks = rows // CHUNK
    lanes = BATCH * HEAD_SIZE
    column = pl.BlockSpec((rows, lanes), lambda s, p: (0, p[0] + s))
    share = pairs * BATCH * chunks
    return pl.pallas_call(
        maps_kernel,
        grid_spec=pltpu.PrefetchScalarGridSpec(
            num_scalar_prefetch=1,
            grid=(pairs,),
            in_specs=[column] * 4
            + [pl.BlockSpec((heads, rows), lambda s, p: (0, 0))]
            + [pl.BlockSpec(memory_space=pltpu.HBM)] * len(previous),
            out_specs=[
                pl.BlockSpec((BATCH, HEAD_SIZE, 2 * HEAD_SIZE), lambda s, p: (s, 0, 0)),
                column,
                column,
            ],
        ),
        out_shape=[
            jax.ShapeDtypeStruct((BATCH * pairs, HEAD_SIZE, 2 * HEAD_SIZE), BF16),
            pltpu.HBM((rows, width), BF16),
            pltpu.HBM((rows, width), F32),
        ],
        input_output_aliases={6 + n: 1 + n for n in range(len(previous))},
        cost_estimate=pl.CostEstimate(
            flops=share * 120_000_000, bytes_accessed=share * 400_000, transcendentals=0
        ),
        compiler_params=pltpu.CompilerParams(vmem_limit_bytes=LIMIT << 20),
    )(first, *operands, *previous)


def project(places, through, settled, gates, states, gain, weight, groups):
    rows, width = through.shape
    model = weight.shape[1]
    chips = groups // 2
    block = rows // groups
    span = width // 2
    vmem = pl.BlockSpec(memory_space=pltpu.VMEM)
    hbm = pl.BlockSpec(memory_space=pltpu.HBM)
    keep, came = states
    gain = gain.reshape(1, HEAD_SIZE)
    pieces = [((rows, span), BF16), ((rows, span), F32), ((rows, span), BF16)]
    pieces.append(((span, model), BF16))
    grant = pltpu.CompilerParams(vmem_limit_bytes=LIMIT << 20)
    cost = pl.CostEstimate(
        flops=rows * width * model, bytes_accessed=2 * width * model, transcendentals=0
    )
    total, *rest = pl.pallas_call(
        functools.partial(early_kernel, chips),
        in_specs=[pl.BlockSpec(memory_space=pltpu.SMEM)] + [hbm] * 4 + [vmem] * 2,
        out_specs=[vmem] * 5,
        out_shape=[pltpu.VMEM((rows, model), F32)] + [pltpu.VMEM(*p) for p in pieces],
        scratch_shapes=[pltpu.VMEM(*p) for p in pieces]
        + [
            pltpu.VMEM((rows, span), BF16),
            pltpu.SemaphoreType.DMA((12 * chips + 2,)),
        ],
        cost_estimate=cost,
        compiler_params=grant,
        name="early",
    )(places, *in_hbm(through, settled, gates, weight), keep, gain)
    return pl.pallas_call(
        late_kernel,
        in_specs=[vmem] * 7,
        out_specs=[vmem] * 2,
        out_shape=[jax.ShapeDtypeStruct((chips, block, model), BF16)] * 2,
        scratch_shapes=[pltpu.VMEM((rows, span), BF16)],
        cost_estimate=cost,
        compiler_params=grant,
        name="late",
    )(*rest, total, came, gain)


def small_call(kernel, place, operands, shapes, scratch):
    def block(shape):
        return pl.BlockSpec(shape, lambda n, p: (0,) * len(shape))

    return pl.pallas_call(
        kernel,
        grid_spec=pltpu.PrefetchScalarGridSpec(
            num_scalar_prefetch=1,
            grid=(1,),
            in_specs=[block(a.shape) for a in operands],
            out_specs=[block(shape) for shape in shapes],
            scratch_shapes=[pltpu.VMEM(shape, BF16) for shape in scratch],
        ),
        out_shape=[jax.ShapeDtypeStruct(shape, BF16) for shape in shapes],
        compiler_params=pltpu.CompilerParams(vmem_limit_bytes=8 << 20),
    )(place, *operands)


def carry_apart(operands, place, axis):
    count = lax.axis_size(axis)
    heads = operands[4].shape[0]
    bits = [lax.rem(lax.div(place, 1 << n), 2) for n in range(3)]
    place_at = jnp.stack(bits).astype(jnp.int32)
    half, quarter = heads // 2, heads // 4
    batches = half // BATCH

    def swap(block, step):
        return lax.ppermute(block, axis, [(d, d ^ step) for d in range(count)])

    def first(group):
        return jnp.reshape(group * batches, (1,)).astype(jnp.int32)

    item, square = (HEAD_SIZE, 2 * HEAD_SIZE), (HEAD_SIZE, HEAD_SIZE)
    far = make_maps(operands, first(1 - bits[0]), batches, [])
    came = swap(far[0], 1)
    near = make_maps(operands, first(bits[0]), batches, far[1:])
    early, keep, send = small_call(
        functools.partial(join_kernel, 0),
        place_at,
        [near[0], came],
        [(half, *item), (quarter, *item), (quarter, *item)],
        [(half, *item)],
    )
    came = swap(send, 2)
    crest, send = small_call(
        functools.partial(crest_kernel, 1),
        place_at,
        [keep, came],
        [(quarter, *item), (quarter, *square)],
        [],
    )
    came = swap(send, 4)
    keep, send = small_call(
        functools.partial(turn_kernel, 1), place_at, [crest, came], [(quarter, *square)] * 2, []
    )
    came = swap(send, 2)
    keep, send = small_call(
        functools.partial(pass_kernel, 0),
        place_at,
        [early, keep, came],
        [(half, *square)] * 2,
        [(half, *square)],
    )
    return near[1:], [keep, swap(send, 1)], bits[0]


def carry_whole(operands, axis):
    heads = operands[4].shape[0]
    made = make_maps(operands, jnp.zeros((1,), jnp.int32), heads // BATCH, [])
    gathered = lax.all_gather(made[0], axis)

    def one(turn, state):
        item = lax.dynamic_index_in_dim(gathered, turn, 0, False).astype(F32)
        moved = jnp.einsum(
            "hij,hjk->hik", item[..., :HEAD_SIZE], state, precision=lax.Precision.HIGHEST
        )
        return moved + item[..., HEAD_SIZE:]

    zero = jnp.zeros((heads, HEAD_SIZE, HEAD_SIZE), F32)
    state = lax.fori_loop(0, lax.axis_index(axis), one, zero)
    return made[1:], jnp.split(state.astype(BF16), 2), 0


def on_device(
    query_vectors,
    key_vectors,
    value_vectors,
    log_decay,
    write_rate,
    out_gate,
    norm_gain,
    out_weight,
):
    heads = query_vectors.shape[1] // HEAD_SIZE
    operands = in_hbm(query_vectors, key_vectors, value_vectors, log_decay, write_rate.T)
    count = lax.axis_size("ctx")
    if count == 8 and heads == 8:
        reads, states, twist = carry_apart(operands, lax.axis_index("ctx"), "ctx")
    else:
        reads, states, twist = carry_whole(operands, "ctx")
    groups = lax.axis_size("head")
    place = lax.axis_index("head")
    core, chip = lax.rem(place, 2), lax.div(place, 2)
    chips = groups // 2

    places = jnp.stack([core, jnp.asarray(twist, core.dtype)]).astype(jnp.int32)
    other, mine = project(places, *reads, out_gate, states, norm_gain, out_weight, groups)
    came = lax.ppermute(other, "head", [(d, d ^ 1) for d in range(groups)])

    def both(block):
        return lax.dynamic_index_in_dim(mine, block, 0, False).astype(
            F32
        ) + lax.dynamic_index_in_dim(came, block, 0, False).astype(F32)

    total = both(chip)
    for turn in range(1, chips):
        away = both(lax.rem(chip + turn, chips)).astype(BF16)
        hops = [(d, (d + 2 * turn) % groups) for d in range(groups)]
        total = total + lax.ppermute(away, "head", hops).astype(F32)
    return total.astype(BF16)


def solution(mesh):
    in_specs = (
        P("ctx", "head"),
        P("ctx", "head"),
        P("ctx", "head"),
        P("ctx", "head"),
        P("ctx", "head"),
        P("ctx", "head"),
        P(),
        P("head", None),
    )
    out_specs = P(("ctx", "head"), None)

    return jax.shard_map(
        on_device, mesh=mesh, in_specs=in_specs, out_specs=out_specs, check_vma=False
    )
```

time: 64.3 us -> 57.3 us (0.89)
  Pallas kernels: 30.3 us -> 22 us
  waiting for transfers between devices: 19.6 us -> 21.8 us
  starting transfers between devices: 12.9 us -> 12 us
    pallas_call x4 -> x2, Pallas kernels: 16.8 us -> 5.8 us  [the longest x1 4.25 us: project(): pl.pallas_call(functools.partial(early_kernel, chips), in_specs=[pl.Block...]
    pallas_call x2, Pallas kernels: 10.6 us -> 13.2 us  [make_maps(): pl.pallas_call(maps_kernel, grid_spec=pltpu.PrefetchScalarGridSpec(num_sc...]
    ppermute x5, waiting for transfers between devices: 6.53 us -> 8.68 us  [swap(): return lax.ppermute(block, axis, [(d, d ^ step) for d in range(count)])]
    ppermute x5, starting transfers between devices: 11.2 us -> 10.3 us  [swap(): return lax.ppermute(block, axis, [(d, d ^ step) for d in range(count)])]
  transfers between devices with their start and end apart: 7 -> 7, of which waited for: 6 -> 5; matrix products, arithmetic and copies ran while one was open for 0% -> 0% of each run, Pallas kernels for 25% -> 19%
where the time goes in v5:
time: 57.3 us; the launch traced here: 57 us
  Pallas kernels  22 us (38%)
  waiting for transfers between devices  21.8 us (38%)
  starting transfers between devices  12 us (21%)
  other arithmetic  1.19 us (2%)
    pallas_call x2, Pallas kernels, make_maps(): pl.pallas_call(maps_kernel, grid_spec=pltpu.PrefetchScalarGridSpec(num_sc...  13.2 us
    ppermute x1, waiting for transfers between devices, on_device(): total = total + lax.ppermute(away, 'head', hops).astype(F32)  10.7 us
    ppermute x5, starting transfers between devices, swap(): return lax.ppermute(block, axis, [(d, d ^ step) for d in range(count)])  10.3 us
    ppermute x5, waiting for transfers between devices, swap(): return lax.ppermute(block, axis, [(d, d ^ step) for d in range(count)])  8.68 us
    pallas_call x1, Pallas kernels, project(): pl.pallas_call(functools.partial(early_kernel, chips), in_specs=[pl.Block...  4.25 us
    pallas_call x4, Pallas kernels, small_call(): pl.pallas_call(kernel, grid_spec=pltpu.PrefetchScalarGridSpec(num_scalar_...  2.94 us
    ppermute x1, waiting for transfers between devices, on_device(): came = lax.ppermute(other, 'head', [(d, d ^ 1) for d in range(groups)])  2.4 us
    ppermute x1, starting transfers between devices, on_device(): total = total + lax.ppermute(away, 'head', hops).astype(F32)  1.58 us
  transfers between devices with their start and end apart: 7, of which 5 were waited for; matrix products, arithmetic and copies ran while one was open for 0% of the time, Pallas kernels for 19%

profile of v5, /device:TPU:0, one launch (start us, length us, event | category | flops | bytes accessed | tf_op | source)
XLA Modules:
  0.0 57.0 jit_solution(4293668416033115740)
XLA Ops:
  0.0 6.6 %shard_map.82 = (bf16[4,128,256]{2,1,0:T(8,128)(2,1)S(1)}, bf16[384,1024]{1,0:T(8,128)(2,1)}, f32[384,1024]{1,0:T(8,128)}) custom-call(s32[1]{0:T(128)} %bitcast.3.first_ref, bf16[384,1024]{1,0:T(8,128)(2,1)} %query_ref.3, bf16[384,1024]{1,0:T(8,128)(2,1)} %key_ref.3, bf16[384,1024]{1,0:T(8,128)(2,1)} %value_ref.3, f32[384,1024]{1,0:T(8,128)} %decay_ref.3, ...), custom_call_target="tpu_custom_call" | custom-call | flops 1440000000 | bytes 4800000 | tf_op jit(solution)/shard_map/pallas_call | solution.py:272
  6.6 3.0 %collective-permute-start = (bf16[4,128,256]{2,1,0:T(8,128)(2,1)S(1)}, bf16[4,128,256]{2,1,0:T(8,128)(2,1)S(1)}, u32[]{:S(2)}, u32[]{:S(2)}) collective-permute-start(bf16[4,128,256]{2,1,0:T(8,128)(2,1)S(1)} %get-tuple-element.32), channel_id=1, source_target_pairs={{0,4},{4,0},{8,12},{12,8},{16,20},{20,16},{24,28},{28,24},{1,5},{5... | collective-permute-start | bytes 786440 | tf_op jit(solution)/shard_map/ppermute | solution.py:368
  9.6 0.1 pad_add_fusion.1.place_ref
  9.7 0.0 copy-start
  9.7 6.6 %shard_map.83 = (bf16[4,128,256]{2,1,0:T(8,128)(2,1)S(1)}, bf16[384,1024]{1,0:T(8,128)(2,1)}, f32[384,1024]{1,0:T(8,128)}) custom-call(s32[1]{0:T(128)} %bitcast.1.first_ref, bf16[384,1024]{1,0:T(8,128)(2,1)} %query_ref.3, bf16[384,1024]{1,0:T(8,128)(2,1)} %key_ref.3, bf16[384,1024]{1,0:T(8,128)(2,1)} %value_ref.3, ...), custom_call_target="tpu_custom_call", output_to_operand_aliasing={{1}: (6, {}), {2}: (7, {})} | custom-call | flops 1440000000 | bytes 4800000 | tf_op jit(solution)/shard_map/pallas_call | solution.py:272
  16.3 0.0 collective-permute-done.came_ref
  16.3 0.8 %shard_map.84 = (bf16[4,128,256]{2,1,0:T(8,128)(2,1)S(1)}, bf16[2,128,256]{2,1,0:T(8,128)(2,1)S(1)}, bf16[2,128,256]{2,1,0:T(8,128)(2,1)S(1)}) custom-call(s32[3]{0:T(128)S(1)} %pad_add_fusion.1.place_ref, bf16[4,128,256]{2,1,0:T(8,128)(2,1)S(1)} %get-tuple-element.31.own_ref, bf16[4,128,256]{2,1,0:T(8,128)(2,1)S(1)} %collective-permute-done.came_ref), custom_call_target="tpu_custom_call" | custom-call | tf_op jit(solution)/shard_map/pallas_call | solution.py:345
  17.1 1.6 %collective-permute-start.1 = (bf16[2,128,256]{2,1,0:T(8,128)(2,1)S(1)}, bf16[2,128,256]{2,1,0:T(8,128)(2,1)S(1)}, u32[]{:S(2)}, u32[]{:S(2)}) collective-permute-start(bf16[2,128,256]{2,1,0:T(8,128)(2,1)S(1)} %get-tuple-element.35), channel_id=1, source_target_pairs={{0,8},{4,12},{8,0},{12,4},{16,24},{20,28},{24,16},{28,20},{1,9},{5... | collective-permute-start | bytes 393224 | tf_op jit(solution)/shard_map/ppermute | solution.py:368
  18.8 3.4 %collective-permute-done.1.came_ref = bf16[2,128,256]{2,1,0:T(8,128)(2,1)S(1)} collective-permute-done((bf16[2,128,256]{2,1,0:T(8,128)(2,1)S(1)}, bf16[2,128,256]{2,1,0:T(8,128)(2,1)S(1)}, u32[]{:S(2)}, u32[]{:S(2)}) %collective-permute-start.1) | collective-permute-done | bytes 131104 | tf_op jit(solution)/shard_map/ppermute | solution.py:368
  22.1 0.7 %shard_map.85 = (bf16[2,128,256]{2,1,0:T(8,128)(2,1)S(1)}, bf16[2,128,128]{2,1,0:T(8,128)(2,1)S(1)}) custom-call(s32[3]{0:T(128)S(1)} %pad_add_fusion.1.place_ref, bf16[2,128,256]{2,1,0:T(8,128)(2,1)S(1)} %get-tuple-element.34.own_ref, bf16[2,128,256]{2,1,0:T(8,128)(2,1)S(1)} %collective-permute-done.1.came_ref), custom_call_target="tpu_custom_call" | custom-call | tf_op jit(solution)/shard_map/pallas_call | solution.py:345
  22.8 2.6 %collective-permute-start.2 = (bf16[2,128,128]{2,1,0:T(8,128)(2,1)S(1)}, bf16[2,128,128]{2,1,0:T(8,128)(2,1)S(1)}, u32[]{:S(2)}, u32[]{:S(2)}) collective-permute-start(bf16[2,128,128]{2,1,0:T(8,128)(2,1)S(1)} %get-tuple-element.37), channel_id=1, source_target_pairs={{0,16},{4,20},{8,24},{12,28},{16,0},{20,4},{24,8},{28,12},{1,17},{... | collective-permute-start | bytes 196616 | tf_op jit(solution)/shard_map/ppermute | solution.py:368
  25.5 2.6 %collective-permute-done.2.came_ref = bf16[2,128,128]{2,1,0:T(8,128)(2,1)S(1)} collective-permute-done((bf16[2,128,128]{2,1,0:T(8,128)(2,1)S(1)}, bf16[2,128,128]{2,1,0:T(8,128)(2,1)S(1)}, u32[]{:S(2)}, u32[]{:S(2)}) %collective-permute-start.2) | collective-permute-done | bytes 65568 | tf_op jit(solution)/shard_map/ppermute | solution.py:368
  28.1 0.7 %shard_map.86 = (bf16[2,128,128]{2,1,0:T(8,128)(2,1)S(1)}, bf16[2,128,128]{2,1,0:T(8,128)(2,1)S(1)}) custom-call(s32[3]{0:T(128)S(1)} %pad_add_fusion.1.place_ref, bf16[2,128,256]{2,1,0:T(8,128)(2,1)S(1)} %get-tuple-element.36.early_ref, bf16[2,128,128]{2,1,0:T(8,128)(2,1)S(1)} %collective-permute-done.2.came_ref), custom_call_target="tpu_custom_call" | custom-call | tf_op jit(solution)/shard_map/pallas_call | solution.py:345
  28.8 1.6 %collective-permute-start.3 = (bf16[2,128,128]{2,1,0:T(8,128)(2,1)S(1)}, bf16[2,128,128]{2,1,0:T(8,128)(2,1)S(1)}, u32[]{:S(2)}, u32[]{:S(2)}) collective-permute-start(bf16[2,128,128]{2,1,0:T(8,128)(2,1)S(1)} %get-tuple-element.39), channel_id=1, source_target_pairs={{0,8},{4,12},{8,0},{12,4},{16,24},{20,28},{24,16},{28,20},{1,9},{5... | collective-permute-start | bytes 196616 | tf_op jit(solution)/shard_map/ppermute | solution.py:368
  30.4 2.7 %collective-permute-done.3.came_ref = bf16[2,128,128]{2,1,0:T(8,128)(2,1)S(1)} collective-permute-done((bf16[2,128,128]{2,1,0:T(8,128)(2,1)S(1)}, bf16[2,128,128]{2,1,0:T(8,128)(2,1)S(1)}, u32[]{:S(2)}, u32[]{:S(2)}) %collective-permute-start.3) | collective-permute-done | bytes 65568 | tf_op jit(solution)/shard_map/ppermute | solution.py:368
  33.1 0.7 %shard_map.87 = (bf16[4,128,128]{2,1,0:T(8,128)(2,1)S(1)}, bf16[4,128,128]{2,1,0:T(8,128)(2,1)S(1)}) custom-call(s32[3]{0:T(128)S(1)} %pad_add_fusion.1.place_ref, bf16[4,128,256]{2,1,0:T(8,128)(2,1)S(1)} %get-tuple-element.33.early_ref, bf16[2,128,128]{2,1,0:T(8,128)(2,1)S(1)} %get-tuple-element.38.own_ref, ...), custom_call_target="tpu_custom_call" | custom-call | tf_op jit(solution)/shard_map/pallas_call | solution.py:345
  33.9 1.4 %collective-permute-start.4 = (bf16[4,128,128]{2,1,0:T(8,128)(2,1)S(1)}, bf16[4,128,128]{2,1,0:T(8,128)(2,1)S(1)}, u32[]{:S(2)}, u32[]{:S(2)}) collective-permute-start(bf16[4,128,128]{2,1,0:T(8,128)(2,1)S(1)} %get-tuple-element.46), channel_id=1, source_target_pairs={{0,4},{4,0},{8,12},{12,8},{16,20},{20,16},{24,28},{28,24},{1,5},{5... | collective-permute-start | bytes 393224 | tf_op jit(solution)/shard_map/ppermute | solution.py:368
  35.3 0.1 pad_add_fusion.place_ref
  35.3 0.0 copy-done
  35.3 4.2 %early.1 = (f32[384,2304]{1,0:T(8,128)S(1)}, bf16[384,512]{1,0:T(8,128)(2,1)S(1)}, f32[384,512]{1,0:T(8,128)S(1)}, bf16[384,512]{1,0:T(8,128)(2,1)S(1)}, bf16[512,2304]{1,0:T(8,128)(2,1)S(1)}) custom-call(s32[2]{0:T(128)S(1)} %pad_add_fusion.place_ref, bf16[384,1024]{1,0:T(8,128)(2,1)} %get-tuple-element.29.through_hbm, ...), custom_call_target="tpu_custom_call" | custom-call | flops 905969664 | bytes 4718592 | tf_op jit(solution)/shard_map/early/pallas_call | solution.py:315
  39.6 0.0 collective-permute-done.4.state_ref
  39.6 1.5 %late.1 = (bf16[2,96,2304]{2,1,0:T(8,128)(2,1)S(1)}, bf16[2,96,2304]{2,1,0:T(8,128)(2,1)S(1)}) custom-call(bf16[384,512]{1,0:T(8,128)(2,1)S(1)} %get-tuple-element.41.through_ref, f32[384,512]{1,0:T(8,128)S(1)} %get-tuple-element.42.settled_ref, bf16[384,512]{1,0:T(8,128)(2,1)S(1)} %get-tuple-element.43.gate_ref, ...), custom_call_target="tpu_custom_call" | custom-call | flops 905969664 | bytes 4718592 | tf_op jit(solution)/shard_map/late/pallas_call | solution.py:329
  41.2 0.1 collective-permute-start.5
  41.3 2.4 %collective-permute-done.5 = bf16[2,96,2304]{2,1,0:T(8,128)(2,1)S(1)} collective-permute-done((bf16[2,96,2304]{2,1,0:T(8,128)(2,1)S(1)}, bf16[2,96,2304]{2,1,0:T(8,128)(2,1)S(1)}, u32[]{:S(2)}, u32[]{:S(2)}) %collective-permute-start.5) | collective-permute-done | bytes 884768 | tf_op jit(solution)/shard_map/ppermute | solution.py:448
  43.7 0.1 fusion.1
  43.8 1.6 %collective-permute-start.6 = (bf16[96,2304]{1,0:T(8,128)(2,1)S(1)}, bf16[96,2304]{1,0:T(8,128)(2,1)S(1)}, u32[]{:S(2)}, u32[]{:S(2)}) collective-permute-start(bf16[96,2304]{1,0:T(8,128)(2,1)S(1)} %fusion.1), channel_id=1, source_target_pairs={{0,2},{1,3},{2,0},{3,1},{4,6},{5,7},{6,4},{7,5},{8,10},{9,11},{10,... | collective-permute-start | bytes 1327112 | tf_op jit(solution)/shard_map/ppermute | solution.py:459
  45.4 10.7 %collective-permute-done.6 = bf16[96,2304]{1,0:T(8,128)(2,1)S(1)} collective-permute-done((bf16[96,2304]{1,0:T(8,128)(2,1)S(1)}, bf16[96,2304]{1,0:T(8,128)(2,1)S(1)}, u32[]{:S(2)}, u32[]{:S(2)}) %collective-permute-start.6) | collective-permute-done | bytes 442400 | tf_op jit(solution)/shard_map/ppermute | solution.py:459
  56.1 0.9 %fusion = bf16[96,2304]{1,0:T(8,128)(2,1)} fusion(bf16[96,2304]{1,0:T(8,128)(2,1)S(1)} %collective-permute-done.6, bf16[2,96,2304]{2,1,0:T(8,128)(2,1)S(1)} %collective-permute-done.5, s32[]{:T(128)S(6)} %select_n.9, bf16[2,96,2304]{2,1,0:T(8,128)(2,1)S(1)} %get-tuple-element.47), kind=kLoop, calls=%fused_computation.1 | loop fusion | flops 1327104 | bytes 1769476 | tf_op jit(solution)/shard_map/convert_element_type | solution.py:460
Async XLA Ops:
  6.6 9.7 %collective-permute-start = (bf16[4,128,256]{2,1,0:T(8,128)(2,1)S(1)}, bf16[4,128,256]{2,1,0:T(8,128)(2,1)S(1)}, u32[]{:S(2)}, u32[]{:S(2)}) collective-permute-start(bf16[4,128,256]{2,1,0:T(8,128)(2,1)S(1)} %get-tuple-element.32), channel_id=1, source_target_pairs={{0,4},{4,0},{8,12},{12,8},{16,20},{20,16},{24,28},{28,24},{1,5},{5... | collective-permute-start | bytes 786440 | tf_op jit(solution)/shard_map/ppermute | solution.py:368
  9.7 25.7 %copy-start = (f32[128]{0:T(128)S(1)}, f32[128]{0:T(128)}, u32[]{:S(2)}) copy-start(f32[128]{0:T(128)} %param.14) | copy-start | bytes 1540
  17.1 5.0 %collective-permute-start.1 = (bf16[2,128,256]{2,1,0:T(8,128)(2,1)S(1)}, bf16[2,128,256]{2,1,0:T(8,128)(2,1)S(1)}, u32[]{:S(2)}, u32[]{:S(2)}) collective-permute-start(bf16[2,128,256]{2,1,0:T(8,128)(2,1)S(1)} %get-tuple-element.35), channel_id=1, source_target_pairs={{0,8},{4,12},{8,0},{12,4},{16,24},{20,28},{24,16},{28,20},{1,9},{5... | collective-permute-start | bytes 393224 | tf_op jit(solution)/shard_map/ppermute | solution.py:368
  22.8 5.2 %collective-permute-start.2 = (bf16[2,128,128]{2,1,0:T(8,128)(2,1)S(1)}, bf16[2,128,128]{2,1,0:T(8,128)(2,1)S(1)}, u32[]{:S(2)}, u32[]{:S(2)}) collective-permute-start(bf16[2,128,128]{2,1,0:T(8,128)(2,1)S(1)} %get-tuple-element.37), channel_id=1, source_target_pairs={{0,16},{4,20},{8,24},{12,28},{16,0},{20,4},{24,8},{28,12},{1,17},{... | collective-permute-start | bytes 196616 | tf_op jit(solution)/shard_map/ppermute | solution.py:368
  28.8 4.3 %collective-permute-start.3 = (bf16[2,128,128]{2,1,0:T(8,128)(2,1)S(1)}, bf16[2,128,128]{2,1,0:T(8,128)(2,1)S(1)}, u32[]{:S(2)}, u32[]{:S(2)}) collective-permute-start(bf16[2,128,128]{2,1,0:T(8,128)(2,1)S(1)} %get-tuple-element.39), channel_id=1, source_target_pairs={{0,8},{4,12},{8,0},{12,4},{16,24},{20,28},{24,16},{28,20},{1,9},{5... | collective-permute-start | bytes 196616 | tf_op jit(solution)/shard_map/ppermute | solution.py:368
  33.9 5.7 %collective-permute-start.4 = (bf16[4,128,128]{2,1,0:T(8,128)(2,1)S(1)}, bf16[4,128,128]{2,1,0:T(8,128)(2,1)S(1)}, u32[]{:S(2)}, u32[]{:S(2)}) collective-permute-start(bf16[4,128,128]{2,1,0:T(8,128)(2,1)S(1)} %get-tuple-element.46), channel_id=1, source_target_pairs={{0,4},{4,0},{8,12},{12,8},{16,20},{20,16},{24,28},{28,24},{1,5},{5... | collective-permute-start | bytes 393224 | tf_op jit(solution)/shard_map/ppermute | solution.py:368
  41.2 2.5 %collective-permute-start.5 = (bf16[2,96,2304]{2,1,0:T(8,128)(2,1)S(1)}, bf16[2,96,2304]{2,1,0:T(8,128)(2,1)S(1)}, u32[]{:S(2)}, u32[]{:S(2)}) collective-permute-start(bf16[2,96,2304]{2,1,0:T(8,128)(2,1)S(1)} %get-tuple-element.48), channel_id=1, source_target_pairs={{0,1},{1,0},{2,3},{3,2},{4,5},{5,4},{6,7},{7,6},{8,9},{9,8},{10,11... | collective-permute-start | bytes 2654216 | tf_op jit(solution)/shard_map/ppermute | solution.py:448
  43.8 12.3 %collective-permute-start.6 = (bf16[96,2304]{1,0:T(8,128)(2,1)S(1)}, bf16[96,2304]{1,0:T(8,128)(2,1)S(1)}, u32[]{:S(2)}, u32[]{:S(2)}) collective-permute-start(bf16[96,2304]{1,0:T(8,128)(2,1)S(1)} %fusion.1), channel_id=1, source_target_pairs={{0,2},{1,3},{2,0},{3,1},{4,6},{5,7},{6,4},{7,5},{8,10},{9,11},{10,... | collective-permute-start | bytes 1327112 | tf_op jit(solution)/shard_map/ppermute | solution.py:459

commit v6 on v5

--- a/solution.py
+++ b/solution.py
@@ -200,14 +200,15 @@
     return [slice(n, n + tile) for n in range(0, model, tile)]
 
 
-def early_kernel(
-    chips, place_ref, through_hbm, settled_hbm, gate_hbm, weight_hbm, state_ref, gain_ref,
-    total_ref, through_rest, settled_rest, gate_rest, weight_rest,
-    through_ref, settled_ref, gate_ref, weight_ref, gated_ref, sems,
-):
+def part_spans(model):
+    tiles = tile_spans(model)
+    return [tiles[:1], tiles[1:]] if len(tiles) > 1 else [tiles]
+
+
+def load_kernel(chips, place_ref, *refs):
+    count = (len(refs) - 1) // 3
+    sources, targets, sems = refs[:count], refs[count:-1], refs[-1]
     core, side = place_ref[0], place_ref[1]
-    rows, span = through_ref.shape
-    block = rows // (2 * chips)
     waits = []
 
     def load(source, target):
@@ -215,47 +216,56 @@
         copy.start()
         waits.append(copy)
 
-    def load_group(group, targets, weight_target):
-        columns = pl.ds(pl.multiple_of(group * span, span), span)
-        for source, target in zip((through_hbm, settled_hbm, gate_hbm), targets):
-            for own in range(2):
-                for chip in range(chips):
-                    first = (2 * chip + (core if own else 1 - core)) * block
-                    load(
-                        source.at[pl.ds(pl.multiple_of(first, block), block), columns],
-                        target.at[pl.ds((own * chips + chip) * block, block)],
-                    )
-        load(weight_hbm.at[columns], weight_target)
-
-    load_group(side, (through_ref, settled_ref, gate_ref), weight_ref)
-    near = len(waits)
-    load_group(1 - side, (through_rest, settled_rest, gate_rest), weight_rest)
-    for copy in waits[: near - 1]:
+    for n, source in enumerate(sources):
+        for rest in range(2):
+            target = targets[2 * n + rest]
+            group = 1 - side if rest else side
+            if source.shape[1] == 2 * target.shape[1]:
+                span = target.shape[1]
+                columns = pl.ds(pl.multiple_of(group * span, span), span)
+                block = source.shape[0] // (2 * chips)
+                for own in range(2):
+                    for chip in range(chips):
+                        first = (2 * chip + (core if own else 1 - core)) * block
+                        load(
+                            source.at[pl.ds(pl.multiple_of(first, block), block), columns],
+                            target.at[pl.ds((own * chips + chip) * block, block)],
+                        )
+            else:
+                span = target.shape[0]
+                load(source.at[pl.ds(pl.multiple_of(group * span, span), span)], target)
+    for copy in waits:
         copy.wait()
+
+
+def early_kernel(
+    through_ref, settled_ref, gate_ref, weight_ref, state_ref, gain_ref, total_ref, gated_ref
+):
     gate_heads(through_ref, settled_ref, gate_ref, state_ref, gain_ref, gated_ref)
-    waits[near - 1].wait()
     for tile in tile_spans(weight_ref.shape[1]):
         total_ref[:, tile] = jnp.dot(
             gated_ref[...], weight_ref[:, tile], preferred_element_type=F32
         )
-    for copy in waits[near:]:
-        copy.wait()
 
 
 def late_kernel(
-    through_ref, settled_ref, gate_ref, weight_ref, total_ref, state_ref, gain_ref,
-    other_ref, mine_ref, gated_ref,
+    through_ref, settled_ref, gate_ref, weight_ref, total_ref, state_ref, gain_ref, *refs
 ):
-    chips, block = other_ref.shape[:2]
+    targets, gated_ref = refs[:-1], refs[-1]
+    chips, block = targets[0].shape[:2]
     gate_heads(through_ref, settled_ref, gate_ref, state_ref, gain_ref, gated_ref)
-    for tile in tile_spans(weight_ref.shape[1]):
-        product = total_ref[:, tile] + jnp.dot(
-            gated_ref[...], weight_ref[:, tile], preferred_element_type=F32
-        )
-        for own, target in enumerate((other_ref, mine_ref)):
-            for chip in range(chips):
-                first = (own * chips + chip) * block
-                target[chip, :, tile] = product[first : first + block].astype(BF16)
+    for n, tiles in enumerate(part_spans(weight_ref.shape[1])):
+        for tile in tiles:
+            product = total_ref[:, tile] + jnp.dot(
+                gated_ref[...], weight_ref[:, tile], preferred_element_type=F32
+            )
+            columns = slice(tile.start - tiles[0].start, tile.stop - tiles[0].start)
+            for own in range(2):
+                for chip in range(chips):
+                    first = (own * chips + chip) * block
+                    targets[2 * n + own][chip, :, columns] = product[
+                        first : first + block
+                    ].astype(BF16)
 
 
 def in_hbm(*arrays):
@@ -296,46 +306,62 @@
     )(first, *operands, *previous)
 
 
-def project(places, through, settled, gates, states, gain, weight, groups):
-    rows, width = through.shape
-    model = weight.shape[1]
+def load_halves(places, arrays, groups):
+    chips = groups // 2
+    hbm = pl.BlockSpec(memory_space=pltpu.HBM)
+    shapes, copies = [], 0
+    for array, by_rows in arrays:
+        rows, width = array.shape
+        shape = (rows // 2, width) if by_rows else (rows, width // 2)
+        shapes += [pltpu.VMEM(shape, array.dtype)] * 2
+        copies += 2 if by_rows else 4 * chips
+    return pl.pallas_call(
+        functools.partial(load_kernel, chips),
+        in_specs=[pl.BlockSpec(memory_space=pltpu.SMEM)] + [hbm] * len(arrays),
+        out_specs=[pl.BlockSpec(memory_space=pltpu.VMEM)] * len(shapes),
+        out_shape=shapes,
+        scratch_shapes=[pltpu.SemaphoreType.DMA((copies,))],
+        cost_estimate=pl.CostEstimate(
+            flops=0, bytes_accessed=10_000_000, transcendentals=0
+        ),
+        compiler_params=pltpu.CompilerParams(vmem_limit_bytes=LIMIT << 20),
+    )(places, *in_hbm(*(array for array, _ in arrays)))
+
+
+def project(through, settled, gates, weights, states, gain, groups):
+    rows, span = through[0].shape
+    model = weights[0].shape[1]
     chips = groups // 2
     block = rows // groups
-    span = width // 2
     vmem = pl.BlockSpec(memory_space=pltpu.VMEM)
-    hbm = pl.BlockSpec(memory_space=pltpu.HBM)
     keep, came = states
     gain = gain.reshape(1, HEAD_SIZE)
-    pieces = [((rows, span), BF16), ((rows, span), F32), ((rows, span), BF16)]
-    pieces.append(((span, model), BF16))
     grant = pltpu.CompilerParams(vmem_limit_bytes=LIMIT << 20)
     cost = pl.CostEstimate(
-        flops=rows * width * model, bytes_accessed=2 * width * model, transcendentals=0
-    )
-    total, *rest = pl.pallas_call(
-        functools.partial(early_kernel, chips),
-        in_specs=[pl.BlockSpec(memory_space=pltpu.SMEM)] + [hbm] * 4 + [vmem] * 2,
-        out_specs=[vmem] * 5,
-        out_shape=[pltpu.VMEM((rows, model), F32)] + [pltpu.VMEM(*p) for p in pieces],
-        scratch_shapes=[pltpu.VMEM(*p) for p in pieces]
-        + [
-            pltpu.VMEM((rows, span), BF16),
-            pltpu.SemaphoreType.DMA((12 * chips + 2,)),
-        ],
+        flops=2 * rows * span * model, bytes_accessed=2 * span * model, transcendentals=0
+    )
+    total = pl.pallas_call(
+        early_kernel,
+        in_specs=[vmem] * 6,
+        out_specs=vmem,
+        out_shape=pltpu.VMEM((rows, model), F32),
+        scratch_shapes=[pltpu.VMEM((rows, span), BF16)],
         cost_estimate=cost,
         compiler_params=grant,
         name="early",
-    )(places, *in_hbm(through, settled, gates, weight), keep, gain)
-    return pl.pallas_call(
+    )(through[0], settled[0], gates[0], weights[0], keep, gain)
+    widths = [tiles[-1].stop - tiles[0].start for tiles in part_spans(model)]
+    shares = pl.pallas_call(
         late_kernel,
         in_specs=[vmem] * 7,
-        out_specs=[vmem] * 2,
-        out_shape=[jax.ShapeDtypeStruct((chips, block, model), BF16)] * 2,
+        out_specs=[vmem] * (2 * len(widths)),
+        out_shape=[jax.ShapeDtypeStruct((chips, block, w), BF16) for w in widths for _ in range(2)],
         scratch_shapes=[pltpu.VMEM((rows, span), BF16)],
         cost_estimate=cost,
         compiler_params=grant,
         name="late",
-    )(*rest, total, came, gain)
+    )(through[1], settled[1], gates[1], weights[1], total, came, gain)
+    return list(zip(shares[::2], shares[1::2]))
 
 
 def small_call(kernel, place, operands, shapes, scratch):
@@ -419,6 +445,23 @@
     zero = jnp.zeros((heads, HEAD_SIZE, HEAD_SIZE), F32)
     state = lax.fori_loop(0, lax.axis_index(axis), one, zero)
     return made[1:], jnp.split(state.astype(BF16), 2), 0
+
+
+def sum_heads(other, mine, chip, groups):
+    chips = groups // 2
+    came = lax.ppermute(other, "head", [(d, d ^ 1) for d in range(groups)])
+
+    def both(block):
+        return lax.dynamic_index_in_dim(mine, block, 0, False).astype(
+            F32
+        ) + lax.dynamic_index_in_dim(came, block, 0, False).astype(F32)
+
+    total = both(chip)
+    for turn in range(1, chips):
+        away = both(lax.rem(chip + turn, chips)).astype(BF16)
+        hops = [(d, (d + 2 * turn) % groups) for d in range(groups)]
+        total = total + lax.ppermute(away, "head", hops).astype(F32)
+    return total.astype(BF16)
 
 
 def on_device(
@@ -441,23 +484,14 @@
     groups = lax.axis_size("head")
     place = lax.axis_index("head")
     core, chip = lax.rem(place, 2), lax.div(place, 2)
-    chips = groups // 2
 
     places = jnp.stack([core, jnp.asarray(twist, core.dtype)]).astype(jnp.int32)
-    other, mine = project(places, *reads, out_gate, states, norm_gain, out_weight, groups)
-    came = lax.ppermute(other, "head", [(d, d ^ 1) for d in range(groups)])
-
-    def both(block):
-        return lax.dynamic_index_in_dim(mine, block, 0, False).astype(
-            F32
-        ) + lax.dynamic_index_in_dim(came, block, 0, False).astype(F32)
-
-    total = both(chip)
-    for turn in range(1, chips):
-        away = both(lax.rem(chip + turn, chips)).astype(BF16)
-        hops = [(d, (d + 2 * turn) % groups) for d in range(groups)]
-        total = total + lax.ppermute(away, "head", hops).astype(F32)
-    return total.astype(BF16)
+    loaded = load_halves(places, [(out_weight, True), (out_gate, False)], groups)
+    weights, gates = loaded[:2], loaded[2:]
+    loaded = load_halves(places, [(reads[0], False), (reads[1], False)], groups)
+    shares = project(loaded[:2], loaded[2:], gates, weights, states, norm_gain, groups)
+    sums = [sum_heads(*share, chip, groups) for share in shares]
+    return jnp.concatenate(sums, axis=1)
 
 
 def solution(mesh):

time: 57.3 us -> 59.9 us (1.045)
  Pallas kernels: 22 us -> 24.6 us
  waiting for transfers between devices: 21.8 us -> 20.6 us
  starting transfers between devices: 12 us -> 13.1 us
    pallas_call x2 -> x4, Pallas kernels: 5.8 us -> 8.54 us  [the longest x2 5.53 us: load_halves(): pl.pallas_call(functools.partial(load_kernel, chips), in_specs=[pl.BlockS...]
    ppermute x2 -> x4, waiting for transfers between devices: 13.1 us -> 11.9 us  [the longest x2 9.98 us: sum_heads(): total = total + lax.ppermute(away, 'head', hops).astype(F32)]
    ppermute x2 -> x4, starting transfers between devices: 1.65 us -> 2.72 us  [the longest x2 2.16 us: sum_heads(): total = total + lax.ppermute(away, 'head', hops).astype(F32)]
    concatenate x0 -> x1, other arithmetic: none -> 0.79 us  [on_device(): return jnp.concatenate(sums, axis=1)]
    convert_element_type x2 -> x4, other arithmetic: 1.04 us -> 0.28 us  [the longest x2 0.17 us: sum_heads(): return total.astype(BF16)]
  transfers between devices with their start and end apart: 7 -> 9, of which waited for: 5 -> 6; matrix products, arithmetic and copies ran while one was open for 0% -> 1% of each run, Pallas kernels for 19% -> 23%
where the time goes in v6:
time: 59.9 us; the launch traced here: 59.6 us
  Pallas kernels  24.6 us (41%)
  waiting for transfers between devices  20.6 us (34%)
  starting transfers between devices  13.1 us (22%)
  other arithmetic  1.22 us (2%)
    pallas_call x2, Pallas kernels, make_maps(): pl.pallas_call(maps_kernel, grid_spec=pltpu.PrefetchScalarGridSpec(num_sc...  13.2 us
    ppermute x5, starting transfers between devices, swap(): return lax.ppermute(block, axis, [(d, d ^ step) for d in range(count)])  10.3 us
    ppermute x2, waiting for transfers between devices, sum_heads(): total = total + lax.ppermute(away, 'head', hops).astype(F32)  9.98 us
    ppermute x5, waiting for transfers between devices, swap(): return lax.ppermute(block, axis, [(d, d ^ step) for d in range(count)])  8.68 us
    pallas_call x2, Pallas kernels, load_halves(): pl.pallas_call(functools.partial(load_kernel, chips), in_specs=[pl.BlockS...  5.53 us
    pallas_call x4, Pallas kernels, small_call(): pl.pallas_call(kernel, grid_spec=pltpu.PrefetchScalarGridSpec(num_scalar_...  2.94 us
    ppermute x2, starting transfers between devices, sum_heads(): total = total + lax.ppermute(away, 'head', hops).astype(F32)  2.16 us
    ppermute x2, waiting for transfers between devices, sum_heads(): came = lax.ppermute(other, 'head', [(d, d ^ 1) for d in range(groups)])  1.92 us
  transfers between devices with their start and end apart: 9, of which 6 were waited for; matrix products, arithmetic and copies ran while one was open for 1% of the time, Pallas kernels for 23%

profile of v6, /device:TPU:0, one launch (start us, length us, event | category | flops | bytes accessed | tf_op | source)
XLA Modules:
  0.0 59.6 jit_solution(14307317282787654575)
XLA Ops:
  0.0 6.6 %shard_map.82 = (bf16[4,128,256]{2,1,0:T(8,128)(2,1)S(1)}, bf16[384,1024]{1,0:T(8,128)(2,1)}, f32[384,1024]{1,0:T(8,128)}) custom-call(s32[1]{0:T(128)} %bitcast.3.first_ref, bf16[384,1024]{1,0:T(8,128)(2,1)} %query_ref.3, bf16[384,1024]{1,0:T(8,128)(2,1)} %key_ref.3, bf16[384,1024]{1,0:T(8,128)(2,1)} %value_ref.3, f32[384,1024]{1,0:T(8,128)} %decay_ref.3, ...), custom_call_target="tpu_custom_call" | custom-call | flops 1440000000 | bytes 4800000 | tf_op jit(solution)/shard_map/pallas_call | solution.py:282
  6.6 3.0 %collective-permute-start = (bf16[4,128,256]{2,1,0:T(8,128)(2,1)S(1)}, bf16[4,128,256]{2,1,0:T(8,128)(2,1)S(1)}, u32[]{:S(2)}, u32[]{:S(2)}) collective-permute-start(bf16[4,128,256]{2,1,0:T(8,128)(2,1)S(1)} %get-tuple-element.45), channel_id=1, source_target_pairs={{0,4},{4,0},{8,12},{12,8},{16,20},{20,16},{24,28},{28,24},{1,5},{5... | collective-permute-start | bytes 786440 | tf_op jit(solution)/shard_map/ppermute | solution.py:394
  9.6 0.1 pad_add_fusion.1.place_ref
  9.6 6.6 %shard_map.83 = (bf16[4,128,256]{2,1,0:T(8,128)(2,1)S(1)}, bf16[384,1024]{1,0:T(8,128)(2,1)}, f32[384,1024]{1,0:T(8,128)}) custom-call(s32[1]{0:T(128)} %bitcast.1.first_ref, bf16[384,1024]{1,0:T(8,128)(2,1)} %query_ref.3, bf16[384,1024]{1,0:T(8,128)(2,1)} %key_ref.3, bf16[384,1024]{1,0:T(8,128)(2,1)} %value_ref.3, ...), custom_call_target="tpu_custom_call", output_to_operand_aliasing={{1}: (6, {}), {2}: (7, {})} | custom-call | flops 1440000000 | bytes 4800000 | tf_op jit(solution)/shard_map/pallas_call | solution.py:282
  16.2 0.0 collective-permute-done.came_ref
  16.2 0.8 %shard_map.86 = (bf16[4,128,256]{2,1,0:T(8,128)(2,1)S(1)}, bf16[2,128,256]{2,1,0:T(8,128)(2,1)S(1)}, bf16[2,128,256]{2,1,0:T(8,128)(2,1)S(1)}) custom-call(s32[3]{0:T(128)S(1)} %pad_add_fusion.1.place_ref, bf16[4,128,256]{2,1,0:T(8,128)(2,1)S(1)} %get-tuple-element.44.own_ref, bf16[4,128,256]{2,1,0:T(8,128)(2,1)S(1)} %collective-permute-done.came_ref), custom_call_target="tpu_custom_call" | custom-call | tf_op jit(solution)/shard_map/pallas_call | solution.py:371
  17.0 1.6 %collective-permute-start.1 = (bf16[2,128,256]{2,1,0:T(8,128)(2,1)S(1)}, bf16[2,128,256]{2,1,0:T(8,128)(2,1)S(1)}, u32[]{:S(2)}, u32[]{:S(2)}) collective-permute-start(bf16[2,128,256]{2,1,0:T(8,128)(2,1)S(1)} %get-tuple-element.48), channel_id=1, source_target_pairs={{0,8},{4,12},{8,0},{12,4},{16,24},{20,28},{24,16},{28,20},{1,9},{5... | collective-permute-start | bytes 393224 | tf_op jit(solution)/shard_map/ppermute | solution.py:394
  18.7 3.4 %collective-permute-done.1.came_ref = bf16[2,128,256]{2,1,0:T(8,128)(2,1)S(1)} collective-permute-done((bf16[2,128,256]{2,1,0:T(8,128)(2,1)S(1)}, bf16[2,128,256]{2,1,0:T(8,128)(2,1)S(1)}, u32[]{:S(2)}, u32[]{:S(2)}) %collective-permute-start.1) | collective-permute-done | bytes 131104 | tf_op jit(solution)/shard_map/ppermute | solution.py:394
  22.1 0.7 %shard_map.87 = (bf16[2,128,256]{2,1,0:T(8,128)(2,1)S(1)}, bf16[2,128,128]{2,1,0:T(8,128)(2,1)S(1)}) custom-call(s32[3]{0:T(128)S(1)} %pad_add_fusion.1.place_ref, bf16[2,128,256]{2,1,0:T(8,128)(2,1)S(1)} %get-tuple-element.47.own_ref, bf16[2,128,256]{2,1,0:T(8,128)(2,1)S(1)} %collective-permute-done.1.came_ref), custom_call_target="tpu_custom_call" | custom-call | tf_op jit(solution)/shard_map/pallas_call | solution.py:371
  22.8 2.6 %collective-permute-start.2 = (bf16[2,128,128]{2,1,0:T(8,128)(2,1)S(1)}, bf16[2,128,128]{2,1,0:T(8,128)(2,1)S(1)}, u32[]{:S(2)}, u32[]{:S(2)}) collective-permute-start(bf16[2,128,128]{2,1,0:T(8,128)(2,1)S(1)} %get-tuple-element.50), channel_id=1, source_target_pairs={{0,16},{4,20},{8,24},{12,28},{16,0},{20,4},{24,8},{28,12},{1,17},{... | collective-permute-start | bytes 196616 | tf_op jit(solution)/shard_map/ppermute | solution.py:394
  25.4 2.6 %collective-permute-done.2.came_ref = bf16[2,128,128]{2,1,0:T(8,128)(2,1)S(1)} collective-permute-done((bf16[2,128,128]{2,1,0:T(8,128)(2,1)S(1)}, bf16[2,128,128]{2,1,0:T(8,128)(2,1)S(1)}, u32[]{:S(2)}, u32[]{:S(2)}) %collective-permute-start.2) | collective-permute-done | bytes 65568 | tf_op jit(solution)/shard_map/ppermute | solution.py:394
  28.0 0.7 %shard_map.88 = (bf16[2,128,128]{2,1,0:T(8,128)(2,1)S(1)}, bf16[2,128,128]{2,1,0:T(8,128)(2,1)S(1)}) custom-call(s32[3]{0:T(128)S(1)} %pad_add_fusion.1.place_ref, bf16[2,128,256]{2,1,0:T(8,128)(2,1)S(1)} %get-tuple-element.49.early_ref, bf16[2,128,128]{2,1,0:T(8,128)(2,1)S(1)} %collective-permute-done.2.came_ref), custom_call_target="tpu_custom_call" | custom-call | tf_op jit(solution)/shard_map/pallas_call | solution.py:371
  28.7 1.6 %collective-permute-start.3 = (bf16[2,128,128]{2,1,0:T(8,128)(2,1)S(1)}, bf16[2,128,128]{2,1,0:T(8,128)(2,1)S(1)}, u32[]{:S(2)}, u32[]{:S(2)}) collective-permute-start(bf16[2,128,128]{2,1,0:T(8,128)(2,1)S(1)} %get-tuple-element.52), channel_id=1, source_target_pairs={{0,8},{4,12},{8,0},{12,4},{16,24},{20,28},{24,16},{28,20},{1,9},{5... | collective-permute-start | bytes 196616 | tf_op jit(solution)/shard_map/ppermute | solution.py:394
  30.3 2.7 %collective-permute-done.3.came_ref = bf16[2,128,128]{2,1,0:T(8,128)(2,1)S(1)} collective-permute-done((bf16[2,128,128]{2,1,0:T(8,128)(2,1)S(1)}, bf16[2,128,128]{2,1,0:T(8,128)(2,1)S(1)}, u32[]{:S(2)}, u32[]{:S(2)}) %collective-permute-start.3) | collective-permute-done | bytes 65568 | tf_op jit(solution)/shard_map/ppermute | solution.py:394
  33.0 0.7 %shard_map.89 = (bf16[4,128,128]{2,1,0:T(8,128)(2,1)S(1)}, bf16[4,128,128]{2,1,0:T(8,128)(2,1)S(1)}) custom-call(s32[3]{0:T(128)S(1)} %pad_add_fusion.1.place_ref, bf16[4,128,256]{2,1,0:T(8,128)(2,1)S(1)} %get-tuple-element.46.early_ref, bf16[2,128,128]{2,1,0:T(8,128)(2,1)S(1)} %get-tuple-element.51.own_ref, ...), custom_call_target="tpu_custom_call" | custom-call | tf_op jit(solution)/shard_map/pallas_call | solution.py:371
  33.8 1.4 %collective-permute-start.4 = (bf16[4,128,128]{2,1,0:T(8,128)(2,1)S(1)}, bf16[4,128,128]{2,1,0:T(8,128)(2,1)S(1)}, u32[]{:S(2)}, u32[]{:S(2)}) collective-permute-start(bf16[4,128,128]{2,1,0:T(8,128)(2,1)S(1)} %get-tuple-element.54), channel_id=1, source_target_pairs={{0,4},{4,0},{8,12},{12,8},{16,20},{20,16},{24,28},{28,24},{1,5},{5... | collective-permute-start | bytes 393224 | tf_op jit(solution)/shard_map/ppermute | solution.py:394
  35.2 0.1 pad_add_fusion.place_ref
  35.3 2.4 %shard_map.84 = (bf16[384,512]{1,0:T(8,128)(2,1)S(1)}, bf16[384,512]{1,0:T(8,128)(2,1)S(1)}, f32[384,512]{1,0:T(8,128)S(1)}, f32[384,512]{1,0:T(8,128)S(1)}) custom-call(s32[2]{0:T(128)S(1)} %pad_add_fusion.place_ref, bf16[384,1024]{1,0:T(8,128)(2,1)} %get-tuple-element.34.refs_0_, f32[384,1024]{1,0:T(8,128)} %get-tuple-element.35.refs_1_), custom_call_target="tpu_custom_call" | custom-call | bytes 10000000 | tf_op jit(solution)/shard_map/pallas_call | solution.py:318
  37.7 0.0 copy-start
  37.7 3.2 %shard_map.85 = (bf16[512,2304]{1,0:T(8,128)(2,1)S(1)}, bf16[512,2304]{1,0:T(8,128)(2,1)S(1)}, bf16[384,512]{1,0:T(8,128)(2,1)S(1)}, bf16[384,512]{1,0:T(8,128)(2,1)S(1)}) custom-call(s32[2]{0:T(128)S(1)} %pad_add_fusion.place_ref, bf16[1024,2304]{1,0:T(8,128)(2,1)} %refs_0_.1, bf16[384,1024]{1,0:T(8,128)(2,1)} %refs_1_.1), custom_call_target="tpu_custom_call" | custom-call | bytes 10000000 | tf_op jit(solution)/shard_map/pallas_call | solution.py:318
  40.9 0.0 copy-done
  40.9 1.5 %early.1.total_ref = f32[384,2304]{1,0:T(8,128)S(1)} custom-call(bf16[384,512]{1,0:T(8,128)(2,1)S(1)} %get-tuple-element.40.through_ref, f32[384,512]{1,0:T(8,128)S(1)} %get-tuple-element.41.settled_ref, bf16[384,512]{1,0:T(8,128)(2,1)S(1)} %get-tuple-element.42.gate_ref, bf16[512,2304]{1,0:T(8,128)(2,1)S(1)} %get-tuple-element.43.weight_ref, ...), custom_call_target="tpu_custom_call" | custom-call | flops 905969664 | bytes 2359296 | tf_op jit(solution)/shard_map/early/pallas_call | solution.py:343
  42.4 0.0 collective-permute-done.4.state_ref
  42.4 1.5 %late.1 = (bf16[2,96,768]{2,1,0:T(8,128)(2,1)S(1)}, bf16[2,96,768]{2,1,0:T(8,128)(2,1)S(1)}, bf16[2,96,1536]{2,1,0:T(8,128)(2,1)S(1)}, bf16[2,96,1536]{2,1,0:T(8,128)(2,1)S(1)}) custom-call(bf16[384,512]{1,0:T(8,128)(2,1)S(1)} %get-tuple-element.36.through_ref, f32[384,512]{1,0:T(8,128)S(1)} %get-tuple-element.37.settled_ref, ...), custom_call_target="tpu_custom_call" | custom-call | flops 905969664 | bytes 2359296 | tf_op jit(solution)/shard_map/late/pallas_call | solution.py:354
  43.9 0.1 collective-permute-start.7
  44.0 0.5 collective-permute-start.5
  44.5 1.9 %collective-permute-done.5 = bf16[2,96,768]{2,1,0:T(8,128)(2,1)S(1)} collective-permute-done((bf16[2,96,768]{2,1,0:T(8,128)(2,1)S(1)}, bf16[2,96,768]{2,1,0:T(8,128)(2,1)S(1)}, u32[]{:S(2)}, u32[]{:S(2)}) %collective-permute-start.5) | collective-permute-done | bytes 294944 | tf_op jit(solution)/shard_map/ppermute | solution.py:452
  46.4 1.6 %collective-permute-start.6 = (bf16[96,768]{1,0:T(8,128)(2,1)S(1)}, bf16[96,768]{1,0:T(8,128)(2,1)S(1)}, u32[]{:S(2)}, u32[]{:S(2)}) collective-permute-start(bf16[96,768]{1,0:T(8,128)(2,1)S(1)} %fusion.3), channel_id=1, source_target_pairs={{0,2},{1,3},{2,0},{3,1},{4,6},{5,7},{6,4},{7,5},{8,10},{9,11},{10,... | collective-permute-start | bytes 442376 | tf_op jit(solution)/shard_map/ppermute | solution.py:463
  48.0 0.0 collective-permute-done.7
  48.0 0.1 fusion.1
  48.1 0.6 collective-permute-start.8
  48.7 4.5 %collective-permute-done.6 = bf16[96,768]{1,0:T(8,128)(2,1)S(1)} collective-permute-done((bf16[96,768]{1,0:T(8,128)(2,1)S(1)}, bf16[96,768]{1,0:T(8,128)(2,1)S(1)}, u32[]{:S(2)}, u32[]{:S(2)}) %collective-permute-start.6) | collective-permute-done | bytes 147488 | tf_op jit(solution)/shard_map/ppermute | solution.py:463
  53.2 0.1 fusion.2
  53.3 5.4 %collective-permute-done.8 = bf16[96,1536]{1,0:T(8,128)(2,1)S(1)} collective-permute-done((bf16[96,1536]{1,0:T(8,128)(2,1)S(1)}, bf16[96,1536]{1,0:T(8,128)(2,1)S(1)}, u32[]{:S(2)}, u32[]{:S(2)}) %collective-permute-start.8) | collective-permute-done | bytes 294944 | tf_op jit(solution)/shard_map/ppermute | solution.py:463
  58.7 0.1 fusion
  58.8 0.8 %pad_maximum_fusion = bf16[96,2304]{1,0:T(8,128)(2,1)} fusion(bf16[96,1536]{1,0:T(8,128)(2,1)S(1)} %fusion, bf16[96,768]{1,0:T(8,128)(2,1)S(1)} %fusion.2), kind=kLoop, calls=%fused_computation.3 | loop fusion | flops 884736 | bytes 884736 | tf_op jit(solution)/shard_map/concatenate | solution.py:494
  (1 shorter events, 0.0 us)
Async XLA Ops:
  6.6 9.6 %collective-permute-start = (bf16[4,128,256]{2,1,0:T(8,128)(2,1)S(1)}, bf16[4,128,256]{2,1,0:T(8,128)(2,1)S(1)}, u32[]{:S(2)}, u32[]{:S(2)}) collective-permute-start(bf16[4,128,256]{2,1,0:T(8,128)(2,1)S(1)} %get-tuple-element.45), channel_id=1, source_target_pairs={{0,4},{4,0},{8,12},{12,8},{16,20},{20,16},{24,28},{28,24},{1,5},{5... | collective-permute-start | bytes 786440 | tf_op jit(solution)/shard_map/ppermute | solution.py:394
  17.0 5.0 %collective-permute-start.1 = (bf16[2,128,256]{2,1,0:T(8,128)(2,1)S(1)}, bf16[2,128,256]{2,1,0:T(8,128)(2,1)S(1)}, u32[]{:S(2)}, u32[]{:S(2)}) collective-permute-start(bf16[2,128,256]{2,1,0:T(8,128)(2,1)S(1)} %get-tuple-element.48), channel_id=1, source_target_pairs={{0,8},{4,12},{8,0},{12,4},{16,24},{20,28},{24,16},{28,20},{1,9},{5... | collective-permute-start | bytes 393224 | tf_op jit(solution)/shard_map/ppermute | solution.py:394
  22.8 5.2 %collective-permute-start.2 = (bf16[2,128,128]{2,1,0:T(8,128)(2,1)S(1)}, bf16[2,128,128]{2,1,0:T(8,128)(2,1)S(1)}, u32[]{:S(2)}, u32[]{:S(2)}) collective-permute-start(bf16[2,128,128]{2,1,0:T(8,128)(2,1)S(1)} %get-tuple-element.50), channel_id=1, source_target_pairs={{0,16},{4,20},{8,24},{12,28},{16,0},{20,4},{24,8},{28,12},{1,17},{... | collective-permute-start | bytes 196616 | tf_op jit(solution)/shard_map/ppermute | solution.py:394
  28.7 4.3 %collective-permute-start.3 = (bf16[2,128,128]{2,1,0:T(8,128)(2,1)S(1)}, bf16[2,128,128]{2,1,0:T(8,128)(2,1)S(1)}, u32[]{:S(2)}, u32[]{:S(2)}) collective-permute-start(bf16[2,128,128]{2,1,0:T(8,128)(2,1)S(1)} %get-tuple-element.52), channel_id=1, source_target_pairs={{0,8},{4,12},{8,0},{12,4},{16,24},{20,28},{24,16},{28,20},{1,9},{5... | collective-permute-start | bytes 196616 | tf_op jit(solution)/shard_map/ppermute | solution.py:394
  33.8 8.6 %collective-permute-start.4 = (bf16[4,128,128]{2,1,0:T(8,128)(2,1)S(1)}, bf16[4,128,128]{2,1,0:T(8,128)(2,1)S(1)}, u32[]{:S(2)}, u32[]{:S(2)}) collective-permute-start(bf16[4,128,128]{2,1,0:T(8,128)(2,1)S(1)} %get-tuple-element.54), channel_id=1, source_target_pairs={{0,4},{4,0},{8,12},{12,8},{16,20},{20,16},{24,28},{28,24},{1,5},{5... | collective-permute-start | bytes 393224 | tf_op jit(solution)/shard_map/ppermute | solution.py:394
  37.7 3.2 %copy-start = (f32[128]{0:T(128)S(1)}, f32[128]{0:T(128)}, u32[]{:S(2)}) copy-start(f32[128]{0:T(128)} %param.14) | copy-start | bytes 1540
  43.9 4.1 %collective-permute-start.7 = (bf16[2,96,1536]{2,1,0:T(8,128)(2,1)S(1)}, bf16[2,96,1536]{2,1,0:T(8,128)(2,1)S(1)}, u32[]{:S(2)}, u32[]{:S(2)}) collective-permute-start(bf16[2,96,1536]{2,1,0:T(8,128)(2,1)S(1)} %get-tuple-element.58), channel_id=1, source_target_pairs={{0,1},{1,0},{2,3},{3,2},{4,5},{5,4},{6,7},{7,6},{8,9},{9,8},{10,11... | collective-permute-start | bytes 1769480 | tf_op jit(solution)/shard_map/ppermute | solution.py:452
  44.0 2.4 %collective-permute-start.5 = (bf16[2,96,768]{2,1,0:T(8,128)(2,1)S(1)}, bf16[2,96,768]{2,1,0:T(8,128)(2,1)S(1)}, u32[]{:S(2)}, u32[]{:S(2)}) collective-permute-start(bf16[2,96,768]{2,1,0:T(8,128)(2,1)S(1)} %get-tuple-element.56), channel_id=1, source_target_pairs={{0,1},{1,0},{2,3},{3,2},{4,5},{5,4},{6,7},{7,6},{8,9},{9,8},{10,11... | collective-permute-start | bytes 884744 | tf_op jit(solution)/shard_map/ppermute | solution.py:452
  46.4 6.8 %collective-permute-start.6 = (bf16[96,768]{1,0:T(8,128)(2,1)S(1)}, bf16[96,768]{1,0:T(8,128)(2,1)S(1)}, u32[]{:S(2)}, u32[]{:S(2)}) collective-permute-start(bf16[96,768]{1,0:T(8,128)(2,1)S(1)} %fusion.3), channel_id=1, source_target_pairs={{0,2},{1,3},{2,0},{3,1},{4,6},{5,7},{6,4},{7,5},{8,10},{9,11},{10,... | collective-permute-start | bytes 442376 | tf_op jit(solution)/shard_map/ppermute | solution.py:463
  48.1 10.6 %collective-permute-start.8 = (bf16[96,1536]{1,0:T(8,128)(2,1)S(1)}, bf16[96,1536]{1,0:T(8,128)(2,1)S(1)}, u32[]{:S(2)}, u32[]{:S(2)}) collective-permute-start(bf16[96,1536]{1,0:T(8,128)(2,1)S(1)} %fusion.1), channel_id=1, source_target_pairs={{0,2},{1,3},{2,0},{3,1},{4,6},{5,7},{6,4},{7,5},{8,10},{9,11},{10,... | collective-permute-start | bytes 884744 | tf_op jit(solution)/shard_map/ppermute | solution.py:463
